TPU v7x, 32 devices: a whole 2x2x4 slice. The times are simulated.
32 devices in a mesh: slide: 2 (over x), row: 16 (over z, y, core).
Axes of the slice: x: 2, y: 2, z: 4, core: 2. Of those that a mesh axis runs over, the one named last changes fastest.
Arguments:
- tokens: bfloat16 [128, 128, 768], P(('slide', 'row')), parts along dimension 0, may hold values from -6 to 6
- norm_gain: float32 [768], replicated, may hold values from 0.1 to 1.9
- query_weight: bfloat16 [768, 768], replicated, may hold values from -0.875 to 0.875
- key_weight: bfloat16 [768, 768], replicated, may hold values from -0.875 to 0.875
- value_weight: bfloat16 [768, 768], replicated, may hold values from -0.21875 to 0.21875
- out_weight: bfloat16 [768, 768], replicated, may hold values from -0.21875 to 0.21875
- head_scale: float32 [12], replicated, may hold values from 0.02 to 0.5
- pool_queries: bfloat16 [16, 768], replicated, may hold values from -24 to 24
Outputs:
- mixed: bfloat16 [128, 128, 768], P(('slide', 'row')), parts along dimension 0
- pooled: float32 [32, 768], P('slide'), parts along dimension 0
There are 2 independent parts, one for each index of `slide`. A program takes and returns all parts, laid end to end along the dimension named above; an argument that names none is the same for every part. Nothing has to cross between parts.
All inputs are finite; a program needn't handle non-finite values.
Results may differ from a plain program's by a relative error of at most 0.007.
The roundings to bfloat16 on the way count: a program that leaves them out, or rounds other values in their place, can miss the bound.
Values may be sent and summed in bfloat16 or wider, within the bound.
No kernel may reach another device: no remote copies, remote signals or barrier semaphores. Data moves between devices by JAX's collectives and lax.ppermute only.
A program may use at most 128 MiB of HBM per device.

v0:
```python
import jax
import jax.numpy as jnp
from jax import lax
from jax.sharding import PartitionSpec as P

RAD = 4


norm_eps = 1e-06


def extended(cells, sides, width):
    for axis, dim in sides:
        count = lax.axis_size(axis)
        ends = count - 1
        head = lax.slice_in_dim(cells, 0, width, axis=dim)
        tail = lax.slice_in_dim(cells, cells.shape[dim] - width, cells.shape[dim], axis=dim)
        cells = jnp.concatenate(
            [
                lax.ppermute(tail, axis, [(i, (i + 1) % count) for i in range(ends)]),
                cells,
                lax.ppermute(head, axis, [((i + 1) % count, i) for i in range(ends)]),
            ],
            axis=dim,
        )
    return cells


def merged_2(shard, axis, combine):
    everything = jax.tree.map(lambda part: lax.all_gather(part, axis), shard)
    initial = jax.tree.map(lambda part: part[0], everything)

    def hop(k, so_far):
        return combine(so_far, jax.tree.map(lambda part: part[k], everything))

    return lax.fori_loop(1, lax.axis_size(axis), hop, initial)


def normalize(tokens, norm_gain):
    feats = tokens.astype(jnp.float32)
    mean_sq = jnp.mean(feats * feats, axis=-1, keepdims=True)
    return (feats * lax.rsqrt(mean_sq + norm_eps) * norm_gain).astype(jnp.bfloat16)


def project(weight, normed, head_count):
    row_count, col_count, feature_width = normed.shape
    flattened = normed.reshape(row_count * col_count, feature_width)
    projected = lax.dot_general(
        weight, flattened, (((0,), (1,)), ((), ())), preferred_element_type=jnp.float32
    )
    return projected.astype(jnp.bfloat16).reshape(
        head_count, feature_width // head_count, row_count, col_count
    )


def lorentz_time(spatial):
    spatial_f = spatial.astype(jnp.float32)
    return jnp.sqrt(1.0 + jnp.sum(spatial_f * spatial_f, axis=1))


def split_cols(array, group, block, reach):
    blocks = group // block
    lead = array.shape[:-1]
    main_part = array[..., :group].reshape(lead + (blocks, block))
    extra = array[..., block:]
    pad_width = [(0, 0)] * len(lead) + [(0, blocks * block - extra.shape[-1])]
    extra = jnp.pad(extra, pad_width).reshape(lead + (blocks, block))[..., : 2 * reach]
    return jnp.concatenate([main_part, extra], axis=-1)


def window_attend(query_heads, key_rows, value_rows, row_inside, head_scale):
    head_count, head_width, row_count, col_count = query_heads.shape
    group = 128
    block = 32
    blocks = group // block
    tile_rows = 4
    key_tile_rows = tile_rows + 2 * RAD
    key_tile_cols = block + 2 * RAD
    key_pad = jnp.pad(key_rows, ((0, 0), (0, 0), (0, 0), (RAD, RAD)))
    value_pad = jnp.pad(value_rows, ((0, 0), (0, 0), (0, 0), (RAD, RAD)))
    key_time = lorentz_time(key_pad)
    value_time = lorentz_time(value_pad)
    query_time = lorentz_time(query_heads)
    col_global = jnp.arange(col_count + 2 * RAD, dtype=jnp.int32) - RAD
    col_inside = (col_global >= 0) & (col_global < col_count)
    query_row = jnp.arange(tile_rows, dtype=jnp.int32)[:, None, None, None]
    query_col = jnp.arange(block, dtype=jnp.int32)[None, :, None, None]
    key_row = jnp.arange(key_tile_rows, dtype=jnp.int32)[None, None, :, None]
    key_col = jnp.arange(key_tile_cols, dtype=jnp.int32)[None, None, None, :]
    row_gap = key_row - query_row
    col_gap = key_col - query_col
    window_mask = (row_gap >= 0) & (row_gap <= 2 * RAD) & (col_gap >= 0) & (col_gap <= 2 * RAD)
    window_mask = window_mask.reshape(tile_rows * block, key_tile_rows * key_tile_cols)
    col_groups = col_count // group
    tile_count = row_count // tile_rows * col_groups

    def one_tile(tile_index):
        query_blocks = query_heads.reshape(head_count, head_width, tile_rows, blocks, block)
        query_blocks = query_blocks.transpose(0, 3, 1, 2, 4).reshape(
            head_count, blocks, head_width, tile_rows * block
        )
        key_blocks = split_cols(key_pad, group, block, RAD).transpose(0, 3, 1, 2, 4)
        key_blocks = key_blocks.reshape(
            head_count, blocks, head_width, key_tile_rows * key_tile_cols
        )
        value_blocks = split_cols(value_pad, group, block, RAD).transpose(0, 3, 1, 2, 4)
        value_blocks = value_blocks.reshape(
            head_count, blocks, head_width, key_tile_rows * key_tile_cols
        )
        qtime_blocks = query_time.reshape(head_count, tile_rows, blocks, block).transpose(
            0, 2, 1, 3
        )
        qtime_blocks = qtime_blocks.reshape(head_count, blocks, tile_rows * block)
        ktime_blocks = split_cols(key_time, group, block, RAD).transpose(0, 2, 1, 3)
        ktime_blocks = ktime_blocks.reshape(head_count, blocks, key_tile_rows * key_tile_cols)
        vtime_blocks = split_cols(value_time, group, block, RAD).transpose(0, 2, 1, 3)
        vtime_blocks = vtime_blocks.reshape(head_count, blocks, key_tile_rows * key_tile_cols)
        cin_blocks = split_cols(col_inside, group, block, RAD)
        key_valid = row_inside[:, None, None] & cin_blocks[None]
        key_valid = key_valid.transpose(1, 0, 2).reshape(blocks, key_tile_rows * key_tile_cols)
        inner = jnp.einsum(
            "hbdq,hbdk->hbqk", query_blocks, key_blocks, preferred_element_type=jnp.float32
        )
        lorentz_dot = inner - qtime_blocks[:, :, :, None] * ktime_blocks[:, :, None, :]
        scores_now = head_scale[:, None, None, None] * (2.0 + 2.0 * lorentz_dot)
        allowed = window_mask[None, None] & key_valid[None, :, None, :]
        scores_now = jnp.where(allowed, scores_now, -jnp.inf)
        peak_score = jnp.max(scores_now, axis=-1, keepdims=True)
        weights = jnp.exp(scores_now - peak_score).astype(jnp.bfloat16)
        mean_space = jnp.einsum(
            "hbqk,hbdk->hbdq", weights, value_blocks, preferred_element_type=jnp.float32
        )
        mean_time = jnp.sum(weights.astype(jnp.float32) * vtime_blocks[:, :, None, :], axis=-1)
        spread = jnp.sqrt(mean_time * mean_time - jnp.sum(mean_space * mean_space, axis=2))
        attended = (mean_space / spread[:, :, None, :]).astype(jnp.bfloat16)
        attended = attended.reshape(head_count, blocks, head_width, tile_rows, block).transpose(
            0, 2, 3, 1, 4
        )
        return attended.reshape(head_count, head_width, tile_rows, group)

    tiles = lax.map(one_tile, jnp.arange(tile_count, dtype=jnp.int32))
    tiles = tiles.reshape(
        row_count // tile_rows, col_groups, head_count, head_width, tile_rows, group
    )
    return tiles.transpose(2, 3, 0, 4, 1, 5).reshape(head_count, head_width, row_count, col_count)


def mix_out(attended, out_weight, token_block):
    head_count, head_width, row_count, col_count = attended.shape
    flattened = attended.reshape(head_count * head_width, row_count * col_count)
    projected = lax.dot_general(
        flattened, out_weight, (((0,), (0,)), ((), ())), preferred_element_type=jnp.float32
    )
    projected = projected.reshape(row_count, col_count, head_count * head_width)
    return (token_block.astype(jnp.float32) + projected).astype(jnp.bfloat16)


def pool_scores(pool_queries, key_heads, head_scale):
    head_count, head_width = (key_heads.shape[0], key_heads.shape[1])
    key_flat = key_heads.reshape(head_count, head_width, -1)
    pool_space = pool_queries.astype(jnp.float32).reshape(
        pool_queries.shape[0], head_count, head_width
    )
    pool_time = jnp.sqrt(1.0 + jnp.sum(pool_space * pool_space, axis=-1))
    lorentz_dot = jnp.einsum(
        "phd,hdt->pht", pool_space, key_flat.astype(jnp.float32), precision=lax.Precision.HIGHEST
    )
    lorentz_dot = lorentz_dot - pool_time[:, :, None] * lorentz_time(key_flat)[None]
    return head_scale[None, :, None] * (2.0 + 2.0 * lorentz_dot)


def pool_partial(pool_score, peak_score, value_heads):
    head_count, head_width = (value_heads.shape[0], value_heads.shape[1])
    value_flat = value_heads.reshape(head_count, head_width, -1)
    weights = jnp.exp(pool_score - peak_score[:, :, None])
    mean_space = jnp.einsum(
        "pht,hdt->phd", weights, value_flat.astype(jnp.float32), precision=lax.Precision.HIGHEST
    )
    mean_time = jnp.sum(weights * lorentz_time(value_flat)[None], axis=-1)
    return (mean_space, mean_time)


def combine_pools(earlier_part, later_part):
    peak_score = jnp.maximum(earlier_part[0], later_part[0])
    factor_early = jnp.exp(earlier_part[0] - peak_score)
    factor_late = jnp.exp(later_part[0] - peak_score)
    mean_space = (
        earlier_part[1] * factor_early[:, :, None] + later_part[1] * factor_late[:, :, None]
    )
    mean_time = earlier_part[2] * factor_early + later_part[2] * factor_late
    return (peak_score, mean_space, mean_time)


def per_device(
    tokens, norm_gain, query_weight, key_weight, value_weight, out_weight, head_scale, pool_queries
):
    row_count, col_count, feature_width = tokens.shape
    head_count = head_scale.shape[0]
    normed = normalize(tokens, norm_gain)
    query_heads = project(query_weight, normed, head_count)
    key_heads = project(key_weight, normed, head_count)
    value_heads = project(value_weight, normed, head_count)
    stacked_rims = extended(jnp.stack([key_heads, value_heads]), (("row", 3),), RAD)
    key_rows = stacked_rims[0]
    value_rows = stacked_rims[1]
    total_rows = row_count * lax.axis_size("row")
    global_rows = (
        lax.axis_index("row") * row_count - RAD + jnp.arange(row_count + 2 * RAD, dtype=jnp.int32)
    )
    row_inside = (global_rows >= 0) & (global_rows < total_rows)
    attended = window_attend(query_heads, key_rows, value_rows, row_inside, head_scale)
    mixed = mix_out(attended, out_weight, tokens)
    pool_score = pool_scores(pool_queries, key_heads, head_scale)
    local_peak = jnp.max(pool_score, axis=-1)
    mean_space, mean_time = pool_partial(pool_score, local_peak, value_heads)
    merged = merged_2((local_peak, mean_space, mean_time), "row", combine_pools)
    mean_space = merged[1]
    mean_time = merged[2]
    spread = jnp.sqrt(mean_time * mean_time - jnp.sum(mean_space * mean_space, axis=-1))
    pooled = (mean_space / spread[:, :, None]).reshape(mean_space.shape[0], feature_width)
    return (mixed, pooled)


def solution(mesh):
    placed = (P(("slide", "row"), None, None), P(), P(), P(), P(), P(), P(), P())
    return jax.shard_map(
        per_device,
        mesh=mesh,
        in_specs=placed,
        out_specs=(P(("slide", "row"), None, None), P("slide", None)),
        check_vma=False,
    )
```

profile of v0, /device:TPU:0, one launch (start us, length us, event | category | flops | bytes accessed | tf_op | source)
XLA Modules:
  0.0 231.4 jit_solution(14739717786627771079)
XLA Ops:
  0.6 1.5 fusion.5
  2.1 1.4 fusion.7
  3.5 2.3 %fusion.10 = bf16[768,512]{0,1:T(8,128)(2,1)S(1)} fusion(bf16[512,768]{1,0:T(8,128)(2,1)S(1)} %bitcast.115, bf16[768,768]{1,0:T(8,128)(2,1)} %param.14), kind=kOutput, calls=%fused_computation.41 | convolution fusion | flops 604372992 | bytes 2752512 | tf_op jit(solution)/shard_map/dot_general | solution.py:48
  6.3 2.9 %fusion.9 = bf16[768,512]{0,1:T(8,128)(2,1)} fusion(bf16[512,768]{1,0:T(8,128)(2,1)S(1)} %bitcast.116, bf16[768,768]{1,0:T(8,128)(2,1)} %param.13), kind=kOutput, calls=%fused_computation.40 | convolution fusion | flops 604372992 | bytes 2752512 | tf_op jit(solution)/shard_map/dot_general | solution.py:48
  9.3 1.4 copy.94
  10.7 1.1 stack_reshape.6
  11.7 2.4 %constant_dynamic-update-slice_fusion.1 = bf16[2,12,64,4,128]{4,3,2,1,0:T(4,128)(2,1)} fusion(bf16[1,12,64,4,128]{4,3,2,1,0:T(4,128)(2,1)} %stack_reshape.6), kind=kLoop, calls=%fused_computation.77 | loop fusion | bytes 1572864
  14.1 1.2 constant_dynamic-update-slice_fusion
  15.3 1.3 collective-permute-start.1
  16.6 4.2 %collective-permute-start = (bf16[2,12,64,4,128]{4,3,2,1,0:T(4,128)(2,1)}, bf16[2,12,64,4,128]{4,3,2,1,0:T(4,128)(2,1)}, u32[]{:S(2)}, u32[]{:S(2)}) collective-permute-start(bf16[2,12,64,4,128]{4,3,2,1,0:T(4,128)(2,1)} %constant_dynamic-update-slice_fusion), channel_id=1, source_target_pairs={{0,1},{1,2},{2,3},{3,4},{4,5},{5,6},{6,7},{7,8},{8,9},{9,10},{10,1... | collective-permute-start | bytes 4718600 | tf_op jit(solution)/shard_map/ppermute | solution.py:20
  20.9 0.8 reshape.249
  22.7 0.4 and_and_fusion
  23.0 1.0 and.116
  24.9 0.8 convolution_bitcast_fusion.1
  26.0 40.6 %all-gather.2 = f32[256,12]{1,0:T(8,128)S(1)} all-gather(f32[16,12]{1,0:T(8,128)S(1)} %copy.117), channel_id=4, replica_groups=mesh['slide'=2,'row'=16] {'row'}, dimensions={0}, use_global_device_ids=true | all-gather | bytes 13056 | tf_op jit(solution)/shard_map/all_gather | solution.py:30
  66.5 21.0 %all-gather = f32[256,12]{1,0:T(8,128)S(1)} all-gather(f32[16,12]{1,0:T(8,128)S(1)} %copy.115), channel_id=2, replica_groups=mesh['slide'=2,'row'=16] {'row'}, dimensions={0}, use_global_device_ids=true | all-gather | bytes 13056 | tf_op jit(solution)/shard_map/all_gather | solution.py:30
  87.5 25.4 %all-gather.1 = f32[256,12,64]{2,0,1:T(8,128)S(1)} all-gather(f32[16,12,64]{2,0,1:T(8,128)S(1)} %convolution_bitcast_fusion.1), channel_id=3, replica_groups=mesh['slide'=2,'row'=16] {'row'}, dimensions={0}, use_global_device_ids=true | all-gather | bytes 835584 | tf_op jit(solution)/shard_map/all_gather | solution.py:30
  113.0 1.1 copy-done.5
  114.1 16.8 %while.23 = (s32[]{:T(128)}, f32[16,12]{1,0:T(8,128)S(1)}, f32[16,12,64]{2,1,0:T(8,128)S(1)}, f32[16,12]{1,0:T(8,128)S(1)}, f32[16,16,12]{2,1,0:T(8,128)S(1)}, /...) while((s32[]{:T(128)}, f32[16,12]{1,0:T(8,128)S(1)}, ...), condition=%wide.region_13.14_spmd, body=%wide.region_12.13_spmd.sunk | while | flops 38021 | bytes 253583 | solution.py:36
  114.1 0.9 constant_dynamic-slice_fusion.2
  115.2 0.9 constant_dynamic-slice_fusion.2
  116.3 0.9 constant_dynamic-slice_fusion.2
  117.4 0.9 constant_dynamic-slice_fusion.2
  118.6 0.9 constant_dynamic-slice_fusion.2
  119.7 0.9 constant_dynamic-slice_fusion.2
  120.8 0.9 constant_dynamic-slice_fusion.2
  121.9 0.9 constant_dynamic-slice_fusion.2
  123.1 0.9 constant_dynamic-slice_fusion.2
  124.2 0.9 constant_dynamic-slice_fusion.2
  125.3 0.9 constant_dynamic-slice_fusion.2
  126.4 0.9 constant_dynamic-slice_fusion.2
  127.6 0.9 constant_dynamic-slice_fusion.2
  128.7 0.9 constant_dynamic-slice_fusion.2
  129.8 0.9 constant_dynamic-slice_fusion.2
  131.1 0.7 reshape.250
  131.9 1.7 convert_multiply_fusion.2
  133.5 1.6 copy.105
  135.1 1.9 mul.230
  137.5 1.3 reshape_reshape.10
  138.8 1.6 copy.99
  140.8 5.0 %pad_maximum_fusion = bf16[2,12,64,12,128]{4,3,2,1,0:T(8,128)(2,1)S(1)} fusion(bf16[2,12,64,4,128]{4,3,2,1,0:T(4,128)(2,1)} %collective-permute-done.1, bf16[2,12,64,4,128]{4,3,2,1,0:T(4,128)(2,1)} %constant_dynamic-update-slice_fusion, bf16[2,12,64,4,128]{4,3,2,1,0:T(4,128)(2,1)} %collective-permute-done), kind=kLoop, calls=%fused_computation.20 | loop fusion | flops 14155776 | bytes 9437184 | tf_op jit(solution)/shard_map/concatenate | solution.py:18
  145.8 1.7 slice_bitcast_fusion
  147.5 5.6 %multiply_reduce_fusion = (f32[12,12,136]{2,1,0:T(8,128)S(1)}, f32[12,12,136]{2,1,0:T(8,128)S(1)}) fusion(bf16[12,64,12,128]{3,2,1,0:T(8,128)(2,1)S(1)} %get-tuple-element.273, bf16[12,64,12,128]{3,2,1,0:T(8,128)(2,1)S(1)} %get-tuple-element.272), kind=kLoop, calls=%fused_computation.10 | loop fusion | flops 7481088 | bytes 4875264 | tf_op jit(solution)/shard_map/reduce_sum | solution.py:58
  153.4 3.8 %pad_slice_fusion = (bf16[12,64,12,104]{3,2,1,0:T(8,128)(2,1)}, bf16[12,64,12,104]{3,2,1,0:T(8,128)(2,1)}) fusion(bf16[12,64,12,128]{3,2,1,0:T(8,128)(2,1)S(1)} %get-tuple-element.272, bf16[12,64,12,128]{3,2,1,0:T(8,128)(2,1)S(1)} %get-tuple-element.273), kind=kLoop, calls=%fused_computation.15 | loop fusion | bytes 8552448 | tf_op jit(solution)/shard_map/while/body/eval_jaxpr/slice | solution.py:65
  157.1 3.8 %pad_slice_fusion.1 = (bf16[12,64,12,128]{3,2,1,0:T(8,128)(2,1)}, bf16[12,64,12,128]{3,2,1,0:T(8,128)(2,1)}) fusion(bf16[12,64,12,128]{3,2,1,0:T(8,128)(2,1)S(1)} %get-tuple-element.272, bf16[12,64,12,128]{3,2,1,0:T(8,128)(2,1)S(1)} %get-tuple-element.273), kind=kLoop, calls=%fused_computation.16 | loop fusion | bytes 9437184 | tf_op jit(solution)/shard_map/while/body/eval_jaxpr/slice | solution.py:64
  162.6 6.4 %copy.125 = bf16[12,64,12,104]{1,3,2,0:T(8,128)(2,1)} copy(bf16[12,64,12,104]{3,2,1,0:T(8,128)(2,1)} %get-tuple-element.284) | data formatting | bytes 3833856
  169.0 3.2 %pad.34.clone = bf16[12,64,12,128]{1,3,2,0:T(8,128)(2,1)S(1)} pad(bf16[12,64,12,104]{1,3,2,0:T(8,128)(2,1)} %copy.125, bf16[]{:T(256)} %constant.84.clone.1), padding=0_0x0_0x0_0x0_24 | pad | bytes 4276226 | tf_op jit(solution)/shard_map/while/body/eval_jaxpr/jit(_pad)/pad | solution.py:67
  172.5 6.5 %copy.100 = bf16[12,64,12,128]{1,3,2,0:T(8,128)(2,1)} copy(bf16[12,64,12,128]{3,2,1,0:T(8,128)(2,1)} %get-tuple-element.286) | data formatting | bytes 4718592 | tf_op jit(solution)/shard_map/while/body/eval_jaxpr/slice | solution.py:64
  179.0 3.9 %maximum_bitcast_fusion.1 = bf16[12,4,64,12,40]{2,4,1,3,0:T(8,128)(2,1)S(1)} fusion(bf16[12,64,12,4,8]{1,4,3,2,0:T(8,128)(2,1)S(1)} %slice.101, bf16[12,64,12,4,32]{1,4,3,2,0:T(8,128)(2,1)} %bitcast.102), kind=kLoop, calls=%fused_computation.22 | loop fusion | flops 5898240 | bytes 5898240 | tf_op jit(solution)/shard_map/while/body/eval_jaxpr/transpose | solution.py:102
  182.9 3.6 %copy.102 = bf16[12,4,64,12,40]{2,4,3,1,0:T(8,128)(2,1)} copy(bf16[12,4,64,12,40]{2,4,1,3,0:T(8,128)(2,1)S(1)} %maximum_bitcast_fusion.1) | data formatting | bytes 5898240 | tf_op jit(solution)/shard_map/while/body/eval_jaxpr/transpose | solution.py:102
  186.6 6.2 %copy.124 = bf16[12,64,12,104]{1,3,2,0:T(8,128)(2,1)} copy(bf16[12,64,12,104]{3,2,1,0:T(8,128)(2,1)} %get-tuple-element.285) | data formatting | bytes 3833856
  192.8 3.2 %pad.31.clone = bf16[12,64,12,128]{1,3,2,0:T(8,128)(2,1)S(1)} pad(bf16[12,64,12,104]{1,3,2,0:T(8,128)(2,1)} %copy.124, bf16[]{:T(256)} %constant.84.clone.1), padding=0_0x0_0x0_0x0_24 | pad | bytes 4276226 | tf_op jit(solution)/shard_map/while/body/eval_jaxpr/jit(_pad)/pad | solution.py:67
  196.3 6.5 %copy.96 = bf16[12,64,12,128]{1,3,2,0:T(8,128)(2,1)} copy(bf16[12,64,12,128]{3,2,1,0:T(8,128)(2,1)} %get-tuple-element.287) | data formatting | bytes 4718592 | tf_op jit(solution)/shard_map/while/body/eval_jaxpr/slice | solution.py:64
  202.8 4.1 %maximum_bitcast_fusion = bf16[12,4,64,12,40]{2,4,1,3,0:T(8,128)(2,1)S(1)} fusion(bf16[12,64,12,4,8]{1,4,3,2,0:T(8,128)(2,1)S(1)} %slice.99, bf16[12,64,12,4,32]{1,4,3,2,0:T(8,128)(2,1)} %bitcast.103), kind=kLoop, calls=%fused_computation.21 | loop fusion | flops 5898240 | bytes 5898240 | tf_op jit(solution)/shard_map/while/body/eval_jaxpr/transpose | solution.py:106
  206.9 1.0 copy.98
  207.9 0.4 slice-done.1
  208.3 0.5 copy-done.6
  208.8 3.7 %fusion.4 = (f32[12,4,128]{2,1,0:T(4,128)S(1)}, f32[12,4,128,480]{2,3,1,0:T(8,128)S(1)}) fusion(f32[12,4,480]{2,1,0:T(4,128)S(1)} %mul.234, f32[12,4,128]{2,1,0:T(4,128)S(1)} %mul.231, f32[12]{0:T(128)S(1)} %copy-done.10, pred[4,128,480]{1,2,0:T(8,128)(4,1)S(1)} %broadcast_and_fusion, bf16[12,4,64,128]{2,3,1,0:T(8,128)(2,1)S(1)} %bitcast.119, ...), kind=kOutput, calls=%fused_computation.19 | convolution fusion | flops 398125056 | bytes 15919152 | tf_op jit(solution)/shard_map/while/body/eval_jaxpr/hbdq,hbdk->hbqk/dot_general | solution.py:121
  212.5 7.3 %multiply_reduce_fusion.2 = (f32[12,4,128]{2,1,0:T(4,128)S(1)}, bf16[12,4,128,480]{2,3,1,0:T(8,128)(2,1)S(1)}) fusion(f32[12,4,480]{2,1,0:T(4,128)S(1)} %mul.240, f32[12,4,128]{2,1,0:T(4,128)S(1)} %get-tuple-element.276, f32[12,4,128,480]{2,3,1,0:T(8,128)S(1)} %get-tuple-element.277, f32[12,4,480]{2,1,0:T(4,128)S(1)} %mul.234, f32[12,4,128]{2,1,0:T(4,128)S(1)} %mul.231, ...), kind=kLoop, calls=%fused_computation.12 | loop fusion | flops 32434176 | bytes 18198576 | tf_op jit(solution)/shard_map/while/body/eval_jaxpr/reduce_sum | solution.py:133
  219.8 1.8 multiply_reduce_fusion.5
  221.8 1.6 copy.110
  223.4 2.6 %copy.111 = bf16[12,64,4,4,32]{1,0,4,3,2:T(8,128)(2,1)S(1)} copy(bf16[12,64,4,4,32]{1,4,2,3,0:T(8,128)(2,1)} %bitcast.111) | data formatting | bytes 1572864 | tf_op jit(solution)/shard_map/while/body/eval_jaxpr/transpose | solution.py:136
  226.0 2.0 reshape_reshape_transpose_reshape.3
  228.0 3.4 %fusion.8 = bf16[4,128,768]{2,1,0:T(8,128)(2,1)} fusion(bf16[4,128,768]{2,1,0:T(8,128)(2,1)} %param.10, bf16[4,128,768]{2,1,0:T(8,128)(2,1)} %bitcast.122, bf16[768,768]{1,0:T(8,128)(2,1)} %param.15), kind=kOutput, calls=%fused_computation.31 | convolution fusion | flops 605159424 | bytes 3538944 | tf_op jit(solution)/shard_map/dot_general | solution.py:151
  (122 shorter events, 9.0 us)
Async XLA Ops:
  0.6 131.2 %copy-start = (bf16[768,768]{1,0:T(8,128)(2,1)S(1)}, bf16[768,768]{1,0:T(8,128)(2,1)}, u32[]{:S(2)}) copy-start(bf16[768,768]{1,0:T(8,128)(2,1)} %param.12) | copy-start | bytes 3538948
  3.5 2.8 %copy-start.2 = (bf16[4,128,768]{2,1,0:T(8,128)(2,1)}, bf16[4,128,768]{2,1,0:T(8,128)(2,1)S(1)}, u32[]{:S(2)}) copy-start(bf16[4,128,768]{2,1,0:T(8,128)(2,1)S(1)} %fusion.7) | copy-start | bytes 2359300
  11.7 9.1 %copy-start.9 = (bf16[16,768]{1,0:T(8,128)(2,1)S(1)}, bf16[16,768]{1,0:T(8,128)(2,1)}, u32[]{:S(2)}) copy-start(bf16[16,768]{1,0:T(8,128)(2,1)} %param.17) | copy-start | bytes 73732
  11.7 12.7 %copy-start.10 = (f32[12]{0:T(128)S(1)}, f32[12]{0:T(128)}, u32[]{:S(2)}) copy-start(f32[12]{0:T(128)} %param.16) | copy-start | bytes 148
  15.3 125.4 %collective-permute-start.1 = (bf16[2,12,64,4,128]{4,3,2,1,0:T(4,128)(2,1)}, bf16[2,12,64,4,128]{4,3,2,1,0:T(4,128)(2,1)}, u32[]{:S(2)}, u32[]{:S(2)}) collective-permute-start(bf16[2,12,64,4,128]{4,3,2,1,0:T(4,128)(2,1)} %constant_dynamic-update-slice_fusion), channel_id=1, source_target_pairs={{1,0},{2,1},{3,2},{4,3},{5,4},{6,5},{7,6},{8,7},{9,8},{10,9},{11,1... | collective-permute-start | bytes 4718600 | tf_op jit(solution)/shard_map/ppermute | solution.py:22
  16.6 124.1 %collective-permute-start = (bf16[2,12,64,4,128]{4,3,2,1,0:T(4,128)(2,1)}, bf16[2,12,64,4,128]{4,3,2,1,0:T(4,128)(2,1)}, u32[]{:S(2)}, u32[]{:S(2)}) collective-permute-start(bf16[2,12,64,4,128]{4,3,2,1,0:T(4,128)(2,1)} %constant_dynamic-update-slice_fusion), channel_id=1, source_target_pairs={{0,1},{1,2},{2,3},{3,4},{4,5},{5,6},{6,7},{7,8},{8,9},{9,10},{10,1... | collective-permute-start | bytes 4718600 | tf_op jit(solution)/shard_map/ppermute | solution.py:20
  66.5 65.3 %copy-start.3 = (bf16[4,128,768]{2,1,0:T(8,128)(2,1)S(1)}, bf16[4,128,768]{2,1,0:T(8,128)(2,1)}, u32[]{:S(2)}) copy-start(bf16[4,128,768]{2,1,0:T(8,128)(2,1)} %copy-done.2) | copy-start | bytes 2359300
  112.9 1.1 copy-start.5
  135.1 2.4 %copy-start.4 = (bf16[768,512]{0,1:T(8,128)(2,1)S(1)}, bf16[768,512]{0,1:T(8,128)(2,1)}, u32[]{:S(2)}) copy-start(bf16[768,512]{0,1:T(8,128)(2,1)} %get-tuple-element.275) | copy-start | bytes 2359300
  137.5 2.9 %copy-start.8 = (pred[128,480]{0,1:T(8,128)(4,1)S(1)}, pred[128,480]{0,1:T(8,128)(4,1)}, u32[]{:S(2)}) copy-start(pred[128,480]{0,1:T(8,128)(4,1)} %and.116) | copy-start | bytes 184324
  153.1 4.1 %copy-start.7 = (f32[12,12,136]{2,1,0:T(8,128)}, f32[12,12,136]{2,1,0:T(8,128)S(1)}, u32[]{:S(2)}) copy-start(f32[12,12,136]{2,1,0:T(8,128)S(1)} %add_sqrt_fusion) | copy-start | bytes 235012
  160.9 1.0 slice-start.2
  202.8 5.2 %slice-start = ((s8[5898240]{0:T(1024)(128)(4,1)}), s8[4194304]{0:T(1024)(128)(4,1)S(1)}, s32[]{:S(2)}) async-start(s8[5898240]{0:T(1024)(128)(4,1)} %bitcast.112), calls=%async_computation | async-start | bytes 8388608
  206.9 1.5 slice-start.1
  206.9 1.9 copy-start.6
  223.4 8.0 %copy-start.1 = (bf16[768,768]{1,0:T(8,128)(2,1)S(1)}, bf16[768,768]{1,0:T(8,128)(2,1)}, u32[]{:S(2)}) copy-start(bf16[768,768]{1,0:T(8,128)(2,1)} %param.12) | copy-start | bytes 3538948
where the time goes:
time: 233 us; the launch traced here: 231 us
  blocking collectives  87 us (37%)
  local copies, waits for them, and re-layouts  86.1 us (37%)
  other arithmetic  34.2 us (15%)
  matrix products  16.9 us (7%)
  starting transfers between devices  5.49 us (2%)
    all_gather x3, blocking collectives, merged_2(): everything = jax.tree.map(lambda part: lax.all_gather(part, axis), shard)  87 us
    unnamed x29, local copies, waits for them, and re-layouts  17 us
    slice x6, local copies, waits for them, and re-layouts, split_cols(): main_part = array[..., :group].reshape(lead + (blocks, block))  16.8 us
    dynamic_slice x15, local copies, waits for them, and re-layouts, hop(): return combine(so_far, jax.tree.map(lambda part: part[k], everything))  13.7 us
    reduce_sum x1, other arithmetic, one_tile(): jnp.sum(weights.astype(jnp.float32) * vtime_blocks[:, :, None, :], axis=-1)  7.33 us
    dot_general x3, matrix products, project(): lax.dot_general(weight, flattened, (((0,), (1,)), ((), ())), preferred_el...  6.92 us
    pad x5, local copies, waits for them, and re-layouts, split_cols(): jnp.pad(extra, pad_width).reshape(lead + (blocks, block))[..., :2 * reach]  6.4 us
    reduce_sum x4, other arithmetic, lorentz_time(): return jnp.sqrt(1.0 + jnp.sum(spatial_f * spatial_f, axis=1))  6.17 us
  transfers between devices with their start and end apart: 2, of which 0 were waited for; matrix products, arithmetic and copies ran while one was open for 13% of the time, Pallas kernels for 0%

commit v1 on v0

v1 whole, which is shorter than its diff:
```python
import math

import jax
import jax.numpy as jnp
from jax import lax
from jax.experimental import pallas as pl
from jax.experimental.pallas import tpu as pltpu
from jax.sharding import PartitionSpec as P

RAD = 4
EPS = 1e-06
HEAD = 64
LANES = 128
BLOCK = 32
SPLIT = 6
BIG = 1e30
F32 = jnp.float32
BF16 = jnp.bfloat16
LOG2E = math.log2(math.e)
NT = (((1,), (1,)), ((), ()))


def lane_iota(shape):
    return lax.broadcasted_iota(jnp.int32, shape, len(shape) - 1)


def row_iota(shape):
    return lax.broadcasted_iota(jnp.int32, shape, 0)


def normalize(tokens, gain):
    feats = tokens.astype(F32)
    mean_sq = jnp.mean(feats * feats, axis=-1, keepdims=True)
    return feats * lax.rsqrt(mean_sq + EPS) * gain


def shift_columns(normed, cols):
    rows = normed.shape[0] // cols
    return jnp.concatenate(
        [pltpu.roll(normed[r * cols : (r + 1) * cols], RAD, 0) for r in range(rows)], axis=0
    )


def head_lanes(heads):
    shape = (heads * HEAD, LANES)
    head, lane = row_iota(shape) // HEAD, lane_iota(shape)
    hit = lane == head
    for piece in range(1, SPLIT):
        hit = hit | (lane == head + piece * heads)
    return hit.astype(F32).astype(BF16)


def time_pieces(points, sums):
    f = points.astype(F32)
    sq = f * f
    hi = sq.astype(BF16)
    lo = (sq - hi.astype(F32)).astype(BF16)
    total = jnp.dot(hi, sums, preferred_element_type=F32) + jnp.dot(
        lo, sums, preferred_element_type=F32
    )
    t = jnp.sqrt(1.0 + total)
    first = t.astype(BF16).astype(F32)
    rest = t - first
    second = rest.astype(BF16).astype(F32)
    third = (rest - second).astype(BF16).astype(F32)
    return first, second, third


def query_times(pieces, heads, lane):
    first, second, third = pieces
    mixed = jnp.where((lane >= heads) & (lane < 2 * heads), second, first)
    mixed = jnp.where((lane >= 2 * heads) & (lane < 3 * heads), third, mixed)
    mixed = jnp.where((lane >= 4 * heads) & (lane < 5 * heads), second, mixed)
    return jnp.where(lane < SPLIT * heads, -mixed, 0.0)


def key_times(pieces, heads, lane):
    first, second, third = pieces
    mixed = jnp.where(lane < 3 * heads, first, jnp.where(lane < 5 * heads, second, third))
    return jnp.where(lane < SPLIT * heads, mixed, 0.0)


def value_times(pieces, heads, lane):
    first, second, third = pieces
    mixed = jnp.where(lane < heads, first, jnp.where(lane < 2 * heads, second, third))
    return jnp.where(lane < 3 * heads, mixed, 0.0)


def store_rows(ref, first_row, pitch, cols, value, lanes):
    rows = value.shape[0] // cols
    for r in range(rows):
        base = (first_row + r) * pitch
        row = value[r * cols : (r + 1) * cols]
        ref[base : base + cols, lanes] = row
        ref[base + cols : base + pitch, lanes] = row[: pitch - cols]


def project_strip(normed, k_w, v_w, sums, heads, cols, pitch, first_row, k_ref, v_ref, invalid):
    width = heads * HEAD
    keys = jnp.dot(normed, k_w[...], preferred_element_type=F32).astype(BF16)
    store_rows(k_ref, first_row, pitch, cols, keys, slice(0, width))
    values = jnp.dot(normed, v_w[...], preferred_element_type=F32).astype(BF16)
    store_rows(v_ref, first_row, pitch, cols, values, slice(0, width))
    lane = lane_iota((normed.shape[0], LANES))
    k_time = key_times(time_pieces(keys, sums), heads, lane).astype(BF16)
    v_time = value_times(time_pieces(values, sums), heads, lane).astype(BF16)
    store_rows(v_ref, first_row, pitch, cols, v_time, slice(width, width + LANES))
    flag_lane = SPLIT * heads + BLOCK + RAD
    place = row_iota((pitch, LANES))
    flag = lane_iota((pitch, LANES)) == flag_lane
    outside = (place < RAD) | (place >= cols + RAD)
    if invalid is not None:
        outside = outside | (invalid > 0)
    bias = jnp.where(flag & outside, -BIG, 0.0).astype(BF16)
    for r in range(normed.shape[0] // cols):
        base = (first_row + r) * pitch
        row = k_time[r * cols : (r + 1) * cols]
        row = jnp.concatenate([row, row[: pitch - cols]], axis=0)
        k_ref[base : base + pitch, width : width + LANES] = row + bias


def window_bias(mask_ref, key_rows, wide, first, heads):
    shape = (key_rows * wide, LANES)
    place, lane = row_iota(shape), lane_iota(shape)
    key_row = place // wide
    key_col = place - key_row * wide
    key_row = key_row + first
    col = lane - SPLIT * heads
    row = col - BLOCK
    bad_col = (col >= 0) & (col < BLOCK) & ((key_col < col) | (key_col > col + 2 * RAD))
    bad_row = (row >= 0) & (row < RAD) & ((key_row < row) | (key_row > row + 2 * RAD))
    mask_ref[...] = jnp.where(bad_col | bad_row, -BIG, 0.0).astype(BF16)


def query_features(token_count, cols, heads):
    shape = (token_count, LANES)
    token, lane = row_iota(shape), lane_iota(shape)
    col = lane - SPLIT * heads
    hit = (col == token % BLOCK) & (col < BLOCK)
    hit = hit | (col == BLOCK + token // cols) | (col == BLOCK + RAD)
    return jnp.where(hit & (col >= 0), 1.0, 0.0)


def head_mask(heads, head, lane, pieces):
    hit = lane == head
    for piece in range(1, pieces):
        hit = hit | (lane == piece * heads + head)
    return hit


def window_scores(q_ref, k_ref, mask_ref, block, pair, rows, cols, pitch, wide, key_rows, heads):
    width = heads * HEAD
    lanes = slice(pair * LANES, (pair + 1) * LANES)
    extra = slice(width, width + LANES)
    lane = lane_iota((1, LANES))
    q_start = [pl.multiple_of(r * cols + block * BLOCK, BLOCK) for r in range(rows)]
    q = jnp.concatenate([q_ref[pl.ds(s, BLOCK), lanes] for s in q_start], axis=0)
    qx = jnp.concatenate([q_ref[pl.ds(s, BLOCK), extra] for s in q_start], axis=0)
    stacked = []
    for half in range(2):
        own = (lane < HEAD) if half == 0 else (lane >= HEAD)
        keep = head_mask(heads, 2 * pair + half, lane, SPLIT) | (lane >= SPLIT * heads)
        stacked.append(
            jnp.concatenate(
                [q * own.astype(F32).astype(BF16), qx * keep.astype(F32).astype(BF16)], axis=1
            )
        )
    k_start = [pl.multiple_of(r * pitch + block * BLOCK, 16) for r in range(key_rows)]
    k = jnp.concatenate([k_ref[pl.ds(s, wide), lanes] for s in k_start], axis=0)
    kx = jnp.concatenate([k_ref[pl.ds(s, wide), extra] for s in k_start], axis=0)
    kx = kx + mask_ref[...]
    return lax.dot_general(
        jnp.concatenate(stacked, axis=0),
        jnp.concatenate([k, kx], axis=1),
        NT,
        preferred_element_type=F32,
    )


def weighted_values(weights, v_ref, block, pair, pitch, wide, key_rows, heads):
    width = heads * HEAD
    starts = [pl.multiple_of(r * pitch + block * BLOCK, 16) for r in range(key_rows)]
    v = jnp.concatenate(
        [v_ref[pl.ds(s, wide), pair * LANES : (pair + 1) * LANES] for s in starts], axis=0
    )
    vx = jnp.concatenate([v_ref[pl.ds(s, wide), width : width + LANES] for s in starts], axis=0)
    return jnp.dot(weights, jnp.concatenate([v, vx], axis=1), preferred_element_type=F32)


def window_pass(
    q_ref, k_ref, v_ref, mask_ref, scale_ref, block, pair, rows, cols, pitch, wide, key_rows, heads
):
    scores = window_scores(
        q_ref, k_ref, mask_ref, block, pair, rows, cols, pitch, wide, key_rows, heads
    )
    half = scores.shape[0] // 2
    lane = lane_iota((1, LANES))
    peak = jnp.max(scores, axis=-1, keepdims=True)
    scale = [scale_ref[2 * pair + i] for i in range(2)]
    weights = [
        jnp.exp2((scores[i * half : (i + 1) * half] - peak[i * half : (i + 1) * half]) * scale[i])
        for i in range(2)
    ]
    weights = jnp.concatenate(weights, axis=0).astype(BF16)
    total = weighted_values(weights, v_ref, block, pair, pitch, wide, key_rows, heads)
    space = jnp.where(lane < HEAD, total[:half, :LANES], total[half:, :LANES])
    times = [
        jnp.sum(
            jnp.where(
                head_mask(heads, 2 * pair + i, lane, 3),
                total[i * half : (i + 1) * half, LANES:],
                0.0,
            ),
            axis=-1,
            keepdims=True,
        )
        for i in range(2)
    ]
    return [peak[:half], peak[half:]], space, times


def keys_body(
    parity_ref, scale_ref, own_ref, mate_ref, gain_ref, k_w, v_w, pool_ref, k_ref, v_ref, out_ref
):
    rows_cols, width = own_ref.shape
    heads = width // HEAD
    cols = LANES
    rows = rows_cols // cols
    pitch = k_ref.shape[0] // (2 * rows)
    sums = head_lanes(heads)
    odd = parity_ref[0] > 0
    own, mate = own_ref[...].astype(F32), mate_ref[...].astype(F32)
    for strip in range(2):
        tokens = jnp.where(odd, mate, own) if strip == 0 else jnp.where(odd, own, mate)
        normed = shift_columns(normalize(tokens, gain_ref[...]), cols).astype(BF16)
        project_strip(
            normed, k_w, v_w, sums, heads, cols, pitch, strip * rows, k_ref, v_ref, None
        )
    pq = pool_ref[...]
    count = pq.shape[0]
    lane = lane_iota((count, LANES))
    q_time = query_times(time_pieces(pq, sums), heads, lane)
    zero = jnp.zeros((count, LANES), F32)
    q_rows = []
    for h in range(heads):
        tiles = [zero] * (width // LANES)
        tile = pq[:, h // 2 * LANES : (h // 2 + 1) * LANES].astype(F32)
        tiles[h // 2] = jnp.where((lane < HEAD) if h % 2 == 0 else (lane >= HEAD), tile, 0.0)
        tiles.append(jnp.where(head_mask(heads, h, lane, SPLIT), q_time, 0.0))
        q_rows.append(jnp.concatenate(tiles, axis=1))
    q_all = jnp.concatenate(q_rows, axis=0).astype(BF16)
    keys = jnp.concatenate([k_ref[r * pitch : r * pitch + cols] for r in range(2 * rows)], axis=0)
    scores = lax.dot_general(q_all, keys, NT, preferred_element_type=F32)
    peak = jnp.max(scores, axis=-1, keepdims=True)
    scale = jnp.concatenate(
        [jnp.full((count, 1), scale_ref[h], F32) for h in range(heads)], axis=0
    )
    f = jnp.exp2((scores - peak) * scale)
    hi = f.astype(BF16)
    lo = (f - hi.astype(F32)).astype(BF16)
    values = jnp.concatenate(
        [v_ref[r * pitch : r * pitch + cols] for r in range(2 * rows)], axis=0
    )
    total = jnp.dot(jnp.concatenate([hi, lo], axis=0), values, preferred_element_type=F32)
    total = total[: heads * count] + total[heads * count :]
    stats = zero
    for h in range(heads):
        part = slice(h * count, (h + 1) * count)
        time = jnp.where(head_mask(heads, h, lane, 3), total[part, width:], 0.0)
        stats = jnp.where(lane == h, jnp.sum(time, axis=-1, keepdims=True), stats)
        stats = jnp.where(lane == HEAD + h, peak[part], stats)
    for j in range(width // LANES):
        tile = slice(j * LANES, (j + 1) * LANES)
        first = total[2 * j * count : (2 * j + 1) * count, tile]
        second = total[(2 * j + 1) * count : (2 * j + 2) * count, tile]
        out_ref[j * count : (j + 1) * count, :] = jnp.where(lane < HEAD, first, second)
    out_ref[width // LANES * count :, :] = stats


def near_body(
    parity_ref, scale_ref, own_ref, gain_ref, q_w, k_ref, v_ref, q_ref, space_ref, stat_ref, mask_ref
):
    token_count, width = own_ref.shape
    heads = width // HEAD
    cols = LANES
    rows = token_count // cols
    key_rows = 2 * rows
    pitch = k_ref.shape[0] // key_rows
    wide = mask_ref.shape[0] // key_rows
    normed = normalize(own_ref[...], gain_ref[...]).astype(BF16)
    queries = jnp.dot(normed, q_w[...], preferred_element_type=F32).astype(BF16)
    q_ref[:, :width] = queries
    lane = lane_iota((token_count, LANES))
    extra = query_times(time_pieces(queries, head_lanes(heads)), heads, lane)
    q_ref[:, width:] = (extra + query_features(token_count, cols, heads)).astype(BF16)
    window_bias(mask_ref, key_rows, wide, RAD * (1 - parity_ref[0]), heads)
    stat_lane = lane_iota((1, LANES))

    def one_block(block, carry):
        stats = jnp.zeros((rows * BLOCK, LANES), F32)
        for pair in range(heads // 2):
            peaks, space, times = window_pass(
                q_ref, k_ref, v_ref, mask_ref, scale_ref, block, pair,
                rows, cols, pitch, wide, key_rows, heads,
            )
            space_ref[block, :, pair * LANES : (pair + 1) * LANES] = space
            for i in range(2):
                stats = jnp.where(stat_lane == 2 * pair + i, times[i], stats)
                stats = jnp.where(stat_lane == HEAD + 2 * pair + i, peaks[i], stats)
        stat_ref[block] = stats
        return carry

    lax.fori_loop(0, cols // BLOCK, one_block, 0)


def far_body(
    parity_ref, scale_ref, own_ref, far_ref, gain_ref, k_w, v_w, o_w, q_ref, space_ref, stat_ref,
    out_ref, k_ref, v_ref, mask_ref, mix_ref,
):
    token_count, width = own_ref.shape
    heads = width // HEAD
    cols = LANES
    rows = token_count // cols
    pitch = k_ref.shape[0] // rows
    wide = mask_ref.shape[0] // rows
    normed = shift_columns(normalize(far_ref[...], gain_ref[...]), cols).astype(BF16)
    project_strip(
        normed, k_w, v_w, head_lanes(heads), heads, cols, pitch, 0, k_ref, v_ref, parity_ref[1]
    )
    window_bias(mask_ref, rows, wide, 2 * RAD * parity_ref[0], heads)
    low = lane_iota((1, LANES)) < HEAD

    def one_block(block, carry):
        stats = stat_ref[block]
        for pair in range(heads // 2):
            peaks, space, times = window_pass(
                q_ref, k_ref, v_ref, mask_ref, scale_ref, block, pair,
                rows, cols, pitch, wide, rows, heads,
            )
            h = 2 * pair
            scale = jnp.where(low, scale_ref[h], scale_ref[h + 1])
            near_time = jnp.where(low, stats[:, h : h + 1], stats[:, h + 1 : h + 2])
            near_peak = jnp.where(
                low, stats[:, HEAD + h : HEAD + h + 1], stats[:, HEAD + h + 1 : HEAD + h + 2]
            )
            far_time = jnp.where(low, times[0], times[1])
            far_peak = jnp.where(low, peaks[0], peaks[1])
            peak = jnp.maximum(near_peak, far_peak)
            near = jnp.exp2((near_peak - peak) * scale)
            far = jnp.exp2((far_peak - peak) * scale)
            mean = space_ref[block, :, pair * LANES : (pair + 1) * LANES] * near + space * far
            time = near_time * near + far_time * far
            sq = mean * mean
            norm = jnp.where(
                low,
                jnp.sum(jnp.where(low, sq, 0.0), axis=-1, keepdims=True),
                jnp.sum(jnp.where(low, 0.0, sq), axis=-1, keepdims=True),
            )
            attended = (mean * lax.rsqrt(time * time - norm)).astype(BF16)
            for r in range(rows):
                start = pl.multiple_of(r * cols + block * BLOCK, BLOCK)
                mix_ref[pl.ds(start, BLOCK), pair * LANES : (pair + 1) * LANES] = attended[
                    r * BLOCK : (r + 1) * BLOCK
                ]
        return carry

    lax.fori_loop(0, cols // BLOCK, one_block, 0)
    projected = jnp.dot(mix_ref[...], o_w[...], preferred_element_type=F32)
    out_ref[...] = (own_ref[...].astype(F32) + projected).astype(BF16)


def merge_parts(first, second, scale, count):
    lane = lane_iota((count, LANES))
    tiles = first.shape[0] // count - 1
    s1, s2 = first[tiles * count :], second[tiles * count :]
    peak = jnp.maximum(s1, s2)
    f1 = jnp.exp2(jnp.where(lane >= HEAD, (s1 - peak) * scale, 0.0))
    f2 = jnp.exp2(jnp.where(lane >= HEAD, (s2 - peak) * scale, 0.0))
    time = s1 * pltpu.roll(f1, HEAD, 1) + s2 * pltpu.roll(f2, HEAD, 1)
    stats = jnp.where(lane < HEAD, time, peak)
    spaces = []
    for j in range(tiles):
        part = slice(j * count, (j + 1) * count)
        a, b = HEAD + 2 * j, HEAD + 2 * j + 1
        g1 = jnp.where(lane < HEAD, f1[:, a : a + 1], f1[:, b : b + 1])
        g2 = jnp.where(lane < HEAD, f2[:, a : a + 1], f2[:, b : b + 1])
        spaces.append(first[part] * g1 + second[part] * g2)
    return spaces, stats


def merge_body(upper_ref, scale_ref, mine_ref, other_ref, out_ref, *, count, last):
    upper = upper_ref[0] > 0
    mine, other = mine_ref[...], other_ref[...]
    first, second = jnp.where(upper, other, mine), jnp.where(upper, mine, other)
    spaces, stats = merge_parts(first, second, scale_ref[...], count)
    if not last:
        out_ref[...] = jnp.concatenate(spaces + [stats], axis=0)
        return
    low = lane_iota((count, LANES)) < HEAD
    for j, mean in enumerate(spaces):
        time = jnp.where(low, stats[:, 2 * j : 2 * j + 1], stats[:, 2 * j + 1 : 2 * j + 2])
        sq = mean * mean
        norm = jnp.where(
            low,
            jnp.sum(jnp.where(low, sq, 0.0), axis=-1, keepdims=True),
            jnp.sum(jnp.where(low, 0.0, sq), axis=-1, keepdims=True),
        )
        out_ref[:, j * LANES : (j + 1) * LANES] = mean / jnp.sqrt(time * time - norm)


SMEM = pl.BlockSpec(memory_space=pltpu.SMEM)
VMEM = pl.BlockSpec(memory_space=pltpu.VMEM)


def local_call(body, args, outs, scratch=(), limit=48, name=None):
    specs = [SMEM if a.ndim == 1 else VMEM for a in args]
    out_specs = jax.tree.map(lambda _: VMEM, outs)
    return pl.pallas_call(
        body,
        out_shape=outs,
        in_specs=specs,
        out_specs=out_specs,
        scratch_shapes=list(scratch),
        compiler_params=pltpu.CompilerParams(vmem_limit_bytes=limit << 20),
        name=name,
    )(*args)


def per_device(
    tokens, norm_gain, query_weight, key_weight, value_weight, out_weight, head_scale, pool_queries
):
    rows, cols, width = tokens.shape
    heads = head_scale.shape[0]
    count = pool_queries.shape[0]
    axis = "row"
    ring = lax.axis_size(axis)
    assert rows == RAD and cols == LANES and width == heads * HEAD
    assert ring & (ring - 1) == 0 and ring > 2
    index = lax.axis_index(axis)
    parity = index % 2
    edge = ((index == 0) | (index == ring - 1)).astype(jnp.int32)
    where = jnp.stack([parity, edge]).astype(jnp.int32)
    own = tokens.reshape(rows * cols, width)
    swap = [(i, i ^ 1) for i in range(ring)]
    cross = [(i, i + 1) for i in range(1, ring - 1, 2)] + [
        (i + 1, i) for i in range(1, ring - 1, 2)
    ]
    far = lax.ppermute(own, axis, cross)
    mate = lax.ppermute(own, axis, swap)
    gain = norm_gain.reshape(1, width)
    scale = head_scale * (2.0 * LOG2E)
    near_pitch, near_wide = cols + 16, BLOCK + 16
    far_pitch, far_wide = cols + 32, 2 * BLOCK
    extra = width + LANES
    struct = jax.ShapeDtypeStruct
    keys, values, part = local_call(
        keys_body,
        (where, scale, own, mate, gain, key_weight, value_weight, pool_queries),
        (
            struct((2 * rows * near_pitch, extra), BF16),
            struct((2 * rows * near_pitch, extra), BF16),
            struct(((width // LANES + 1) * count, LANES), F32),
        ),
        name="keys",
    )
    blocks = cols // BLOCK
    queries, space, stat = local_call(
        near_body,
        (where, scale, own, gain, query_weight, keys, values),
        (
            struct((rows * cols, extra), BF16),
            struct((blocks, rows * BLOCK, width), F32),
            struct((blocks, rows * BLOCK, LANES), F32),
        ),
        [pltpu.VMEM((2 * rows * near_wide, LANES), BF16)],
        name="near",
    )
    lane_scale = jnp.zeros((1, LANES), F32).at[0, HEAD : HEAD + heads].set(scale)
    step = 2
    while step < ring:
        other = lax.ppermute(part, axis, [(i, i ^ step) for i in range(ring)])
        upper = ((index // step) % 2).astype(jnp.int32).reshape(1)
        last = 2 * step >= ring
        shape = (count, width) if last else part.shape
        part = local_call(
            lambda *refs, last=last: merge_body(*refs, count=count, last=last),
            (upper, lane_scale, part, other),
            struct(shape, F32),
            limit=8,
            name="merge",
        )
        step *= 2
    mixed = local_call(
        far_body,
        (where, scale, own, far, gain, key_weight, value_weight, out_weight, queries, space, stat),
        struct((rows * cols, width), BF16),
        [
            pltpu.VMEM((rows * far_pitch, extra), BF16),
            pltpu.VMEM((rows * far_pitch, extra), BF16),
            pltpu.VMEM((rows * far_wide, LANES), BF16),
            pltpu.VMEM((rows * cols, width), BF16),
        ],
        name="far",
    )
    return mixed.reshape(rows, cols, width), part


def solution(mesh):
    placed = (P(("slide", "row"), None, None), P(), P(), P(), P(), P(), P(), P())
    return jax.shard_map(
        per_device,
        mesh=mesh,
        in_specs=placed,
        out_specs=(P(("slide", "row"), None, None), P("slide", None)),
        check_vma=False,
    )
```

time: 233 us -> 62.6 us (0.27)
  blocking collectives: 87 us -> 0 us
  local copies, waits for them, and re-layouts: 86.1 us -> 9.05 us
  Pallas kernels: 0 us -> 35.6 us
  other arithmetic: 34.2 us -> 2.06 us
  matrix products: 16.9 us -> 0 us
  starting transfers between devices: 5.49 us -> 11.7 us
  waiting for transfers between devices: 0.01 us -> 3.05 us
    all_gather x3 -> x0, blocking collectives: 87 us -> none  [merged_2(): everything = jax.tree.map(lambda part: lax.all_gather(part, axis), shard)]
    pallas_call x0 -> x6, Pallas kernels: none -> 35.6 us  [local_call(): pl.pallas_call(body, out_shape=outs, in_specs=specs, out_specs=out_specs,...]
    slice x15 -> x0, local copies, waits for them, and re-layouts: 21.4 us -> none  [the longest x6 16.8 us: split_cols(): main_part = array[..., :group].reshape(lead + (blocks, block))]
    dot_general x8 -> x0, matrix products: 16.9 us -> none  [the longest x3 6.92 us: project(): lax.dot_general(weight, flattened, (((0,), (1,)), ((), ())), preferred_el...]
    reduce_sum x9 -> x0, other arithmetic: 15.4 us -> none  [the longest x1 7.33 us: one_tile(): jnp.sum(weights.astype(jnp.float32) * vtime_blocks[:, :, None, :], axis=-1)]
    dynamic_slice x15 -> x0, local copies, waits for them, and re-layouts: 13.7 us -> none  [hop(): return combine(so_far, jax.tree.map(lambda part: part[k], everything))]
    unnamed x29 -> x20, local copies, waits for them, and re-layouts: 17 us -> 6.89 us
    transpose x7 -> x0, local copies, waits for them, and re-layouts: 8.94 us -> none  [the longest x1 3.64 us: one_tile(): key_blocks = split_cols(key_pad, group, block, RAD).transpose(0, 3, 1, 2, 4)]
  transfers between devices with their start and end apart: 2 -> 5, of which waited for: 0 -> 2; matrix products, arithmetic and copies ran while one was open for 13% -> 7% of each run, Pallas kernels for 0% -> 56%
where the time goes in v1:
time: 62.6 us; the launch traced here: 62.2 us
  Pallas kernels  35.6 us (57%)
  starting transfers between devices  11.7 us (19%)
  local copies, waits for them, and re-layouts  9.05 us (14%)
  waiting for transfers between devices  3.05 us (5%)
  other arithmetic  2.06 us (3%)
  between operations  0.73 us (1%)
    pallas_call x6, Pallas kernels, local_call(): pl.pallas_call(body, out_shape=outs, in_specs=specs, out_specs=out_specs,...  35.6 us
    ppermute x3, starting transfers between devices, per_device(): other = lax.ppermute(part, axis, [(i, i ^ step) for i in range(ring)])  10.5 us
    unnamed x20, local copies, waits for them, and re-layouts  6.89 us
    ppermute x3, waiting for transfers between devices, per_device(): other = lax.ppermute(part, axis, [(i, i ^ step) for i in range(ring)])  3.05 us
    another operation x3, other arithmetic  1.98 us
  transfers between devices with their start and end apart: 5, of which 2 were waited for; matrix products, arithmetic and copies ran while one was open for 7% of the time, Pallas kernels for 56%

profile of v1, /device:TPU:0, one launch (start us, length us, event | category | flops | bytes accessed | tf_op | source)
XLA Modules:
  0.0 62.2 jit_solution(12192375680874509826)
XLA Ops:
  0.6 0.6 collective-permute-start.1
  1.2 0.7 %collective-permute-start = (bf16[512,768]{1,0:T(8,128)(2,1)}, bf16[512,768]{1,0:T(8,128)(2,1)S(1)}, u32[]{:S(2)}, u32[]{:S(2)}) collective-permute-start(bf16[512,768]{1,0:T(8,128)(2,1)} %bitcast.11), channel_id=1, source_target_pairs={{1,2},{3,4},{5,6},{7,8},{9,10},{11,12},{13,14},{2,1},{4,3},{6,5},{... | collective-permute-start | bytes 2359304 | tf_op jit(solution)/shard_map/ppermute | solution.py:448
  1.9 0.7 %reshape.57.gain_ref = f32[1,768]{1,0:T(1,128)S(1)} reshape(f32[768]{0:T(1024)} %param.11) | data formatting | bytes 6144 | tf_op jit(solution)/shard_map/reshape | solution.py:450
  2.6 0.7 %and_reduce_fusion = pred[]{:T(512)} fusion(), kind=kLoop, calls=%fused_computation | loop fusion | flops 11 | bytes 1 | tf_op jit(solution)/shard_map/reduce.1
  3.3 0.1 pad_add_fusion.parity_ref
  3.4 1.3 %fusion = (f32[1,12]{1,0:T(1,128)S(1)}, f32[12]{0:T(128)S(1)}) fusion(pred[]{:T(512)} %and_reduce_fusion, f32[12]{0:T(128)} %param.16), kind=kLoop, calls=%fused_computation.2 | loop fusion | flops 24 | bytes 145 | tf_op jit(solution)/shard_map/reshape.37
  4.7 0.0 collective-permute-done.1.mate_ref
  4.7 0.0 copy-start
  4.7 1.1 %copy-done = bf16[4,128,768]{2,1,0:T(8,128)(2,1)S(1)} copy-done((bf16[4,128,768]{2,1,0:T(8,128)(2,1)S(1)}, bf16[4,128,768]{2,1,0:T(8,128)(2,1)}, u32[]{:S(2)}) %copy-start) | copy-done | bytes 786456
  5.8 0.0 copy-start.2
  5.8 1.3 %copy-done.2 = bf16[768,768]{1,0:T(8,128)(2,1)S(1)} copy-done((bf16[768,768]{1,0:T(8,128)(2,1)S(1)}, bf16[768,768]{1,0:T(8,128)(2,1)}, u32[]{:S(2)}) %copy-start.2) | copy-done | bytes 1179672
  7.1 0.0 copy-start.4
  7.1 1.3 %copy-done.4 = bf16[768,768]{1,0:T(8,128)(2,1)S(1)} copy-done((bf16[768,768]{1,0:T(8,128)(2,1)S(1)}, bf16[768,768]{1,0:T(8,128)(2,1)}, u32[]{:S(2)}) %copy-start.4) | copy-done | bytes 1179672
  8.4 0.0 copy-start.9
  8.4 0.7 %copy-done.9 = bf16[16,768]{1,0:T(8,128)(2,1)S(1)} copy-done((bf16[16,768]{1,0:T(8,128)(2,1)S(1)}, bf16[16,768]{1,0:T(8,128)(2,1)}, u32[]{:S(2)}) %copy-start.9) | copy-done | bytes 24600
  9.1 0.0 copy-start.1
  9.1 0.0 copy-start.8
  9.1 8.1 %keys.1 = (bf16[1152,896]{1,0:T(8,128)(2,1)S(1)}, bf16[1152,896]{1,0:T(8,128)(2,1)}, f32[112,128]{1,0:T(8,128)}) custom-call(s32[2]{0:T(128)S(1)} %pad_add_fusion.parity_ref, f32[12]{0:T(128)S(1)} %get-tuple-element.27.scale_ref, bf16[512,768]{1,0:T(8,128)(2,1)S(1)} %bitcast.12, bf16[512,768]{1,0:T(8,128)(2,1)S(1)} %collective-permute-done.1.mate_ref, ...), custom_call_target="tpu_custom_call" | custom-call | tf_op jit(solution)/shard_map/keys/pallas_call | solution.py:418
  17.2 0.0 copy-start.6
  17.2 1.3 %copy-done.6 = bf16[1152,896]{1,0:T(8,128)(2,1)} copy-done((bf16[1152,896]{1,0:T(8,128)(2,1)}, bf16[1152,896]{1,0:T(8,128)(2,1)S(1)}, u32[]{:S(2)}) %copy-start.6) | copy-done | bytes 2064408
  18.5 3.7 %collective-permute-start.2 = (f32[112,128]{1,0:T(8,128)}, f32[112,128]{1,0:T(8,128)S(1)}, u32[]{:S(2)}, u32[]{:S(2)}) collective-permute-start(f32[112,128]{1,0:T(8,128)} %get-tuple-element.25.refs_2_), channel_id=1, source_target_pairs={{0,2},{1,3},{2,0},{3,1},{4,6},{5,7},{6,4},{7,5},{8,10},{9,11},{10,... | collective-permute-start | bytes 172040 | tf_op jit(solution)/shard_map/ppermute | solution.py:481
  22.3 0.6 slice.20
  22.8 0.9 %scatter.4.refs_1_ = f32[1,128]{1,0:T(1,128)S(1)} dynamic-update-slice(f32[1,128]{1,0:T(1,128)S(1)} %broadcast_in_dim.3, f32[1,12]{1,0:T(1,128)S(1)} %get-tuple-element.26, s32[]{:T(128)} %constant.80.clone.1, s32[]{:T(128)} %bitcast.6) | dynamic-update-slice | bytes 100 | tf_op jit(solution)/shard_map/scatter | solution.py:478
  23.7 0.9 %collective-permute-done.2.refs_3_ = f32[112,128]{1,0:T(8,128)S(1)} collective-permute-done((f32[112,128]{1,0:T(8,128)}, f32[112,128]{1,0:T(8,128)S(1)}, u32[]{:S(2)}, u32[]{:S(2)}) %collective-permute-start.2) | collective-permute-done | bytes 57376 | tf_op jit(solution)/shard_map/ppermute | solution.py:481
  24.6 1.0 %merge.3.refs_2_ = f32[112,128]{1,0:T(8,128)S(1)} custom-call(s32[1]{0:T(128)} %bitcast.8.refs_0_, f32[1,128]{1,0:T(1,128)S(1)} %scatter.4.refs_1_, f32[112,128]{1,0:T(8,128)} %get-tuple-element.25.refs_2_, f32[112,128]{1,0:T(8,128)S(1)} %collective-permute-done.2.refs_3_), custom_call_target="tpu_custom_call" | custom-call | tf_op jit(solution)/shard_map/merge/pallas_call | solution.py:418
  25.6 3.6 %collective-permute-start.3 = (f32[112,128]{1,0:T(8,128)S(1)}, f32[112,128]{1,0:T(8,128)S(1)}, u32[]{:S(2)}, u32[]{:S(2)}) collective-permute-start(f32[112,128]{1,0:T(8,128)S(1)} %merge.3.refs_2_), channel_id=1, source_target_pairs={{0,4},{1,5},{2,6},{3,7},{4,0},{5,1},{6,2},{7,3},{8,12},{9,13},{10,... | collective-permute-start | bytes 172040 | tf_op jit(solution)/shard_map/ppermute | solution.py:481
  29.2 2.2 %collective-permute-done.3.refs_3_ = f32[112,128]{1,0:T(8,128)S(1)} collective-permute-done((f32[112,128]{1,0:T(8,128)S(1)}, f32[112,128]{1,0:T(8,128)S(1)}, u32[]{:S(2)}, u32[]{:S(2)}) %collective-permute-start.3) | collective-permute-done | bytes 57376 | tf_op jit(solution)/shard_map/ppermute | solution.py:481
  31.4 0.2 merge.4.refs_2_
  31.5 3.1 %collective-permute-start.4 = (f32[112,128]{1,0:T(8,128)S(1)}, f32[112,128]{1,0:T(8,128)S(1)}, u32[]{:S(2)}, u32[]{:S(2)}) collective-permute-start(f32[112,128]{1,0:T(8,128)S(1)} %merge.4.refs_2_), channel_id=1, source_target_pairs={{0,8},{1,9},{2,10},{3,11},{4,12},{5,13},{6,14},{7,15},{8,0},{9,1},... | collective-permute-start | bytes 172040 | tf_op jit(solution)/shard_map/ppermute | solution.py:481
  34.6 0.0 copy-done.1
  34.6 0.0 copy-done.8
  34.6 0.0 copy-start.3
  34.7 0.0 copy-start.5
  34.7 9.6 %near.1 = (bf16[512,896]{1,0:T(8,128)(2,1)S(1)}, f32[4,128,768]{2,1,0:T(8,128)S(1)}, f32[4,128,128]{2,1,0:T(8,128)S(1)}) custom-call(s32[2]{0:T(128)S(1)} %pad_add_fusion.parity_ref, f32[12]{0:T(128)S(1)} %get-tuple-element.27.scale_ref, bf16[512,768]{1,0:T(8,128)(2,1)S(1)} %bitcast.13, f32[1,768]{1,0:T(1,128)S(1)} %reshape.57.gain_ref, ...), custom_call_target="tpu_custom_call" | custom-call | tf_op jit(solution)/shard_map/near/pallas_call | solution.py:418
  44.3 0.0 copy-start.7
  44.3 1.2 %copy-done.7 = f32[4,128,768]{2,1,0:T(8,128)} copy-done((f32[4,128,768]{2,1,0:T(8,128)}, f32[4,128,768]{2,1,0:T(8,128)S(1)}, u32[]{:S(2)}) %copy-start.7) | copy-done | bytes 1572888
  45.5 0.0 collective-permute-done.far_ref
  45.5 0.0 copy-done.3
  45.5 0.0 copy-done.5
  45.5 15.7 %far.1 = bf16[512,768]{1,0:T(8,128)(2,1)} custom-call(s32[2]{0:T(128)S(1)} %pad_add_fusion.parity_ref, f32[12]{0:T(128)S(1)} %get-tuple-element.27.scale_ref, bf16[512,768]{1,0:T(8,128)(2,1)S(1)} %bitcast.14, bf16[512,768]{1,0:T(8,128)(2,1)S(1)} %collective-permute-done.far_ref, f32[1,768]{1,0:T(1,128)S(1)} %reshape.57.gain_ref, ...), custom_call_target="tpu_custom_call" | custom-call | tf_op jit(solution)/shard_map/far/pallas_call | solution.py:418
  61.2 0.0 collective-permute-done.4.refs_3_
  61.2 1.0 %merge.5 = f32[16,768]{1,0:T(8,128)} custom-call(s32[1]{0:T(128)} %bitcast.4.refs_0_, f32[1,128]{1,0:T(1,128)S(1)} %scatter.4.refs_1_, f32[112,128]{1,0:T(8,128)S(1)} %merge.4.refs_2_, f32[112,128]{1,0:T(8,128)S(1)} %collective-permute-done.4.refs_3_), custom_call_target="tpu_custom_call" | custom-call | tf_op jit(solution)/shard_map/merge/pallas_call | solution.py:418
  (2 shorter events, 0.0 us)
Async XLA Ops:
  0.6 4.1 %collective-permute-start.1 = (bf16[512,768]{1,0:T(8,128)(2,1)}, bf16[512,768]{1,0:T(8,128)(2,1)S(1)}, u32[]{:S(2)}, u32[]{:S(2)}) collective-permute-start(bf16[512,768]{1,0:T(8,128)(2,1)} %bitcast.10), channel_id=1, source_target_pairs={{0,1},{1,0},{2,3},{3,2},{4,5},{5,4},{6,7},{7,6},{8,9},{9,8},{10,11... | collective-permute-start | bytes 2359304 | tf_op jit(solution)/shard_map/ppermute | solution.py:449
  1.2 44.3 %collective-permute-start = (bf16[512,768]{1,0:T(8,128)(2,1)}, bf16[512,768]{1,0:T(8,128)(2,1)S(1)}, u32[]{:S(2)}, u32[]{:S(2)}) collective-permute-start(bf16[512,768]{1,0:T(8,128)(2,1)} %bitcast.11), channel_id=1, source_target_pairs={{1,2},{3,4},{5,6},{7,8},{9,10},{11,12},{13,14},{2,1},{4,3},{6,5},{... | collective-permute-start | bytes 2359304 | tf_op jit(solution)/shard_map/ppermute | solution.py:448
  4.7 1.1 %copy-start = (bf16[4,128,768]{2,1,0:T(8,128)(2,1)S(1)}, bf16[4,128,768]{2,1,0:T(8,128)(2,1)}, u32[]{:S(2)}) copy-start(bf16[4,128,768]{2,1,0:T(8,128)(2,1)} %param.10) | copy-start | bytes 2359300
  5.8 1.3 %copy-start.2 = (bf16[768,768]{1,0:T(8,128)(2,1)S(1)}, bf16[768,768]{1,0:T(8,128)(2,1)}, u32[]{:S(2)}) copy-start(bf16[768,768]{1,0:T(8,128)(2,1)} %k_w.3) | copy-start | bytes 3538948
  7.1 1.3 %copy-start.4 = (bf16[768,768]{1,0:T(8,128)(2,1)S(1)}, bf16[768,768]{1,0:T(8,128)(2,1)}, u32[]{:S(2)}) copy-start(bf16[768,768]{1,0:T(8,128)(2,1)} %v_w.3) | copy-start | bytes 3538948
  8.4 0.7 %copy-start.9 = (bf16[16,768]{1,0:T(8,128)(2,1)S(1)}, bf16[16,768]{1,0:T(8,128)(2,1)}, u32[]{:S(2)}) copy-start(bf16[16,768]{1,0:T(8,128)(2,1)} %pool_ref.1) | copy-start | bytes 73732
  9.1 25.5 %copy-start.1 = (bf16[4,128,768]{2,1,0:T(8,128)(2,1)S(1)}, bf16[4,128,768]{2,1,0:T(8,128)(2,1)}, u32[]{:S(2)}) copy-start(bf16[4,128,768]{2,1,0:T(8,128)(2,1)} %param.10) | copy-start | bytes 2359300
  9.1 25.5 %copy-start.8 = (bf16[768,768]{1,0:T(8,128)(2,1)S(1)}, bf16[768,768]{1,0:T(8,128)(2,1)}, u32[]{:S(2)}) copy-start(bf16[768,768]{1,0:T(8,128)(2,1)} %q_w.1) | copy-start | bytes 3538948
  17.2 1.3 %copy-start.6 = (bf16[1152,896]{1,0:T(8,128)(2,1)}, bf16[1152,896]{1,0:T(8,128)(2,1)S(1)}, u32[]{:S(2)}) copy-start(bf16[1152,896]{1,0:T(8,128)(2,1)S(1)} %get-tuple-element.20.k_ref) | copy-start | bytes 6193156
  18.5 6.1 %collective-permute-start.2 = (f32[112,128]{1,0:T(8,128)}, f32[112,128]{1,0:T(8,128)S(1)}, u32[]{:S(2)}, u32[]{:S(2)}) collective-permute-start(f32[112,128]{1,0:T(8,128)} %get-tuple-element.25.refs_2_), channel_id=1, source_target_pairs={{0,2},{1,3},{2,0},{3,1},{4,6},{5,7},{6,4},{7,5},{8,10},{9,11},{10,... | collective-permute-start | bytes 172040 | tf_op jit(solution)/shard_map/ppermute | solution.py:481
  25.6 5.8 %collective-permute-start.3 = (f32[112,128]{1,0:T(8,128)S(1)}, f32[112,128]{1,0:T(8,128)S(1)}, u32[]{:S(2)}, u32[]{:S(2)}) collective-permute-start(f32[112,128]{1,0:T(8,128)S(1)} %merge.3.refs_2_), channel_id=1, source_target_pairs={{0,4},{1,5},{2,6},{3,7},{4,0},{5,1},{6,2},{7,3},{8,12},{9,13},{10,... | collective-permute-start | bytes 172040 | tf_op jit(solution)/shard_map/ppermute | solution.py:481
  31.5 29.6 %collective-permute-start.4 = (f32[112,128]{1,0:T(8,128)S(1)}, f32[112,128]{1,0:T(8,128)S(1)}, u32[]{:S(2)}, u32[]{:S(2)}) collective-permute-start(f32[112,128]{1,0:T(8,128)S(1)} %merge.4.refs_2_), channel_id=1, source_target_pairs={{0,8},{1,9},{2,10},{3,11},{4,12},{5,13},{6,14},{7,15},{8,0},{9,1},... | collective-permute-start | bytes 172040 | tf_op jit(solution)/shard_map/ppermute | solution.py:481
  34.6 10.8 %copy-start.3 = (bf16[768,768]{1,0:T(8,128)(2,1)S(1)}, bf16[768,768]{1,0:T(8,128)(2,1)}, u32[]{:S(2)}) copy-start(bf16[768,768]{1,0:T(8,128)(2,1)} %k_w.3) | copy-start | bytes 3538948
  34.7 10.8 %copy-start.5 = (bf16[768,768]{1,0:T(8,128)(2,1)S(1)}, bf16[768,768]{1,0:T(8,128)(2,1)}, u32[]{:S(2)}) copy-start(bf16[768,768]{1,0:T(8,128)(2,1)} %v_w.3) | copy-start | bytes 3538948
  44.3 1.2 %copy-start.7 = (f32[4,128,768]{2,1,0:T(8,128)}, f32[4,128,768]{2,1,0:T(8,128)S(1)}, u32[]{:S(2)}) copy-start(f32[4,128,768]{2,1,0:T(8,128)S(1)} %get-tuple-element.23.space_ref) | copy-start | bytes 4718596

commit v2 on v1

v2 whole, which is shorter than its diff:
```python
import math

import jax
import jax.numpy as jnp
from jax import lax
from jax.experimental import pallas as pl
from jax.experimental.pallas import tpu as pltpu
from jax.sharding import PartitionSpec as P


RAD = 4
EPS = 1e-06
HEAD = 64
LANES = 128
BLOCK = 16
WIDE = 2 * BLOCK
SPLIT = 6
BIG = 1e30
F32 = jnp.float32
BF16 = jnp.bfloat16
DOUBLE_LOG2E = 2.0 * math.log2(math.e)
NT = (((1,), (1,)), ((), ()))
AXIS = "row"


def lane_iota(shape):
    return lax.broadcasted_iota(jnp.int32, shape, len(shape) - 1)


def row_iota(shape):
    return lax.broadcasted_iota(jnp.int32, shape, 0)


def normalize(tokens, gain):
    feats = tokens.astype(F32)
    mean_sq = jnp.mean(feats * feats, axis=-1, keepdims=True)
    return feats * lax.rsqrt(mean_sq + EPS) * gain


def shift_columns(normed, cols):
    rows = normed.shape[0] // cols
    return jnp.concatenate(
        [pltpu.roll(normed[r * cols : (r + 1) * cols], RAD, 0) for r in range(rows)], axis=0
    )


def lane_heads(heads):
    lane = lane_iota((1, LANES))
    head = lane
    for piece in range(1, LANES // heads + 1):
        head = jnp.where(lane >= piece * heads, lane - piece * heads, head)
    return head


def value_lane_heads(heads):
    lane = lane_iota((1, LANES))
    high = jnp.where(lane >= HEAD, 1, 0)
    place = lane - HEAD * high
    pairs = heads // 2
    rest = place
    for piece in range(1, 3):
        rest = jnp.where(place >= piece * pairs, place - piece * pairs, rest)
    return jnp.where(place < 3 * pairs, 2 * rest + high, -1)


def value_mask(heads, head):
    lane = lane_iota((1, LANES))
    first = HEAD * (head % 2) + head // 2
    pairs = heads // 2
    return (lane == first) | (lane == first + pairs) | (lane == first + 2 * pairs)


def half_sums(squares):
    low = lane_iota((1, LANES)) < HEAD
    return (
        jnp.sum(jnp.where(low, squares, 0.0), axis=-1, keepdims=True),
        jnp.sum(jnp.where(low, 0.0, squares), axis=-1, keepdims=True),
    )


def time_pieces(points, heads, head):
    total = jnp.zeros((points.shape[0], LANES), F32)
    for j in range(heads // 2):
        f = points[:, j * LANES : (j + 1) * LANES].astype(F32)
        first, second = half_sums(f * f)
        total = jnp.where(head == 2 * j, first, jnp.where(head == 2 * j + 1, second, total))
    t = jnp.sqrt(1.0 + total)
    first = t.astype(BF16).astype(F32)
    rest = t - first
    second = rest.astype(BF16).astype(F32)
    third = (rest - second).astype(BF16).astype(F32)
    return first, second, third


def query_times(pieces, heads):
    first, second, third = pieces
    lane = lane_iota((1, LANES))
    mixed = jnp.where((lane >= heads) & (lane < 2 * heads), second, first)
    mixed = jnp.where((lane >= 2 * heads) & (lane < 3 * heads), third, mixed)
    mixed = jnp.where((lane >= 4 * heads) & (lane < 5 * heads), second, mixed)
    return jnp.where(lane < SPLIT * heads, -mixed, 0.0)


def key_times(pieces, heads):
    first, second, third = pieces
    lane = lane_iota((1, LANES))
    mixed = jnp.where(lane < 3 * heads, first, jnp.where(lane < 5 * heads, second, third))
    return jnp.where(lane < SPLIT * heads, mixed, 0.0)


def value_times(pieces, heads):
    first, second, third = pieces
    lane = lane_iota((1, LANES))
    place = jnp.where(lane >= HEAD, lane - HEAD, lane)
    pairs = heads // 2
    mixed = jnp.where(place < pairs, first, jnp.where(place < 2 * pairs, second, third))
    return jnp.where(place < 3 * pairs, mixed, 0.0)


def store_rows(ref, pitch, cols, value, lane):
    for r in range(value.shape[0] // cols):
        row = value[r * cols : (r + 1) * cols]
        lanes = slice(lane, lane + value.shape[1])
        ref[r * pitch : r * pitch + cols, lanes] = row
        ref[r * pitch + cols : (r + 1) * pitch, lanes] = row[: pitch - cols]


def store_keys(keys, heads, cols, pitch, ref, invalid):
    width = heads * HEAD
    store_rows(ref, pitch, cols, keys, 0)
    times = key_times(time_pieces(keys, heads, lane_heads(heads)), heads)
    place = row_iota((pitch, LANES))
    outside = (place < RAD) | (place >= cols + RAD)
    if invalid is not None:
        outside = outside | invalid
    flag = lane_iota((pitch, LANES)) == SPLIT * heads + BLOCK + RAD
    bias = jnp.where(flag & outside, -BIG, 0.0)
    for r in range(keys.shape[0] // cols):
        row = times[r * cols : (r + 1) * cols]
        row = jnp.concatenate([row, row[: pitch - cols]], axis=0)
        ref[r * pitch : (r + 1) * pitch, width : width + LANES] = (row + bias).astype(BF16)


def store_values(values, heads, cols, pitch, ref):
    width = heads * HEAD
    base = width + LANES
    store_rows(ref, pitch, cols, values, base)
    times = value_times(time_pieces(values, heads, value_lane_heads(heads)), heads).astype(BF16)
    store_rows(ref, pitch, cols, times, base + width)


def window_bias(mask_ref, first, heads):
    shape = mask_ref.shape
    place, lane = row_iota(shape), lane_iota(shape)
    key_row = place // WIDE
    key_col = place - key_row * WIDE
    key_row = key_row + first
    col = lane - SPLIT * heads
    row = col - BLOCK
    bad_col = (col >= 0) & (col < BLOCK) & ((key_col < col) | (key_col > col + 2 * RAD))
    bad_row = (row >= 0) & (row < RAD) & ((key_row < row) | (key_row > row + 2 * RAD))
    mask_ref[...] = jnp.where(bad_col | bad_row, -BIG, 0.0).astype(BF16)


def query_features(cols, heads, row):
    shape = (cols, LANES)
    token, lane = row_iota(shape), lane_iota(shape)
    col = lane - SPLIT * heads
    hit = (col == token % BLOCK) | (col == BLOCK + row) | (col == BLOCK + RAD)
    return jnp.where(hit & (col >= 0), 1.0, 0.0)


def head_mask(heads, head, lane, pieces):
    hit = lane == head
    for piece in range(1, pieces):
        hit = hit | (lane == piece * heads + head)
    return hit


def as_factor(hit):
    return jnp.where(hit, 1.0, 0.0).astype(BF16)


def window_attention(q_ref, kv_refs, mask_ref, scale_ref, heads, finish):
    width = heads * HEAD
    extra = width + LANES
    cols = LANES
    rows = q_ref.shape[0] // cols
    blocks = cols // BLOCK
    pairs = range(heads // 2)
    lane = lane_iota((1, LANES))
    low = lane < HEAD
    sides = [as_factor(low), as_factor(lane >= HEAD)]
    keeps = [
        as_factor(head_mask(heads, h, lane, SPLIT) | (lane >= SPLIT * heads)) for h in range(heads)
    ]
    scale = [scale_ref[h] * DOUBLE_LOG2E for h in range(heads)]
    half = rows * BLOCK
    parts = (slice(0, half), slice(half, 2 * half))

    def queries_of(block, lanes):
        starts = [r * cols + block * BLOCK for r in range(rows)]
        return jnp.concatenate([q_ref[s : s + BLOCK, lanes] for s in starts], axis=0)

    def keys_of(block, lanes):
        tiles = []
        for ref in kv_refs:
            pitch = ref.shape[0] // rows
            starts = [r * pitch + block * BLOCK for r in range(rows)]
            tiles += [ref[s : s + WIDE, lanes] for s in starts]
        return jnp.concatenate(tiles, axis=0)

    def extras(block):
        return (
            queries_of(block, slice(width, extra)),
            keys_of(block, slice(width, extra)) + mask_ref[...],
        )

    def scores_of(block, pair, qx, kx):
        tile = slice(pair * LANES, (pair + 1) * LANES)
        q = queries_of(block, tile)
        stacked = [
            jnp.concatenate([q * sides[i], qx * keeps[2 * pair + i]], axis=1) for i in range(2)
        ]
        return lax.dot_general(
            jnp.concatenate(stacked, axis=0),
            jnp.concatenate([keys_of(block, tile), kx], axis=1),
            NT,
            preferred_element_type=F32,
        )

    extra_now = extras(0)
    scores = [scores_of(0, pair, *extra_now) for pair in pairs]
    behind = None
    for block in range(blocks):
        ahead = extras(block + 1) if block + 1 < blocks else None
        peaks, coming = [], []
        for pair in pairs:
            peaks.append(jnp.max(scores[pair], axis=-1, keepdims=True))
            if ahead is not None:
                coming.append(scores_of(block + 1, pair, *ahead))
        vx = keys_of(block, slice(extra + width, 2 * extra))
        totals = []
        for pair in pairs:
            both = [
                jnp.exp2((scores[pair][part] - peaks[pair][part]) * scale[2 * pair + i])
                for i, part in enumerate(parts)
            ]
            weights = jnp.concatenate(both, axis=0).astype(BF16)
            v = keys_of(block, slice(extra + pair * LANES, extra + (pair + 1) * LANES))
            totals.append(
                jnp.dot(weights, jnp.concatenate([v, vx], axis=1), preferred_element_type=F32)
            )
            if behind is not None:
                finish(block - 1, pair, *behind[pair])
        behind = []
        for pair in pairs:
            total, peak = totals[pair], peaks[pair]
            behind.append(
                (
                    jnp.where(low, peak[parts[0]], peak[parts[1]]),
                    jnp.where(low, total[parts[0], :LANES], total[parts[1], :LANES]),
                    jnp.where(low, total[parts[0], LANES:], total[parts[1], LANES:]),
                    jnp.where(low, scale[2 * pair], scale[2 * pair + 1]),
                )
            )
        scores = coming
    for pair in pairs:
        finish(blocks - 1, pair, *behind[pair])


def project_body(
    gain_ref, own_hbm, q_hbm, k_hbm, v_hbm, kv_ref, q_ref, own_ref, q_w, k_w, v_w, sems
):
    copies = [
        pltpu.make_async_copy(src, dst, sems.at[i])
        for i, (src, dst) in enumerate(
            ((own_hbm, own_ref), (k_hbm, k_w), (v_hbm, v_w), (q_hbm, q_w))
        )
    ]
    for copy in copies:
        copy.start()
    width = own_ref.shape[1]
    heads = width // HEAD
    cols = LANES
    rows = own_ref.shape[0] // cols
    pitch = kv_ref.shape[0] // rows
    copies[0].wait()
    normed = normalize(own_ref[...], gain_ref[...][None, :])
    shifted = shift_columns(normed, cols).astype(BF16)
    normed = normed.astype(BF16)
    copies[1].wait()
    keys = jnp.dot(shifted, k_w[...], preferred_element_type=F32).astype(BF16)
    copies[2].wait()
    values = jnp.dot(shifted, v_w[...], preferred_element_type=F32).astype(BF16)
    store_keys(keys, heads, cols, pitch, kv_ref, None)
    copies[3].wait()
    queries = jnp.dot(normed, q_w[...], preferred_element_type=F32).astype(BF16)
    store_values(values, heads, cols, pitch, kv_ref)
    q_ref[:, :width] = queries
    times = query_times(time_pieces(queries, heads, lane_heads(heads)), heads)
    for r in range(rows):
        part = slice(r * cols, (r + 1) * cols)
        q_ref[part, width:] = (times[part] + query_features(cols, heads, r)).astype(BF16)


def pool_body(scale_ref, pool_ref, kv_ref, out_ref):
    pq = pool_ref[...]
    count, width = pq.shape
    heads = width // HEAD
    cols = LANES
    extra = width + LANES
    pitch = cols + WIDE - BLOCK
    rows = kv_ref.shape[0] // pitch
    lane = lane_iota((count, LANES))
    q_time = query_times(time_pieces(pq, heads, lane_heads(heads)), heads)
    zero = jnp.zeros((count, LANES), F32)
    q_rows = []
    for h in range(heads):
        tiles = [zero] * (width // LANES)
        tile = pq[:, h // 2 * LANES : (h // 2 + 1) * LANES].astype(F32)
        tiles[h // 2] = jnp.where((lane < HEAD) if h % 2 == 0 else (lane >= HEAD), tile, 0.0)
        tiles.append(jnp.where(head_mask(heads, h, lane, SPLIT), q_time, 0.0))
        q_rows.append(jnp.concatenate(tiles, axis=1))
    q_all = jnp.concatenate(q_rows, axis=0).astype(BF16)
    keys = jnp.concatenate(
        [kv_ref[r * pitch : r * pitch + cols, :extra] for r in range(rows)], axis=0
    )
    scores = lax.dot_general(q_all, keys, NT, preferred_element_type=F32)
    peak = jnp.max(scores, axis=-1, keepdims=True)
    scale = jnp.concatenate(
        [jnp.full((count, 1), scale_ref[h] * DOUBLE_LOG2E, F32) for h in range(heads)], axis=0
    )
    f = jnp.exp2((scores - peak) * scale)
    hi = f.astype(BF16)
    lo = (f - hi.astype(F32)).astype(BF16)
    values = jnp.concatenate(
        [kv_ref[r * pitch : r * pitch + cols, extra:] for r in range(rows)], axis=0
    )
    total = jnp.dot(jnp.concatenate([hi, lo], axis=0), values, preferred_element_type=F32)
    total = total[: heads * count] + total[heads * count :]
    stats = zero
    for h in range(heads):
        part = slice(h * count, (h + 1) * count)
        time = jnp.where(value_mask(heads, h), total[part, width:], 0.0)
        stats = jnp.where(lane == h, jnp.sum(time, axis=-1, keepdims=True), stats)
        stats = jnp.where(lane == HEAD + h, peak[part], stats)
    for j in range(width // LANES):
        tile = slice(j * LANES, (j + 1) * LANES)
        first = total[2 * j * count : (2 * j + 1) * count, tile]
        second = total[(2 * j + 1) * count : (2 * j + 2) * count, tile]
        out_ref[j * count : (j + 1) * count, :] = jnp.where(lane < HEAD, first, second)
    out_ref[width // LANES * count :, :] = stats


def near_body(scale_ref, q_ref, own_ref, mate_ref, peak_ref, space_ref, time_ref, mask_ref):
    width = q_ref.shape[1] - LANES
    heads = width // HEAD
    size = q_ref.shape[0] // LANES * BLOCK
    half = mask_ref.shape[0] // 2
    odd = lax.axis_index(AXIS) % 2
    window_bias(mask_ref.at[:half], RAD, heads)
    window_bias(mask_ref.at[half:], 2 * RAD * (1 - odd), heads)
    mine = [value_mask(heads, 2 * j) | value_mask(heads, 2 * j + 1) for j in range(heads // 2)]
    block_times = {}

    def finish(block, pair, peak, space, times, scale):
        part = slice(block * size, (block + 1) * size)
        tile = slice(pair * LANES, (pair + 1) * LANES)
        peak_ref[part, tile] = peak
        space_ref[part, tile] = space
        so_far = block_times.get(block)
        times = times if so_far is None else jnp.where(mine[pair], times, so_far)
        block_times[block] = times
        if pair == heads // 2 - 1:
            time_ref[part, :] = times

    window_attention(q_ref, (own_ref, mate_ref), mask_ref, scale_ref, heads, finish)


def far_body(
    scale_ref, gain_ref, far_ref, k_w, v_w, o_w, own_ref, q_ref, peak_ref, space_ref, time_ref,
    out_ref, kv_ref, mask_ref, mix_ref,
):
    width = own_ref.shape[1]
    heads = width // HEAD
    cols = LANES
    rows = own_ref.shape[0] // cols
    size = rows * BLOCK
    pitch = kv_ref.shape[0] // rows
    index = lax.axis_index(AXIS)
    odd = index % 2
    invalid = (index == 0) | (index == lax.axis_size(AXIS) - 1)
    window_bias(mask_ref, 2 * RAD * odd, heads)
    shifted = normalize(far_ref[...], gain_ref[...][None, :])
    shifted = shift_columns(shifted, cols).astype(BF16)
    keys = jnp.dot(shifted, k_w[...], preferred_element_type=F32).astype(BF16)
    values = jnp.dot(shifted, v_w[...], preferred_element_type=F32).astype(BF16)
    store_keys(keys, heads, cols, pitch, kv_ref, invalid)
    store_values(values, heads, cols, pitch, kv_ref)
    low = lane_iota((1, LANES)) < HEAD
    mine = [value_mask(heads, 2 * j) | value_mask(heads, 2 * j + 1) for j in range(heads // 2)]

    def finish(block, pair, far_peak, far_space, far_times, scale):
        part = slice(block * size, (block + 1) * size)
        tile = slice(pair * LANES, (pair + 1) * LANES)
        near_peak = peak_ref[part, tile]
        peak = jnp.maximum(near_peak, far_peak)
        near = jnp.exp2((near_peak - peak) * scale)
        far = jnp.exp2((far_peak - peak) * scale)
        mean = space_ref[part, tile] * near + far_space * far
        times = jnp.where(mine[pair], time_ref[part, :] * near + far_times * far, 0.0)
        time = jnp.where(low, *half_sums(times))
        spread = time * time - jnp.where(low, *half_sums(mean * mean))
        attended = (mean * lax.rsqrt(spread)).astype(BF16)
        for r in range(rows):
            start = r * cols + block * BLOCK
            mix_ref[start : start + BLOCK, tile] = attended[r * BLOCK : (r + 1) * BLOCK]

    window_attention(q_ref, (kv_ref,), mask_ref, scale_ref, heads, finish)
    projected = jnp.dot(mix_ref[...], o_w[...], preferred_element_type=F32)
    out_ref[...] = (own_ref[...].astype(F32) + projected).astype(BF16)


def merge_body(scale_ref, mine_ref, other_ref, out_ref, *, count, step, last):
    upper = (lax.axis_index(AXIS) // step) % 2 > 0
    mine, other = mine_ref[...], other_ref[...]
    first, second = jnp.where(upper, other, mine), jnp.where(upper, mine, other)
    lane = lane_iota((count, LANES))
    low = lane < HEAD
    tiles = first.shape[0] // count - 1
    scale = jnp.zeros((count, LANES), F32)
    for h in range(2 * tiles):
        scale = jnp.where(lane == HEAD + h, scale_ref[h] * DOUBLE_LOG2E, scale)
    s1, s2 = first[tiles * count :], second[tiles * count :]
    peak = jnp.maximum(s1, s2)
    f1 = jnp.exp2((s1 - peak) * scale)
    f2 = jnp.exp2((s2 - peak) * scale)
    time = s1 * pltpu.roll(f1, HEAD, 1) + s2 * pltpu.roll(f2, HEAD, 1)
    stats = jnp.where(low, time, peak)
    for j in range(tiles):
        part = slice(j * count, (j + 1) * count)
        a, b = HEAD + 2 * j, HEAD + 2 * j + 1
        g1 = jnp.where(low, f1[:, a : a + 1], f1[:, b : b + 1])
        g2 = jnp.where(low, f2[:, a : a + 1], f2[:, b : b + 1])
        mean = first[part] * g1 + second[part] * g2
        if not last:
            out_ref[part, :] = mean
            continue
        time = jnp.where(low, stats[:, 2 * j : 2 * j + 1], stats[:, 2 * j + 1 : 2 * j + 2])
        one, two = half_sums(mean * mean)
        out_ref[:, j * LANES : (j + 1) * LANES] = mean / jnp.sqrt(
            time * time - jnp.where(low, one, two)
        )
    if not last:
        out_ref[tiles * count :, :] = stats


SMEM = pl.BlockSpec(memory_space=pltpu.SMEM)
VMEM = pl.BlockSpec(memory_space=pltpu.VMEM)
HBM = pl.BlockSpec(memory_space=pltpu.HBM)


def local_call(body, specs, args, outs, scratch=(), limit=24):
    return pl.pallas_call(
        body,
        out_shape=outs,
        in_specs=list(specs),
        out_specs=jax.tree.map(lambda _: VMEM, outs),
        scratch_shapes=list(scratch),
        compiler_params=pltpu.CompilerParams(vmem_limit_bytes=limit << 20),
    )(*args)


def exchange(value, pairs):
    return lax.ppermute(value, AXIS, pairs)


def per_device(
    tokens, norm_gain, query_weight, key_weight, value_weight, out_weight, head_scale, pool_queries
):
    rows, cols, width = tokens.shape
    heads = head_scale.shape[0]
    count = pool_queries.shape[0]
    ring = lax.axis_size(AXIS)
    assert rows == RAD and cols == LANES and width == heads * HEAD
    assert ring & (ring - 1) == 0 and ring > 1
    struct = jax.ShapeDtypeStruct
    cells = rows * cols
    own = tokens.reshape(cells, width)
    swap = [(i, i ^ 1) for i in range(ring)]
    cross = [(i, i + 1) for i in range(1, ring - 1, 2)]
    cross = cross + [(b, a) for a, b in cross]
    far = exchange(own, cross)
    extra = width + LANES
    pitch = cols + WIDE - BLOCK
    keys_values, queries = local_call(
        project_body,
        (VMEM, HBM, HBM, HBM, HBM),
        (norm_gain, own, query_weight, key_weight, value_weight),
        (struct((rows * pitch, 2 * extra), BF16), struct((cells, extra), BF16)),
        [pltpu.VMEM((cells, width), BF16)]
        + [pltpu.VMEM((width, width), BF16)] * 3
        + [pltpu.SemaphoreType.DMA((4,))],
        limit=60,
    )
    mate = exchange(keys_values, swap)
    part = local_call(
        pool_body,
        (SMEM, VMEM, VMEM),
        (head_scale, pool_queries, keys_values),
        struct(((width // LANES + 1) * count, LANES), F32),
    )
    near = local_call(
        near_body,
        (SMEM, VMEM, VMEM, VMEM),
        (head_scale, queries, keys_values, mate),
        (
            struct((cells, width), F32),
            struct((cells, width), F32),
            struct((cells, LANES), F32),
        ),
        [pltpu.VMEM((2 * rows * WIDE, LANES), BF16)],
    )
    for hop in range(ring.bit_length() - 1):
        step = 1 << hop
        other = exchange(part, [(i, i ^ step) for i in range(ring)])
        last = 2 * step >= ring
        part = local_call(
            lambda *refs, step=step, last=last: merge_body(
                *refs, count=count, step=step, last=last
            ),
            (SMEM, VMEM, VMEM),
            (head_scale, part, other),
            struct((count, width) if last else part.shape, F32),
            limit=4,
        )
    mixed = local_call(
        far_body,
        (SMEM,) + (VMEM,) * 10,
        (head_scale, norm_gain, far, key_weight, value_weight, out_weight, own, queries, *near),
        struct((cells, width), BF16),
        [
            pltpu.VMEM((rows * pitch, 2 * extra), BF16),
            pltpu.VMEM((rows * WIDE, LANES), BF16),
            pltpu.VMEM((cells, width), BF16),
        ],
    )
    return mixed.reshape(rows, cols, width), part


def solution(mesh):
    placed = (P(("slide", "row"), None, None), P(), P(), P(), P(), P(), P(), P())
    return jax.shard_map(
        per_device,
        mesh=mesh,
        in_specs=placed,
        out_specs=(P(("slide", "row"), None, None), P("slide", None)),
        check_vma=False,
    )
```

time: 62.6 us -> 58.4 us (0.933)
  Pallas kernels: 35.6 us -> 25.6 us
  starting transfers between devices: 11.7 us -> 20.1 us
  local copies, waits for them, and re-layouts: 9.05 us -> 1.61 us
  waiting for transfers between devices: 3.05 us -> 10.1 us
  other arithmetic: 2.06 us -> 0 us
    pallas_call x6 -> x8, Pallas kernels: 35.6 us -> 25.6 us  [local_call(): pl.pallas_call(body, out_shape=outs, in_specs=list(specs), out_specs=jax....]
    ppermute x5 -> x6, starting transfers between devices: 11.7 us -> 20.1 us  [exchange(): return lax.ppermute(value, AXIS, pairs)]
    ppermute x5 -> x6, waiting for transfers between devices: 3.05 us -> 10.1 us  [exchange(): return lax.ppermute(value, AXIS, pairs)]
    unnamed x20 -> x18, local copies, waits for them, and re-layouts: 6.89 us -> 1.61 us
    another operation x4 -> x0, other arithmetic: 2.06 us -> none
    scatter x1 -> x0, local copies, waits for them, and re-layouts: 0.89 us -> none  [per_device(): lane_scale = jnp.zeros((1, LANES), F32).at[0, HEAD:HEAD + heads].set(scale)]
    reshape x1 -> x0, local copies, waits for them, and re-layouts: 0.69 us -> none  [per_device(): gain = norm_gain.reshape(1, width)]
  transfers between devices with their start and end apart: 5 -> 6, of which waited for: 2 -> 4; matrix products, arithmetic and copies ran while one was open for 7% -> 0% of each run, Pallas kernels for 56% -> 16%
where the time goes in v2:
time: 58.4 us; the launch traced here: 58.2 us
  Pallas kernels  25.6 us (44%)
  starting transfers between devices  20.1 us (34%)
  waiting for transfers between devices  10.1 us (17%)
  local copies, waits for them, and re-layouts  1.61 us (3%)
  between operations  0.79 us (1%)
    pallas_call x8, Pallas kernels, local_call(): pl.pallas_call(body, out_shape=outs, in_specs=list(specs), out_specs=jax....  25.6 us
    ppermute x6, starting transfers between devices, exchange(): return lax.ppermute(value, AXIS, pairs)  20.1 us
    ppermute x6, waiting for transfers between devices, exchange(): return lax.ppermute(value, AXIS, pairs)  10.1 us
    unnamed x18, local copies, waits for them, and re-layouts  1.61 us
  transfers between devices with their start and end apart: 6, of which 4 were waited for; matrix products, arithmetic and copies ran while one was open for 0% of the time, Pallas kernels for 16%

profile of v2, /device:TPU:0, one launch (start us, length us, event | category | flops | bytes accessed | tf_op | source)
XLA Modules:
  0.0 58.2 jit_solution(13670087626766222306)
XLA Ops:
  0.6 0.0 copy-start.4
  0.6 0.0 copy-start.6
  0.7 0.0 copy-start.7
  0.7 8.1 %shard_map.95 = (bf16[576,1792]{1,0:T(8,128)(2,1)}, bf16[512,896]{1,0:T(8,128)(2,1)}) custom-call(f32[768]{0:T(1024)} %gain_ref.3, bf16[512,768]{1,0:T(8,128)(2,1)} %bitcast.2, bf16[768,768]{1,0:T(8,128)(2,1)} %q_hbm.1, bf16[768,768]{1,0:T(8,128)(2,1)} %k_w.1, bf16[768,768]{1,0:T(8,128)(2,1)} %v_w.1), custom_call_target="tpu_custom_call" | custom-call | tf_op jit(solution)/shard_map/pallas_call | solution.py:465
  8.7 0.6 collective-permute-start.1
  9.3 0.0 copy-done.4
  9.3 0.9 %collective-permute-start = (bf16[512,768]{1,0:T(8,128)(2,1)S(1)}, bf16[512,768]{1,0:T(8,128)(2,1)S(1)}, u32[]{:S(2)}, u32[]{:S(2)}) collective-permute-start(bf16[512,768]{1,0:T(8,128)(2,1)S(1)} %bitcast.3), channel_id=1, source_target_pairs={{1,2},{3,4},{5,6},{7,8},{9,10},{11,12},{13,14},{2,1},{4,3},{6,5},{... | collective-permute-start | bytes 2359304 | tf_op jit(solution)/shard_map/ppermute | solution.py:476
  10.2 0.0 copy-done.6
  10.2 0.0 copy-done.7
  10.2 0.0 copy-start
  10.2 1.6 %copy-done = bf16[576,1792]{1,0:T(8,128)(2,1)S(1)} copy-done((bf16[576,1792]{1,0:T(8,128)(2,1)S(1)}, bf16[576,1792]{1,0:T(8,128)(2,1)}, u32[]{:S(2)}) %copy-start) | copy-done | bytes 2064408
  11.8 0.0 copy-start.3
  11.8 1.7 %shard_map.98.refs_1_ = f32[112,128]{1,0:T(8,128)S(1)} custom-call(f32[12]{0:T(128)S(1)} %copy-done.6, bf16[16,768]{1,0:T(8,128)(2,1)S(1)} %copy-done.7, bf16[576,1792]{1,0:T(8,128)(2,1)S(1)} %copy-done), custom_call_target="tpu_custom_call" | custom-call | tf_op jit(solution)/shard_map/pallas_call | solution.py:465
  13.5 3.9 %collective-permute-start.2 = (f32[112,128]{1,0:T(8,128)S(1)}, f32[112,128]{1,0:T(8,128)S(1)}, u32[]{:S(2)}, u32[]{:S(2)}) collective-permute-start(f32[112,128]{1,0:T(8,128)S(1)} %shard_map.98.refs_1_), channel_id=1, source_target_pairs={{0,1},{1,0},{2,3},{3,2},{4,5},{5,4},{6,7},{7,6},{8,9},{9,8},{10,11... | collective-permute-start | bytes 172040 | tf_op jit(solution)/shard_map/ppermute | solution.py:476
  17.4 0.9 %collective-permute-done.2.refs_2_ = f32[112,128]{1,0:T(8,128)S(1)} collective-permute-done((f32[112,128]{1,0:T(8,128)S(1)}, f32[112,128]{1,0:T(8,128)S(1)}, u32[]{:S(2)}, u32[]{:S(2)}) %collective-permute-start.2) | collective-permute-done | bytes 57376 | tf_op jit(solution)/shard_map/ppermute | solution.py:476
  18.3 0.7 %shard_map.99.refs_1_ = f32[112,128]{1,0:T(8,128)S(1)} custom-call(f32[12]{0:T(128)S(1)} %copy-done.6, f32[112,128]{1,0:T(8,128)S(1)} %shard_map.98.refs_1_, f32[112,128]{1,0:T(8,128)S(1)} %collective-permute-done.2.refs_2_), custom_call_target="tpu_custom_call" | custom-call | tf_op jit(solution)/shard_map/pallas_call | solution.py:465
  19.0 1.6 %collective-permute-start.3 = (f32[112,128]{1,0:T(8,128)S(1)}, f32[112,128]{1,0:T(8,128)S(1)}, u32[]{:S(2)}, u32[]{:S(2)}) collective-permute-start(f32[112,128]{1,0:T(8,128)S(1)} %shard_map.99.refs_1_), channel_id=1, source_target_pairs={{0,2},{1,3},{2,0},{3,1},{4,6},{5,7},{6,4},{7,5},{8,10},{9,11},{10,... | collective-permute-start | bytes 172040 | tf_op jit(solution)/shard_map/ppermute | solution.py:476
  20.6 4.9 %collective-permute-done.3.refs_2_ = f32[112,128]{1,0:T(8,128)S(1)} collective-permute-done((f32[112,128]{1,0:T(8,128)S(1)}, f32[112,128]{1,0:T(8,128)S(1)}, u32[]{:S(2)}, u32[]{:S(2)}) %collective-permute-start.3) | collective-permute-done | bytes 57376 | tf_op jit(solution)/shard_map/ppermute | solution.py:476
  25.5 0.7 %shard_map.100.refs_1_ = f32[112,128]{1,0:T(8,128)S(1)} custom-call(f32[12]{0:T(128)S(1)} %copy-done.6, f32[112,128]{1,0:T(8,128)S(1)} %shard_map.99.refs_1_, f32[112,128]{1,0:T(8,128)S(1)} %collective-permute-done.3.refs_2_), custom_call_target="tpu_custom_call" | custom-call | tf_op jit(solution)/shard_map/pallas_call | solution.py:465
  26.2 10.0 %collective-permute-start.4 = (f32[112,128]{1,0:T(8,128)S(1)}, f32[112,128]{1,0:T(8,128)S(1)}, u32[]{:S(2)}, u32[]{:S(2)}) collective-permute-start(f32[112,128]{1,0:T(8,128)S(1)} %shard_map.100.refs_1_), channel_id=1, source_target_pairs={{0,4},{1,5},{2,6},{3,7},{4,0},{5,1},{6,2},{7,3},{8,12},{9,13},{10,... | collective-permute-start | bytes 172040 | tf_op jit(solution)/shard_map/ppermute | solution.py:476
  36.3 2.2 %collective-permute-done.4.refs_2_ = f32[112,128]{1,0:T(8,128)S(1)} collective-permute-done((f32[112,128]{1,0:T(8,128)S(1)}, f32[112,128]{1,0:T(8,128)S(1)}, u32[]{:S(2)}, u32[]{:S(2)}) %collective-permute-start.4) | collective-permute-done | bytes 57376 | tf_op jit(solution)/shard_map/ppermute | solution.py:476
  38.4 0.7 %shard_map.101.refs_1_ = f32[112,128]{1,0:T(8,128)S(1)} custom-call(f32[12]{0:T(128)S(1)} %copy-done.6, f32[112,128]{1,0:T(8,128)S(1)} %shard_map.100.refs_1_, f32[112,128]{1,0:T(8,128)S(1)} %collective-permute-done.4.refs_2_), custom_call_target="tpu_custom_call" | custom-call | tf_op jit(solution)/shard_map/pallas_call | solution.py:465
  39.2 3.1 %collective-permute-start.5 = (f32[112,128]{1,0:T(8,128)S(1)}, f32[112,128]{1,0:T(8,128)S(1)}, u32[]{:S(2)}, u32[]{:S(2)}) collective-permute-start(f32[112,128]{1,0:T(8,128)S(1)} %shard_map.101.refs_1_), channel_id=1, source_target_pairs={{0,8},{1,9},{2,10},{3,11},{4,12},{5,13},{6,14},{7,15},{8,0},{9,1},... | collective-permute-start | bytes 172040 | tf_op jit(solution)/shard_map/ppermute | solution.py:476
  42.3 2.2 %collective-permute-done.5.refs_2_ = f32[112,128]{1,0:T(8,128)S(1)} collective-permute-done((f32[112,128]{1,0:T(8,128)S(1)}, f32[112,128]{1,0:T(8,128)S(1)}, u32[]{:S(2)}, u32[]{:S(2)}) %collective-permute-start.5) | collective-permute-done | bytes 57376 | tf_op jit(solution)/shard_map/ppermute | solution.py:476
  44.4 1.7 %shard_map.102 = f32[16,768]{1,0:T(8,128)} custom-call(f32[12]{0:T(128)S(1)} %copy-done.6, f32[112,128]{1,0:T(8,128)S(1)} %shard_map.101.refs_1_, f32[112,128]{1,0:T(8,128)S(1)} %collective-permute-done.5.refs_2_), custom_call_target="tpu_custom_call" | custom-call | tf_op jit(solution)/shard_map/pallas_call | solution.py:465
  46.1 0.0 collective-permute-done.1.mate_ref
  46.1 0.0 copy-done.3
  46.1 0.0 copy-start.1
  46.1 0.0 copy-start.2
  46.2 0.0 copy-start.5
  46.2 0.0 copy-start.8
  46.2 4.0 %shard_map.96 = (f32[512,768]{1,0:T(8,128)S(1)}, f32[512,768]{1,0:T(8,128)S(1)}, f32[512,128]{1,0:T(8,128)S(1)}) custom-call(f32[12]{0:T(128)S(1)} %copy-done.6, bf16[512,896]{1,0:T(8,128)(2,1)S(1)} %copy-done.3, bf16[576,1792]{1,0:T(8,128)(2,1)S(1)} %copy-done, bf16[576,1792]{1,0:T(8,128)(2,1)S(1)} %collective-permute-done.1.mate_ref), custom_call_target="tpu_custom_call" | custom-call | tf_op jit(solution)/shard_map/pallas_call | solution.py:465
  50.2 0.0 collective-permute-done.far_ref
  50.2 0.0 copy-done.1
  50.2 0.0 copy-done.2
  50.3 0.0 copy-done.5
  50.3 0.0 copy-done.8
  50.3 7.9 %shard_map.97 = bf16[512,768]{1,0:T(8,128)(2,1)} custom-call(f32[12]{0:T(128)S(1)} %copy-done.6, f32[768]{0:T(1024)S(1)} %copy-done.8, bf16[512,768]{1,0:T(8,128)(2,1)S(1)} %collective-permute-done.far_ref, bf16[768,768]{1,0:T(8,128)(2,1)S(1)} %copy-done.1, bf16[768,768]{1,0:T(8,128)(2,1)S(1)} %copy-done.2, bf16[768,768]{1,0:T(8,128)(2,1)S(1)} %copy-done.5, ...), custom_call_target="tpu_custom_call" | custom-call | tf_op jit(solution)/shard_map/pallas_call | solution.py:465
Async XLA Ops:
  0.6 8.7 %copy-start.4 = (bf16[4,128,768]{2,1,0:T(8,128)(2,1)S(1)}, bf16[4,128,768]{2,1,0:T(8,128)(2,1)}, u32[]{:S(2)}) copy-start(bf16[4,128,768]{2,1,0:T(8,128)(2,1)} %param.8) | copy-start | bytes 2359300
  0.6 9.5 %copy-start.6 = (f32[12]{0:T(128)S(1)}, f32[12]{0:T(128)}, u32[]{:S(2)}) copy-start(f32[12]{0:T(128)} %refs_0_.7) | copy-start | bytes 148
  0.7 9.5 %copy-start.7 = (bf16[16,768]{1,0:T(8,128)(2,1)S(1)}, bf16[16,768]{1,0:T(8,128)(2,1)}, u32[]{:S(2)}) copy-start(bf16[16,768]{1,0:T(8,128)(2,1)} %pool_ref.1) | copy-start | bytes 73732
  8.7 37.4 %collective-permute-start.1 = (bf16[576,1792]{1,0:T(8,128)(2,1)}, bf16[576,1792]{1,0:T(8,128)(2,1)S(1)}, u32[]{:S(2)}, u32[]{:S(2)}) collective-permute-start(bf16[576,1792]{1,0:T(8,128)(2,1)} %get-tuple-element.8.own_ref.kv_ref), channel_id=1, source_target_pairs={{0,1},{1,0},{2,3},{3,2},{4,5},{5,4},{6,7},{7,6},{8,9},{9,8},{10,11... | collective-permute-start | bytes 6193160 | tf_op jit(solution)/shard_map/ppermute | solution.py:476
  9.3 40.9 %collective-permute-start = (bf16[512,768]{1,0:T(8,128)(2,1)S(1)}, bf16[512,768]{1,0:T(8,128)(2,1)S(1)}, u32[]{:S(2)}, u32[]{:S(2)}) collective-permute-start(bf16[512,768]{1,0:T(8,128)(2,1)S(1)} %bitcast.3), channel_id=1, source_target_pairs={{1,2},{3,4},{5,6},{7,8},{9,10},{11,12},{13,14},{2,1},{4,3},{6,5},{... | collective-permute-start | bytes 2359304 | tf_op jit(solution)/shard_map/ppermute | solution.py:476
  10.2 1.6 %copy-start = (bf16[576,1792]{1,0:T(8,128)(2,1)S(1)}, bf16[576,1792]{1,0:T(8,128)(2,1)}, u32[]{:S(2)}) copy-start(bf16[576,1792]{1,0:T(8,128)(2,1)} %get-tuple-element.8.own_ref.kv_ref) | copy-start | bytes 6193156
  11.8 34.4 %copy-start.3 = (bf16[512,896]{1,0:T(8,128)(2,1)S(1)}, bf16[512,896]{1,0:T(8,128)(2,1)}, u32[]{:S(2)}) copy-start(bf16[512,896]{1,0:T(8,128)(2,1)} %get-tuple-element.7.q_ref) | copy-start | bytes 2752516
  13.5 4.8 %collective-permute-start.2 = (f32[112,128]{1,0:T(8,128)S(1)}, f32[112,128]{1,0:T(8,128)S(1)}, u32[]{:S(2)}, u32[]{:S(2)}) collective-permute-start(f32[112,128]{1,0:T(8,128)S(1)} %shard_map.98.refs_1_), channel_id=1, source_target_pairs={{0,1},{1,0},{2,3},{3,2},{4,5},{5,4},{6,7},{7,6},{8,9},{9,8},{10,11... | collective-permute-start | bytes 172040 | tf_op jit(solution)/shard_map/ppermute | solution.py:476
  19.0 6.5 %collective-permute-start.3 = (f32[112,128]{1,0:T(8,128)S(1)}, f32[112,128]{1,0:T(8,128)S(1)}, u32[]{:S(2)}, u32[]{:S(2)}) collective-permute-start(f32[112,128]{1,0:T(8,128)S(1)} %shard_map.99.refs_1_), channel_id=1, source_target_pairs={{0,2},{1,3},{2,0},{3,1},{4,6},{5,7},{6,4},{7,5},{8,10},{9,11},{10,... | collective-permute-start | bytes 172040 | tf_op jit(solution)/shard_map/ppermute | solution.py:476
  26.2 12.2 %collective-permute-start.4 = (f32[112,128]{1,0:T(8,128)S(1)}, f32[112,128]{1,0:T(8,128)S(1)}, u32[]{:S(2)}, u32[]{:S(2)}) collective-permute-start(f32[112,128]{1,0:T(8,128)S(1)} %shard_map.100.refs_1_), channel_id=1, source_target_pairs={{0,4},{1,5},{2,6},{3,7},{4,0},{5,1},{6,2},{7,3},{8,12},{9,13},{10,... | collective-permute-start | bytes 172040 | tf_op jit(solution)/shard_map/ppermute | solution.py:476
  39.2 5.3 %collective-permute-start.5 = (f32[112,128]{1,0:T(8,128)S(1)}, f32[112,128]{1,0:T(8,128)S(1)}, u32[]{:S(2)}, u32[]{:S(2)}) collective-permute-start(f32[112,128]{1,0:T(8,128)S(1)} %shard_map.101.refs_1_), channel_id=1, source_target_pairs={{0,8},{1,9},{2,10},{3,11},{4,12},{5,13},{6,14},{7,15},{8,0},{9,1},... | collective-permute-start | bytes 172040 | tf_op jit(solution)/shard_map/ppermute | solution.py:476
  46.1 4.1 %copy-start.1 = (bf16[768,768]{1,0:T(8,128)(2,1)S(1)}, bf16[768,768]{1,0:T(8,128)(2,1)}, u32[]{:S(2)}) copy-start(bf16[768,768]{1,0:T(8,128)(2,1)} %k_w.1) | copy-start | bytes 3538948
  46.1 4.1 %copy-start.2 = (bf16[768,768]{1,0:T(8,128)(2,1)S(1)}, bf16[768,768]{1,0:T(8,128)(2,1)}, u32[]{:S(2)}) copy-start(bf16[768,768]{1,0:T(8,128)(2,1)} %v_w.1) | copy-start | bytes 3538948
  46.2 4.1 %copy-start.5 = (bf16[768,768]{1,0:T(8,128)(2,1)S(1)}, bf16[768,768]{1,0:T(8,128)(2,1)}, u32[]{:S(2)}) copy-start(bf16[768,768]{1,0:T(8,128)(2,1)} %o_w.1) | copy-start | bytes 3538948
  46.2 4.1 %copy-start.8 = (f32[768]{0:T(1024)S(1)}, f32[768]{0:T(1024)}, u32[]{:S(2)}) copy-start(f32[768]{0:T(1024)} %gain_ref.3) | copy-start | bytes 9220

commit v3 on v2

--- a/solution.py
+++ b/solution.py
@@ -78,9 +78,20 @@
     )
 
 
-def time_pieces(points, heads, head):
+def time_pieces(points, heads, head, matmul_tiles=0):
+    tiles = heads // 2
+    split = (tiles - matmul_tiles) * LANES
     total = jnp.zeros((points.shape[0], LANES), F32)
-    for j in range(heads // 2):
+    if matmul_tiles:
+        f = points[:, split:].astype(F32)
+        sq = f * f
+        hi = sq.astype(BF16)
+        lo = (sq - hi.astype(F32)).astype(BF16)
+        hit = row_iota((sq.shape[1], LANES)) // HEAD + split // HEAD == head
+        sums = as_factor(hit)
+        total = jnp.dot(hi, sums, preferred_element_type=F32)
+        total = total + jnp.dot(lo, sums, preferred_element_type=F32)
+    for j in range(tiles - matmul_tiles):
         f = points[:, j * LANES : (j + 1) * LANES].astype(F32)
         first, second = half_sums(f * f)
         total = jnp.where(head == 2 * j, first, jnp.where(head == 2 * j + 1, second, total))
@@ -145,7 +156,7 @@
     width = heads * HEAD
     base = width + LANES
     store_rows(ref, pitch, cols, values, base)
-    times = value_times(time_pieces(values, heads, value_lane_heads(heads)), heads).astype(BF16)
+    times = value_times(time_pieces(values, heads, value_lane_heads(heads), heads // 4), heads).astype(BF16)
     store_rows(ref, pitch, cols, times, base + width)
 
 
@@ -181,12 +192,11 @@
     return jnp.where(hit, 1.0, 0.0).astype(BF16)
 
 
-def window_attention(q_ref, kv_refs, mask_ref, scale_ref, heads, finish):
+def window_attention(q_ref, kv_refs, mask_ref, scale_ref, heads, blocks, finish):
     width = heads * HEAD
     extra = width + LANES
     cols = LANES
     rows = q_ref.shape[0] // cols
-    blocks = cols // BLOCK
     pairs = range(heads // 2)
     lane = lane_iota((1, LANES))
     low = lane < HEAD
@@ -229,11 +239,12 @@
             preferred_element_type=F32,
         )
 
-    extra_now = extras(0)
-    scores = [scores_of(0, pair, *extra_now) for pair in pairs]
+    first, last = blocks[0], blocks[-1]
+    extra_now = extras(first)
+    scores = [scores_of(first, pair, *extra_now) for pair in pairs]
     behind = None
-    for block in range(blocks):
-        ahead = extras(block + 1) if block + 1 < blocks else None
+    for block in blocks:
+        ahead = extras(block + 1) if block < last else None
         peaks, coming = [], []
         for pair in pairs:
             peaks.append(jnp.max(scores[pair], axis=-1, keepdims=True))
@@ -266,52 +277,48 @@
             )
         scores = coming
     for pair in pairs:
-        finish(blocks - 1, pair, *behind[pair])
-
-
-def project_body(
-    gain_ref, own_hbm, q_hbm, k_hbm, v_hbm, kv_ref, q_ref, own_ref, q_w, k_w, v_w, sems
-):
-    copies = [
-        pltpu.make_async_copy(src, dst, sems.at[i])
-        for i, (src, dst) in enumerate(
-            ((own_hbm, own_ref), (k_hbm, k_w), (v_hbm, v_w), (q_hbm, q_w))
-        )
-    ]
+        finish(last, pair, *behind[pair])
+
+
+def project_body(gain_hbm, own_hbm, k_hbm, v_hbm, kv_ref, normed_ref, gain_ref, own_ref, k_w, v_w, sems):
+    cells, width = own_ref.shape
+    heads = width // HEAD
+    cols = LANES
+    rows = cells // cols
+    pitch = kv_ref.shape[0] // rows
+    strips = [slice(r * cols, (r + 1) * cols) for r in range(rows)]
+    moves = [(gain_hbm, gain_ref)] + [(own_hbm.at[part], own_ref.at[part]) for part in strips]
+    moves += [(k_hbm, k_w), (v_hbm, v_w)]
+    copies = [pltpu.make_async_copy(src, dst, sems.at[i]) for i, (src, dst) in enumerate(moves)]
     for copy in copies:
         copy.start()
-    width = own_ref.shape[1]
-    heads = width // HEAD
-    cols = LANES
-    rows = own_ref.shape[0] // cols
-    pitch = kv_ref.shape[0] // rows
     copies[0].wait()
-    normed = normalize(own_ref[...], gain_ref[...][None, :])
-    shifted = shift_columns(normed, cols).astype(BF16)
-    normed = normed.astype(BF16)
-    copies[1].wait()
+    gain = gain_ref[...][None, :]
+    shifted = []
+    for r, part in enumerate(strips):
+        copies[1 + r].wait()
+        normed = normalize(own_ref[part], gain)
+        normed_ref[part] = normed.astype(BF16)
+        shifted.append(pltpu.roll(normed, RAD, 0).astype(BF16))
+    shifted = jnp.concatenate(shifted, axis=0)
+    copies[-2].wait()
     keys = jnp.dot(shifted, k_w[...], preferred_element_type=F32).astype(BF16)
-    copies[2].wait()
+    copies[-1].wait()
     values = jnp.dot(shifted, v_w[...], preferred_element_type=F32).astype(BF16)
     store_keys(keys, heads, cols, pitch, kv_ref, None)
-    copies[3].wait()
-    queries = jnp.dot(normed, q_w[...], preferred_element_type=F32).astype(BF16)
     store_values(values, heads, cols, pitch, kv_ref)
-    q_ref[:, :width] = queries
-    times = query_times(time_pieces(queries, heads, lane_heads(heads)), heads)
-    for r in range(rows):
-        part = slice(r * cols, (r + 1) * cols)
-        q_ref[part, width:] = (times[part] + query_features(cols, heads, r)).astype(BF16)
-
-
-def pool_body(scale_ref, pool_ref, kv_ref, out_ref):
+
+
+def query_body(scale_ref, pool_ref, normed_ref, q_hbm, kv_ref, q_ref, out_ref, q_w, sem):
+    copy = pltpu.make_async_copy(q_hbm, q_w, sem)
+    copy.start()
     pq = pool_ref[...]
     count, width = pq.shape
     heads = width // HEAD
     cols = LANES
     extra = width + LANES
-    pitch = cols + WIDE - BLOCK
-    rows = kv_ref.shape[0] // pitch
+    rows = q_ref.shape[0] // cols
+    pitch = kv_ref.shape[0] // rows
     lane = lane_iota((count, LANES))
     q_time = query_times(time_pieces(pq, heads, lane_heads(heads)), heads)
     zero = jnp.zeros((count, LANES), F32)
@@ -326,12 +333,20 @@
     keys = jnp.concatenate(
         [kv_ref[r * pitch : r * pitch + cols, :extra] for r in range(rows)], axis=0
     )
+    copy.wait()
+    queries = jnp.dot(normed_ref[...], q_w[...], preferred_element_type=F32).astype(BF16)
+    q_ref[:, :width] = queries
     scores = lax.dot_general(q_all, keys, NT, preferred_element_type=F32)
-    peak = jnp.max(scores, axis=-1, keepdims=True)
+    times = query_times(time_pieces(queries, heads, lane_heads(heads)), heads)
+    for r in range(rows):
+        part = slice(r * cols, (r + 1) * cols)
+        q_ref[part, width:] = (times[part] + query_features(cols, heads, r)).astype(BF16)
     scale = jnp.concatenate(
         [jnp.full((count, 1), scale_ref[h] * DOUBLE_LOG2E, F32) for h in range(heads)], axis=0
     )
-    f = jnp.exp2((scores - peak) * scale)
+    scores = scores * scale
+    peak = jnp.max(scores, axis=-1, keepdims=True)
+    f = jnp.exp2(scores - peak)
     hi = f.astype(BF16)
     lo = (f - hi.astype(F32)).astype(BF16)
     values = jnp.concatenate(
@@ -353,7 +368,7 @@
     out_ref[width // LANES * count :, :] = stats
 
 
-def near_body(scale_ref, q_ref, own_ref, mate_ref, peak_ref, space_ref, time_ref, mask_ref):
+def near_body(scale_ref, q_ref, own_ref, mate_ref, peak_ref, space_ref, time_ref, mask_ref, *, blocks):
     width = q_ref.shape[1] - LANES
     heads = width // HEAD
     size = q_ref.shape[0] // LANES * BLOCK
@@ -365,7 +380,8 @@
     block_times = {}
 
     def finish(block, pair, peak, space, times, scale):
-        part = slice(block * size, (block + 1) * size)
+        place = block - blocks[0]
+        part = slice(place * size, (place + 1) * size)
         tile = slice(pair * LANES, (pair + 1) * LANES)
         peak_ref[part, tile] = peak
         space_ref[part, tile] = space
@@ -375,12 +391,12 @@
         if pair == heads // 2 - 1:
             time_ref[part, :] = times
 
-    window_attention(q_ref, (own_ref, mate_ref), mask_ref, scale_ref, heads, finish)
+    window_attention(q_ref, (own_ref, mate_ref), mask_ref, scale_ref, heads, blocks, finish)
 
 
 def far_body(
-    scale_ref, gain_ref, far_ref, k_w, v_w, o_w, own_ref, q_ref, peak_ref, space_ref, time_ref,
-    out_ref, kv_ref, mask_ref, mix_ref,
+    scale_ref, gain_ref, far_ref, k_w, v_w, o_w, own_ref, q_ref,
+    peak_a, space_a, time_a, peak_b, space_b, time_b, out_ref, kv_ref, mask_ref, mix_ref,
 ):
     width = own_ref.shape[1]
     heads = width // HEAD
@@ -402,7 +418,12 @@
     mine = [value_mask(heads, 2 * j) | value_mask(heads, 2 * j + 1) for j in range(heads // 2)]
 
     def finish(block, pair, far_peak, far_space, far_times, scale):
-        part = slice(block * size, (block + 1) * size)
+        second = block * size >= peak_a.shape[0]
+        peak_ref, space_ref, time_ref = (
+            (peak_b, space_b, time_b) if second else (peak_a, space_a, time_a)
+        )
+        place = block * size - (peak_a.shape[0] if second else 0)
+        part = slice(place, place + size)
         tile = slice(pair * LANES, (pair + 1) * LANES)
         near_peak = peak_ref[part, tile]
         peak = jnp.maximum(near_peak, far_peak)
@@ -417,25 +438,22 @@
             start = r * cols + block * BLOCK
             mix_ref[start : start + BLOCK, tile] = attended[r * BLOCK : (r + 1) * BLOCK]
 
-    window_attention(q_ref, (kv_ref,), mask_ref, scale_ref, heads, finish)
+    window_attention(q_ref, (kv_ref,), mask_ref, scale_ref, heads, range(cols // BLOCK), finish)
     projected = jnp.dot(mix_ref[...], o_w[...], preferred_element_type=F32)
     out_ref[...] = (own_ref[...].astype(F32) + projected).astype(BF16)
 
 
-def merge_body(scale_ref, mine_ref, other_ref, out_ref, *, count, step, last):
+def merge_body(mine_ref, other_ref, out_ref, *, count, step, last):
     upper = (lax.axis_index(AXIS) // step) % 2 > 0
     mine, other = mine_ref[...], other_ref[...]
     first, second = jnp.where(upper, other, mine), jnp.where(upper, mine, other)
     lane = lane_iota((count, LANES))
     low = lane < HEAD
     tiles = first.shape[0] // count - 1
-    scale = jnp.zeros((count, LANES), F32)
-    for h in range(2 * tiles):
-        scale = jnp.where(lane == HEAD + h, scale_ref[h] * DOUBLE_LOG2E, scale)
     s1, s2 = first[tiles * count :], second[tiles * count :]
     peak = jnp.maximum(s1, s2)
-    f1 = jnp.exp2((s1 - peak) * scale)
-    f2 = jnp.exp2((s2 - peak) * scale)
+    f1 = jnp.exp2(jnp.where(low, 0.0, s1 - peak))
+    f2 = jnp.exp2(jnp.where(low, 0.0, s2 - peak))
     time = s1 * pltpu.roll(f1, HEAD, 1) + s2 * pltpu.roll(f2, HEAD, 1)
     stats = jnp.where(low, time, peak)
     for j in range(tiles):
@@ -484,7 +502,7 @@
     count = pool_queries.shape[0]
     ring = lax.axis_size(AXIS)
     assert rows == RAD and cols == LANES and width == heads * HEAD
-    assert ring & (ring - 1) == 0 and ring > 1
+    assert ring & (ring - 1) == 0 and ring > 8
     struct = jax.ShapeDtypeStruct
     cells = rows * cols
     own = tokens.reshape(cells, width)
@@ -494,34 +512,45 @@
     far = exchange(own, cross)
     extra = width + LANES
     pitch = cols + WIDE - BLOCK
-    keys_values, queries = local_call(
+    in_hbm = [
+        pltpu.with_memory_space_constraint(a, pltpu.HBM)
+        for a in (norm_gain, own, key_weight, value_weight, query_weight)
+    ]
+    keys_values, normed = local_call(
         project_body,
-        (VMEM, HBM, HBM, HBM, HBM),
-        (norm_gain, own, query_weight, key_weight, value_weight),
-        (struct((rows * pitch, 2 * extra), BF16), struct((cells, extra), BF16)),
-        [pltpu.VMEM((cells, width), BF16)]
-        + [pltpu.VMEM((width, width), BF16)] * 3
-        + [pltpu.SemaphoreType.DMA((4,))],
-        limit=60,
+        (HBM,) * 4,
+        in_hbm[:4],
+        (struct((rows * pitch, 2 * extra), BF16), struct((cells, width), BF16)),
+        [pltpu.VMEM((width,), F32), pltpu.VMEM((cells, width), BF16)]
+        + [pltpu.VMEM((width, width), BF16)] * 2
+        + [pltpu.SemaphoreType.DMA((3 + rows,))],
     )
     mate = exchange(keys_values, swap)
-    part = local_call(
-        pool_body,
-        (SMEM, VMEM, VMEM),
-        (head_scale, pool_queries, keys_values),
-        struct(((width // LANES + 1) * count, LANES), F32),
-    )
-    near = local_call(
-        near_body,
-        (SMEM, VMEM, VMEM, VMEM),
-        (head_scale, queries, keys_values, mate),
+    queries, part = local_call(
+        query_body,
+        (SMEM, VMEM, VMEM, HBM, VMEM),
+        (head_scale, pool_queries, normed, in_hbm[4], keys_values),
         (
-            struct((cells, width), F32),
-            struct((cells, width), F32),
-            struct((cells, LANES), F32),
+            struct((cells, extra), BF16),
+            struct(((width // LANES + 1) * count, LANES), F32),
         ),
-        [pltpu.VMEM((2 * rows * WIDE, LANES), BF16)],
-    )
+        [pltpu.VMEM((width, width), BF16), pltpu.SemaphoreType.DMA(())],
+    )
+    near = []
+    split = cols // BLOCK // 2
+    for blocks in (range(split), range(split, 2 * split)):
+        size = split * rows * BLOCK
+        near += local_call(
+            lambda *refs, blocks=blocks: near_body(*refs, blocks=blocks),
+            (SMEM, VMEM, VMEM, VMEM),
+            (head_scale, queries, keys_values, mate),
+            (
+                struct((size, width), F32),
+                struct((size, width), F32),
+                struct((size, LANES), F32),
+            ),
+            [pltpu.VMEM((2 * rows * WIDE, LANES), BF16)],
+        )
     for hop in range(ring.bit_length() - 1):
         step = 1 << hop
         other = exchange(part, [(i, i ^ step) for i in range(ring)])
@@ -530,14 +559,14 @@
             lambda *refs, step=step, last=last: merge_body(
                 *refs, count=count, step=step, last=last
             ),
-            (SMEM, VMEM, VMEM),
-            (head_scale, part, other),
+            (VMEM, VMEM),
+            (part, other),
             struct((count, width) if last else part.shape, F32),
             limit=4,
         )
     mixed = local_call(
         far_body,
-        (SMEM,) + (VMEM,) * 10,
+        (SMEM,) + (VMEM,) * 13,
         (head_scale, norm_gain, far, key_weight, value_weight, out_weight, own, queries, *near),
         struct((cells, width), BF16),
         [

time: 58.4 us -> 53.4 us (0.914)
  Pallas kernels: 25.6 us -> 22.2 us
  local copies, waits for them, and re-layouts: 1.61 us -> 0.04 us
    pallas_call x8 -> x9, Pallas kernels: 25.6 us -> 22.2 us  [local_call(): pl.pallas_call(body, out_shape=outs, in_specs=list(specs), out_specs=jax....]
    unnamed x18 -> x14, local copies, waits for them, and re-layouts: 1.61 us -> 0.04 us
  transfers between devices with their start and end apart: 6 -> 6, of which waited for: 4 -> 4; matrix products, arithmetic and copies ran while one was open for 0% -> 0% of each run, Pallas kernels for 16% -> 19%
where the time goes in v3:
time: 53.4 us; the launch traced here: 53.2 us
  Pallas kernels  22.2 us (42%)
  starting transfers between devices  20.1 us (38%)
  waiting for transfers between devices  10.1 us (19%)
  between operations  0.8 us (1%)
    pallas_call x9, Pallas kernels, local_call(): pl.pallas_call(body, out_shape=outs, in_specs=list(specs), out_specs=jax....  22.2 us
    ppermute x6, starting transfers between devices, exchange(): return lax.ppermute(value, AXIS, pairs)  20.1 us
    ppermute x6, waiting for transfers between devices, exchange(): return lax.ppermute(value, AXIS, pairs)  10.1 us
  transfers between devices with their start and end apart: 6, of which 4 were waited for; matrix products, arithmetic and copies ran while one was open for 0% of the time, Pallas kernels for 19%

profile of v3, /device:TPU:0, one launch (start us, length us, event | category | flops | bytes accessed | tf_op | source)
XLA Modules:
  0.0 53.2 jit_solution(8945414403030438897)
XLA Ops:
  0.6 0.0 copy-start.2
  0.6 0.0 copy-start.4
  0.6 0.0 copy-start.6
  0.7 4.5 %shard_map.95 = (bf16[576,1792]{1,0:T(8,128)(2,1)S(1)}, bf16[512,768]{1,0:T(8,128)(2,1)S(1)}) custom-call(f32[768]{0:T(1024)} %gain_ref.1, bf16[512,768]{1,0:T(8,128)(2,1)} %bitcast.2, bf16[768,768]{1,0:T(8,128)(2,1)} %k_w.1, bf16[768,768]{1,0:T(8,128)(2,1)} %v_w.1), custom_call_target="tpu_custom_call" | custom-call | tf_op jit(solution)/shard_map/pallas_call | solution.py:483
  5.2 0.6 %collective-permute-start.1 = (bf16[576,1792]{1,0:T(8,128)(2,1)S(1)}, bf16[576,1792]{1,0:T(8,128)(2,1)S(1)}, u32[]{:S(2)}, u32[]{:S(2)}) collective-permute-start(bf16[576,1792]{1,0:T(8,128)(2,1)S(1)} %get-tuple-element.13.kv_ref.refs_2_), channel_id=1, source_target_pairs={{0,1},{1,0},{2,3},{3,2},{4,5},{5,4},{6,7},{7,6},{8,9},{9,8},{10,11... | collective-permute-start | bytes 6193160 | tf_op jit(solution)/shard_map/ppermute | solution.py:494
  5.7 0.0 copy-done.2
  5.7 0.9 %collective-permute-start = (bf16[512,768]{1,0:T(8,128)(2,1)S(1)}, bf16[512,768]{1,0:T(8,128)(2,1)S(1)}, u32[]{:S(2)}, u32[]{:S(2)}) collective-permute-start(bf16[512,768]{1,0:T(8,128)(2,1)S(1)} %bitcast.3), channel_id=1, source_target_pairs={{1,2},{3,4},{5,6},{7,8},{9,10},{11,12},{13,14},{2,1},{4,3},{6,5},{... | collective-permute-start | bytes 2359304 | tf_op jit(solution)/shard_map/ppermute | solution.py:494
  6.6 0.0 copy-done.4
  6.6 0.0 copy-done.6
  6.6 3.8 %shard_map.96 = (bf16[512,896]{1,0:T(8,128)(2,1)S(1)}, f32[112,128]{1,0:T(8,128)S(1)}) custom-call(f32[12]{0:T(128)S(1)} %copy-done.6, bf16[16,768]{1,0:T(8,128)(2,1)S(1)} %copy-done.4, bf16[512,768]{1,0:T(8,128)(2,1)S(1)} %get-tuple-element.12.normed_ref, bf16[768,768]{1,0:T(8,128)(2,1)} %q_hbm.1, bf16[576,1792]{1,0:T(8,128)(2,1)S(1)} %get-tuple-element.13.kv_ref.refs_2_), custom_call_target="tpu_custom_call" | custom-call | tf_op jit(solution)/shard_map/pallas_call | solution.py:483
  10.5 3.9 %collective-permute-start.2 = (f32[112,128]{1,0:T(8,128)S(1)}, f32[112,128]{1,0:T(8,128)S(1)}, u32[]{:S(2)}, u32[]{:S(2)}) collective-permute-start(f32[112,128]{1,0:T(8,128)S(1)} %get-tuple-element.21.refs_0_), channel_id=1, source_target_pairs={{0,1},{1,0},{2,3},{3,2},{4,5},{5,4},{6,7},{7,6},{8,9},{9,8},{10,11... | collective-permute-start | bytes 172040 | tf_op jit(solution)/shard_map/ppermute | solution.py:494
  14.4 0.9 %collective-permute-done.2.refs_1_ = f32[112,128]{1,0:T(8,128)S(1)} collective-permute-done((f32[112,128]{1,0:T(8,128)S(1)}, f32[112,128]{1,0:T(8,128)S(1)}, u32[]{:S(2)}, u32[]{:S(2)}) %collective-permute-start.2) | collective-permute-done | bytes 57376 | tf_op jit(solution)/shard_map/ppermute | solution.py:494
  15.3 0.2 shard_map.100.refs_0_
  15.5 1.6 %collective-permute-start.3 = (f32[112,128]{1,0:T(8,128)S(1)}, f32[112,128]{1,0:T(8,128)S(1)}, u32[]{:S(2)}, u32[]{:S(2)}) collective-permute-start(f32[112,128]{1,0:T(8,128)S(1)} %shard_map.100.refs_0_), channel_id=1, source_target_pairs={{0,2},{1,3},{2,0},{3,1},{4,6},{5,7},{6,4},{7,5},{8,10},{9,11},{10,... | collective-permute-start | bytes 172040 | tf_op jit(solution)/shard_map/ppermute | solution.py:494
  17.0 4.9 %collective-permute-done.3.refs_1_ = f32[112,128]{1,0:T(8,128)S(1)} collective-permute-done((f32[112,128]{1,0:T(8,128)S(1)}, f32[112,128]{1,0:T(8,128)S(1)}, u32[]{:S(2)}, u32[]{:S(2)}) %collective-permute-start.3) | collective-permute-done | bytes 57376 | tf_op jit(solution)/shard_map/ppermute | solution.py:494
  22.0 0.2 shard_map.101.refs_0_
  22.1 10.0 %collective-permute-start.4 = (f32[112,128]{1,0:T(8,128)S(1)}, f32[112,128]{1,0:T(8,128)S(1)}, u32[]{:S(2)}, u32[]{:S(2)}) collective-permute-start(f32[112,128]{1,0:T(8,128)S(1)} %shard_map.101.refs_0_), channel_id=1, source_target_pairs={{0,4},{1,5},{2,6},{3,7},{4,0},{5,1},{6,2},{7,3},{8,12},{9,13},{10,... | collective-permute-start | bytes 172040 | tf_op jit(solution)/shard_map/ppermute | solution.py:494
  32.1 2.2 %collective-permute-done.4.refs_1_ = f32[112,128]{1,0:T(8,128)S(1)} collective-permute-done((f32[112,128]{1,0:T(8,128)S(1)}, f32[112,128]{1,0:T(8,128)S(1)}, u32[]{:S(2)}, u32[]{:S(2)}) %collective-permute-start.4) | collective-permute-done | bytes 57376 | tf_op jit(solution)/shard_map/ppermute | solution.py:494
  34.3 0.2 shard_map.102.refs_0_
  34.5 3.1 %collective-permute-start.5 = (f32[112,128]{1,0:T(8,128)S(1)}, f32[112,128]{1,0:T(8,128)S(1)}, u32[]{:S(2)}, u32[]{:S(2)}) collective-permute-start(f32[112,128]{1,0:T(8,128)S(1)} %shard_map.102.refs_0_), channel_id=1, source_target_pairs={{0,8},{1,9},{2,10},{3,11},{4,12},{5,13},{6,14},{7,15},{8,0},{9,1},... | collective-permute-start | bytes 172040 | tf_op jit(solution)/shard_map/ppermute | solution.py:494
  37.6 2.2 %collective-permute-done.5.refs_1_ = f32[112,128]{1,0:T(8,128)S(1)} collective-permute-done((f32[112,128]{1,0:T(8,128)S(1)}, f32[112,128]{1,0:T(8,128)S(1)}, u32[]{:S(2)}, u32[]{:S(2)}) %collective-permute-start.5) | collective-permute-done | bytes 57376 | tf_op jit(solution)/shard_map/ppermute | solution.py:494
  39.7 1.2 %shard_map.103 = f32[16,768]{1,0:T(8,128)} custom-call(f32[112,128]{1,0:T(8,128)S(1)} %shard_map.102.refs_0_, f32[112,128]{1,0:T(8,128)S(1)} %collective-permute-done.5.refs_1_), custom_call_target="tpu_custom_call" | custom-call | tf_op jit(solution)/shard_map/pallas_call | solution.py:483
  40.9 0.0 collective-permute-done.1.refs_3_
  40.9 2.3 %shard_map.98 = (f32[256,768]{1,0:T(8,128)S(1)}, f32[256,768]{1,0:T(8,128)S(1)}, f32[256,128]{1,0:T(8,128)S(1)}) custom-call(f32[12]{0:T(128)S(1)} %copy-done.6, bf16[512,896]{1,0:T(8,128)(2,1)S(1)} %get-tuple-element.14.refs_1_.q_ref, bf16[576,1792]{1,0:T(8,128)(2,1)S(1)} %get-tuple-element.13.kv_ref.refs_2_, ...), custom_call_target="tpu_custom_call" | custom-call | tf_op jit(solution)/shard_map/pallas_call | solution.py:483
  43.3 0.0 copy-start
  43.3 0.0 copy-start.1
  43.3 0.0 copy-start.3
  43.3 0.0 copy-start.5
  43.3 2.4 %shard_map.97 = (f32[256,768]{1,0:T(8,128)S(1)}, f32[256,768]{1,0:T(8,128)S(1)}, f32[256,128]{1,0:T(8,128)S(1)}) custom-call(f32[12]{0:T(128)S(1)} %copy-done.6, bf16[512,896]{1,0:T(8,128)(2,1)S(1)} %get-tuple-element.14.refs_1_.q_ref, bf16[576,1792]{1,0:T(8,128)(2,1)S(1)} %get-tuple-element.13.kv_ref.refs_2_, ...), custom_call_target="tpu_custom_call" | custom-call | tf_op jit(solution)/shard_map/pallas_call | solution.py:483
  45.7 0.0 collective-permute-done.far_ref
  45.7 0.0 copy-done
  45.7 0.0 copy-done.1
  45.7 0.0 copy-done.3
  45.7 0.0 copy-done.5
  45.7 7.5 %shard_map.99 = bf16[512,768]{1,0:T(8,128)(2,1)} custom-call(f32[12]{0:T(128)S(1)} %copy-done.6, f32[768]{0:T(1024)S(1)} %copy-done.5, bf16[512,768]{1,0:T(8,128)(2,1)S(1)} %collective-permute-done.far_ref, bf16[768,768]{1,0:T(8,128)(2,1)S(1)} %copy-done, bf16[768,768]{1,0:T(8,128)(2,1)S(1)} %copy-done.1, bf16[768,768]{1,0:T(8,128)(2,1)S(1)} %copy-done.3, ...), custom_call_target="tpu_custom_call" | custom-call | tf_op jit(solution)/shard_map/pallas_call | solution.py:483
Async XLA Ops:
  0.6 5.1 %copy-start.2 = (bf16[4,128,768]{2,1,0:T(8,128)(2,1)S(1)}, bf16[4,128,768]{2,1,0:T(8,128)(2,1)}, u32[]{:S(2)}) copy-start(bf16[4,128,768]{2,1,0:T(8,128)(2,1)} %param.8) | copy-start | bytes 2359300
  0.6 6.0 %copy-start.4 = (bf16[16,768]{1,0:T(8,128)(2,1)S(1)}, bf16[16,768]{1,0:T(8,128)(2,1)}, u32[]{:S(2)}) copy-start(bf16[16,768]{1,0:T(8,128)(2,1)} %pool_ref.1) | copy-start | bytes 73732
  0.6 6.0 %copy-start.6 = (f32[12]{0:T(128)S(1)}, f32[12]{0:T(128)}, u32[]{:S(2)}) copy-start(f32[12]{0:T(128)} %scale_ref.3) | copy-start | bytes 148
  5.2 35.7 %collective-permute-start.1 = (bf16[576,1792]{1,0:T(8,128)(2,1)S(1)}, bf16[576,1792]{1,0:T(8,128)(2,1)S(1)}, u32[]{:S(2)}, u32[]{:S(2)}) collective-permute-start(bf16[576,1792]{1,0:T(8,128)(2,1)S(1)} %get-tuple-element.13.kv_ref.refs_2_), channel_id=1, source_target_pairs={{0,1},{1,0},{2,3},{3,2},{4,5},{5,4},{6,7},{7,6},{8,9},{9,8},{10,11... | collective-permute-start | bytes 6193160 | tf_op jit(solution)/shard_map/ppermute | solution.py:494
  5.7 39.9 %collective-permute-start = (bf16[512,768]{1,0:T(8,128)(2,1)S(1)}, bf16[512,768]{1,0:T(8,128)(2,1)S(1)}, u32[]{:S(2)}, u32[]{:S(2)}) collective-permute-start(bf16[512,768]{1,0:T(8,128)(2,1)S(1)} %bitcast.3), channel_id=1, source_target_pairs={{1,2},{3,4},{5,6},{7,8},{9,10},{11,12},{13,14},{2,1},{4,3},{6,5},{... | collective-permute-start | bytes 2359304 | tf_op jit(solution)/shard_map/ppermute | solution.py:494
  10.5 4.8 %collective-permute-start.2 = (f32[112,128]{1,0:T(8,128)S(1)}, f32[112,128]{1,0:T(8,128)S(1)}, u32[]{:S(2)}, u32[]{:S(2)}) collective-permute-start(f32[112,128]{1,0:T(8,128)S(1)} %get-tuple-element.21.refs_0_), channel_id=1, source_target_pairs={{0,1},{1,0},{2,3},{3,2},{4,5},{5,4},{6,7},{7,6},{8,9},{9,8},{10,11... | collective-permute-start | bytes 172040 | tf_op jit(solution)/shard_map/ppermute | solution.py:494
  15.5 6.5 %collective-permute-start.3 = (f32[112,128]{1,0:T(8,128)S(1)}, f32[112,128]{1,0:T(8,128)S(1)}, u32[]{:S(2)}, u32[]{:S(2)}) collective-permute-start(f32[112,128]{1,0:T(8,128)S(1)} %shard_map.100.refs_0_), channel_id=1, source_target_pairs={{0,2},{1,3},{2,0},{3,1},{4,6},{5,7},{6,4},{7,5},{8,10},{9,11},{10,... | collective-permute-start | bytes 172040 | tf_op jit(solution)/shard_map/ppermute | solution.py:494
  22.1 12.2 %collective-permute-start.4 = (f32[112,128]{1,0:T(8,128)S(1)}, f32[112,128]{1,0:T(8,128)S(1)}, u32[]{:S(2)}, u32[]{:S(2)}) collective-permute-start(f32[112,128]{1,0:T(8,128)S(1)} %shard_map.101.refs_0_), channel_id=1, source_target_pairs={{0,4},{1,5},{2,6},{3,7},{4,0},{5,1},{6,2},{7,3},{8,12},{9,13},{10,... | collective-permute-start | bytes 172040 | tf_op jit(solution)/shard_map/ppermute | solution.py:494
  34.5 5.3 %collective-permute-start.5 = (f32[112,128]{1,0:T(8,128)S(1)}, f32[112,128]{1,0:T(8,128)S(1)}, u32[]{:S(2)}, u32[]{:S(2)}) collective-permute-start(f32[112,128]{1,0:T(8,128)S(1)} %shard_map.102.refs_0_), channel_id=1, source_target_pairs={{0,8},{1,9},{2,10},{3,11},{4,12},{5,13},{6,14},{7,15},{8,0},{9,1},... | collective-permute-start | bytes 172040 | tf_op jit(solution)/shard_map/ppermute | solution.py:494
  43.3 2.4 %copy-start = (bf16[768,768]{1,0:T(8,128)(2,1)S(1)}, bf16[768,768]{1,0:T(8,128)(2,1)}, u32[]{:S(2)}) copy-start(bf16[768,768]{1,0:T(8,128)(2,1)} %k_w.1) | copy-start | bytes 3538948
  43.3 2.4 %copy-start.1 = (bf16[768,768]{1,0:T(8,128)(2,1)S(1)}, bf16[768,768]{1,0:T(8,128)(2,1)}, u32[]{:S(2)}) copy-start(bf16[768,768]{1,0:T(8,128)(2,1)} %v_w.1) | copy-start | bytes 3538948
  43.3 2.4 %copy-start.3 = (bf16[768,768]{1,0:T(8,128)(2,1)S(1)}, bf16[768,768]{1,0:T(8,128)(2,1)}, u32[]{:S(2)}) copy-start(bf16[768,768]{1,0:T(8,128)(2,1)} %o_w.1) | copy-start | bytes 3538948
  43.3 2.4 %copy-start.5 = (f32[768]{0:T(1024)S(1)}, f32[768]{0:T(1024)}, u32[]{:S(2)}) copy-start(f32[768]{0:T(1024)} %gain_ref.1) | copy-start | bytes 9220

commit v4 on v3

--- a/solution.py
+++ b/solution.py
@@ -95,7 +95,8 @@
         f = points[:, j * LANES : (j + 1) * LANES].astype(F32)
         first, second = half_sums(f * f)
         total = jnp.where(head == 2 * j, first, jnp.where(head == 2 * j + 1, second, total))
-    t = jnp.sqrt(1.0 + total)
+    total = 1.0 + total
+    t = total * lax.rsqrt(total)
     first = t.astype(BF16).astype(F32)
     rest = t - first
     second = rest.astype(BF16).astype(F32)
@@ -309,9 +310,7 @@
     store_values(values, heads, cols, pitch, kv_ref)
 
 
-def query_body(scale_ref, pool_ref, normed_ref, q_hbm, kv_ref, q_ref, out_ref, q_w, sem):
-    copy = pltpu.make_async_copy(q_hbm, q_w, sem)
-    copy.start()
+def query_body(scale_ref, pool_ref, normed_ref, q_w, kv_ref, q_ref, out_ref):
     pq = pool_ref[...]
     count, width = pq.shape
     heads = width // HEAD
@@ -333,7 +332,6 @@
     keys = jnp.concatenate(
         [kv_ref[r * pitch : r * pitch + cols, :extra] for r in range(rows)], axis=0
     )
-    copy.wait()
     queries = jnp.dot(normed_ref[...], q_w[...], preferred_element_type=F32).astype(BF16)
     q_ref[:, :width] = queries
     scores = lax.dot_general(q_all, keys, NT, preferred_element_type=F32)
@@ -490,6 +488,10 @@
     )(*args)
 
 
+def hop_steps(ring):
+    return [1] + [1 << bit for bit in range(2, ring.bit_length() - 1)] + [2]
+
+
 def exchange(value, pairs):
     return lax.ppermute(value, AXIS, pairs)
 
@@ -514,12 +516,12 @@
     pitch = cols + WIDE - BLOCK
     in_hbm = [
         pltpu.with_memory_space_constraint(a, pltpu.HBM)
-        for a in (norm_gain, own, key_weight, value_weight, query_weight)
+        for a in (norm_gain, own, key_weight, value_weight)
     ]
     keys_values, normed = local_call(
         project_body,
         (HBM,) * 4,
-        in_hbm[:4],
+        in_hbm,
         (struct((rows * pitch, 2 * extra), BF16), struct((cells, width), BF16)),
         [pltpu.VMEM((width,), F32), pltpu.VMEM((cells, width), BF16)]
         + [pltpu.VMEM((width, width), BF16)] * 2
@@ -528,13 +530,12 @@
     mate = exchange(keys_values, swap)
     queries, part = local_call(
         query_body,
-        (SMEM, VMEM, VMEM, HBM, VMEM),
-        (head_scale, pool_queries, normed, in_hbm[4], keys_values),
+        (SMEM,) + (VMEM,) * 4,
+        (head_scale, pool_queries, normed, query_weight, keys_values),
         (
             struct((cells, extra), BF16),
             struct(((width // LANES + 1) * count, LANES), F32),
         ),
-        [pltpu.VMEM((width, width), BF16), pltpu.SemaphoreType.DMA(())],
     )
     near = []
     split = cols // BLOCK // 2
@@ -551,10 +552,10 @@
             ),
             [pltpu.VMEM((2 * rows * WIDE, LANES), BF16)],
         )
-    for hop in range(ring.bit_length() - 1):
-        step = 1 << hop
+    steps = hop_steps(ring)
+    for hop, step in enumerate(steps):
         other = exchange(part, [(i, i ^ step) for i in range(ring)])
-        last = 2 * step >= ring
+        last = hop == len(steps) - 1
         part = local_call(
             lambda *refs, step=step, last=last: merge_body(
                 *refs, count=count, step=step, last=last

time: 53.4 us -> 46.5 us (0.87)
  starting transfers between devices: 20.1 us -> 10.1 us
  waiting for transfers between devices: 10.1 us -> 14.7 us
  Pallas kernels: 22.2 us -> 20.7 us
    ppermute x6, starting transfers between devices: 20.1 us -> 10.1 us  [exchange(): return lax.ppermute(value, AXIS, pairs)]
    ppermute x6, waiting for transfers between devices: 10.1 us -> 14.7 us  [exchange(): return lax.ppermute(value, AXIS, pairs)]
    pallas_call x9, Pallas kernels: 22.2 us -> 20.7 us  [local_call(): pl.pallas_call(body, out_shape=outs, in_specs=list(specs), out_specs=jax....]
where the time goes in v4:
time: 46.5 us; the launch traced here: 46.4 us
  Pallas kernels  20.7 us (45%)
  waiting for transfers between devices  14.7 us (32%)
  starting transfers between devices  10.1 us (22%)
  between operations  0.82 us (2%)
    pallas_call x9, Pallas kernels, local_call(): pl.pallas_call(body, out_shape=outs, in_specs=list(specs), out_specs=jax....  20.7 us
    ppermute x6, waiting for transfers between devices, exchange(): return lax.ppermute(value, AXIS, pairs)  14.7 us
    ppermute x6, starting transfers between devices, exchange(): return lax.ppermute(value, AXIS, pairs)  10.1 us
  transfers between devices with their start and end apart: 6, of which 4 were waited for; matrix products, arithmetic and copies ran while one was open for 0% of the time, Pallas kernels for 19%

profile of v4, /device:TPU:0, one launch (start us, length us, event | category | flops | bytes accessed | tf_op | source)
XLA Modules:
  0.0 46.4 jit_solution(1192490344383636951)
XLA Ops:
  0.6 0.0 copy-start.2
  0.6 0.0 copy-start.4
  0.7 0.0 copy-start.5
  0.7 0.0 copy-start.7
  0.7 4.4 %shard_map.95 = (bf16[576,1792]{1,0:T(8,128)(2,1)S(1)}, bf16[512,768]{1,0:T(8,128)(2,1)S(1)}) custom-call(f32[768]{0:T(1024)} %gain_ref.1, bf16[512,768]{1,0:T(8,128)(2,1)} %bitcast.2, bf16[768,768]{1,0:T(8,128)(2,1)} %k_w.1, bf16[768,768]{1,0:T(8,128)(2,1)} %v_w.1), custom_call_target="tpu_custom_call" | custom-call | tf_op jit(solution)/shard_map/pallas_call | solution.py:481
  5.1 0.6 %collective-permute-start.1 = (bf16[576,1792]{1,0:T(8,128)(2,1)S(1)}, bf16[576,1792]{1,0:T(8,128)(2,1)S(1)}, u32[]{:S(2)}, u32[]{:S(2)}) collective-permute-start(bf16[576,1792]{1,0:T(8,128)(2,1)S(1)} %get-tuple-element.13.kv_ref.refs_2_), channel_id=1, source_target_pairs={{0,1},{1,0},{2,3},{3,2},{4,5},{5,4},{6,7},{7,6},{8,9},{9,8},{10,11... | collective-permute-start | bytes 6193160 | tf_op jit(solution)/shard_map/ppermute | solution.py:496
  5.7 0.0 copy-done.2
  5.7 0.9 %collective-permute-start = (bf16[512,768]{1,0:T(8,128)(2,1)S(1)}, bf16[512,768]{1,0:T(8,128)(2,1)S(1)}, u32[]{:S(2)}, u32[]{:S(2)}) collective-permute-start(bf16[512,768]{1,0:T(8,128)(2,1)S(1)} %bitcast.3), channel_id=1, source_target_pairs={{1,2},{3,4},{5,6},{7,8},{9,10},{11,12},{13,14},{2,1},{4,3},{6,5},{... | collective-permute-start | bytes 2359304 | tf_op jit(solution)/shard_map/ppermute | solution.py:496
  6.6 0.0 copy-done.4
  6.6 0.0 copy-done.5
  6.6 0.0 copy-done.7
  6.6 2.5 %shard_map.96 = (bf16[512,896]{1,0:T(8,128)(2,1)S(1)}, f32[112,128]{1,0:T(8,128)S(1)}) custom-call(f32[12]{0:T(128)S(1)} %copy-done.7, bf16[16,768]{1,0:T(8,128)(2,1)S(1)} %copy-done.5, bf16[512,768]{1,0:T(8,128)(2,1)S(1)} %get-tuple-element.12.normed_ref, bf16[768,768]{1,0:T(8,128)(2,1)S(1)} %copy-done.4, bf16[576,1792]{1,0:T(8,128)(2,1)S(1)} %get-tuple-element.13.kv_ref.refs_2_), custom_call_target="tpu_custom_call" | custom-call | tf_op jit(solution)/shard_map/pallas_call | solution.py:481
  9.1 3.9 %collective-permute-start.2 = (f32[112,128]{1,0:T(8,128)S(1)}, f32[112,128]{1,0:T(8,128)S(1)}, u32[]{:S(2)}, u32[]{:S(2)}) collective-permute-start(f32[112,128]{1,0:T(8,128)S(1)} %get-tuple-element.21.refs_0_), channel_id=1, source_target_pairs={{0,1},{1,0},{2,3},{3,2},{4,5},{5,4},{6,7},{7,6},{8,9},{9,8},{10,11... | collective-permute-start | bytes 172040 | tf_op jit(solution)/shard_map/ppermute | solution.py:496
  13.0 0.9 %collective-permute-done.2.refs_1_ = f32[112,128]{1,0:T(8,128)S(1)} collective-permute-done((f32[112,128]{1,0:T(8,128)S(1)}, f32[112,128]{1,0:T(8,128)S(1)}, u32[]{:S(2)}, u32[]{:S(2)}) %collective-permute-start.2) | collective-permute-done | bytes 57376 | tf_op jit(solution)/shard_map/ppermute | solution.py:496
  13.9 0.2 shard_map.100.refs_0_
  14.0 1.8 %collective-permute-start.3 = (f32[112,128]{1,0:T(8,128)S(1)}, f32[112,128]{1,0:T(8,128)S(1)}, u32[]{:S(2)}, u32[]{:S(2)}) collective-permute-start(f32[112,128]{1,0:T(8,128)S(1)} %shard_map.100.refs_0_), channel_id=1, source_target_pairs={{0,4},{1,5},{2,6},{3,7},{4,0},{5,1},{6,2},{7,3},{8,12},{9,13},{10,... | collective-permute-start | bytes 172040 | tf_op jit(solution)/shard_map/ppermute | solution.py:496
  15.9 7.4 %collective-permute-done.3.refs_1_ = f32[112,128]{1,0:T(8,128)S(1)} collective-permute-done((f32[112,128]{1,0:T(8,128)S(1)}, f32[112,128]{1,0:T(8,128)S(1)}, u32[]{:S(2)}, u32[]{:S(2)}) %collective-permute-start.3) | collective-permute-done | bytes 57376 | tf_op jit(solution)/shard_map/ppermute | solution.py:496
  23.3 0.2 shard_map.101.refs_0_
  23.4 2.9 %collective-permute-start.4 = (f32[112,128]{1,0:T(8,128)S(1)}, f32[112,128]{1,0:T(8,128)S(1)}, u32[]{:S(2)}, u32[]{:S(2)}) collective-permute-start(f32[112,128]{1,0:T(8,128)S(1)} %shard_map.101.refs_0_), channel_id=1, source_target_pairs={{0,8},{1,9},{2,10},{3,11},{4,12},{5,13},{6,14},{7,15},{8,0},{9,1},... | collective-permute-start | bytes 172040 | tf_op jit(solution)/shard_map/ppermute | solution.py:496
  26.3 2.3 %collective-permute-done.4.refs_1_ = f32[112,128]{1,0:T(8,128)S(1)} collective-permute-done((f32[112,128]{1,0:T(8,128)S(1)}, f32[112,128]{1,0:T(8,128)S(1)}, u32[]{:S(2)}, u32[]{:S(2)}) %collective-permute-start.4) | collective-permute-done | bytes 57376 | tf_op jit(solution)/shard_map/ppermute | solution.py:496
  28.6 0.2 shard_map.102.refs_0_
  28.7 0.1 collective-permute-start.5
  28.8 4.2 %collective-permute-done.5.refs_1_ = f32[112,128]{1,0:T(8,128)S(1)} collective-permute-done((f32[112,128]{1,0:T(8,128)S(1)}, f32[112,128]{1,0:T(8,128)S(1)}, u32[]{:S(2)}, u32[]{:S(2)}) %collective-permute-start.5) | collective-permute-done | bytes 57376 | tf_op jit(solution)/shard_map/ppermute | solution.py:496
  33.0 1.2 %shard_map.103 = f32[16,768]{1,0:T(8,128)} custom-call(f32[112,128]{1,0:T(8,128)S(1)} %shard_map.102.refs_0_, f32[112,128]{1,0:T(8,128)S(1)} %collective-permute-done.5.refs_1_), custom_call_target="tpu_custom_call" | custom-call | tf_op jit(solution)/shard_map/pallas_call | solution.py:481
  34.2 0.0 collective-permute-done.1.refs_3_
  34.2 2.3 %shard_map.98 = (f32[256,768]{1,0:T(8,128)S(1)}, f32[256,768]{1,0:T(8,128)S(1)}, f32[256,128]{1,0:T(8,128)S(1)}) custom-call(f32[12]{0:T(128)S(1)} %copy-done.7, bf16[512,896]{1,0:T(8,128)(2,1)S(1)} %get-tuple-element.14.refs_1_.q_ref, bf16[576,1792]{1,0:T(8,128)(2,1)S(1)} %get-tuple-element.13.kv_ref.refs_2_, ...), custom_call_target="tpu_custom_call" | custom-call | tf_op jit(solution)/shard_map/pallas_call | solution.py:481
  36.5 0.0 copy-start
  36.5 0.0 copy-start.1
  36.5 0.0 copy-start.3
  36.6 0.0 copy-start.6
  36.6 2.4 %shard_map.97 = (f32[256,768]{1,0:T(8,128)S(1)}, f32[256,768]{1,0:T(8,128)S(1)}, f32[256,128]{1,0:T(8,128)S(1)}) custom-call(f32[12]{0:T(128)S(1)} %copy-done.7, bf16[512,896]{1,0:T(8,128)(2,1)S(1)} %get-tuple-element.14.refs_1_.q_ref, bf16[576,1792]{1,0:T(8,128)(2,1)S(1)} %get-tuple-element.13.kv_ref.refs_2_, ...), custom_call_target="tpu_custom_call" | custom-call | tf_op jit(solution)/shard_map/pallas_call | solution.py:481
  38.9 0.0 collective-permute-done.far_ref
  38.9 0.0 copy-done
  38.9 0.0 copy-done.1
  39.0 0.0 copy-done.3
  39.0 0.0 copy-done.6
  39.0 7.4 %shard_map.99 = bf16[512,768]{1,0:T(8,128)(2,1)} custom-call(f32[12]{0:T(128)S(1)} %copy-done.7, f32[768]{0:T(1024)S(1)} %copy-done.6, bf16[512,768]{1,0:T(8,128)(2,1)S(1)} %collective-permute-done.far_ref, bf16[768,768]{1,0:T(8,128)(2,1)S(1)} %copy-done, bf16[768,768]{1,0:T(8,128)(2,1)S(1)} %copy-done.1, bf16[768,768]{1,0:T(8,128)(2,1)S(1)} %copy-done.3, ...), custom_call_target="tpu_custom_call" | custom-call | tf_op jit(solution)/shard_map/pallas_call | solution.py:481
Async XLA Ops:
  0.6 5.0 %copy-start.2 = (bf16[4,128,768]{2,1,0:T(8,128)(2,1)S(1)}, bf16[4,128,768]{2,1,0:T(8,128)(2,1)}, u32[]{:S(2)}) copy-start(bf16[4,128,768]{2,1,0:T(8,128)(2,1)} %param.8) | copy-start | bytes 2359300
  0.6 5.9 %copy-start.4 = (bf16[768,768]{1,0:T(8,128)(2,1)S(1)}, bf16[768,768]{1,0:T(8,128)(2,1)}, u32[]{:S(2)}) copy-start(bf16[768,768]{1,0:T(8,128)(2,1)} %q_w.1) | copy-start | bytes 3538948
  0.7 5.9 %copy-start.5 = (bf16[16,768]{1,0:T(8,128)(2,1)S(1)}, bf16[16,768]{1,0:T(8,128)(2,1)}, u32[]{:S(2)}) copy-start(bf16[16,768]{1,0:T(8,128)(2,1)} %pool_ref.1) | copy-start | bytes 73732
  0.7 5.9 %copy-start.7 = (f32[12]{0:T(128)S(1)}, f32[12]{0:T(128)}, u32[]{:S(2)}) copy-start(f32[12]{0:T(128)} %scale_ref.3) | copy-start | bytes 148
  5.1 29.0 %collective-permute-start.1 = (bf16[576,1792]{1,0:T(8,128)(2,1)S(1)}, bf16[576,1792]{1,0:T(8,128)(2,1)S(1)}, u32[]{:S(2)}, u32[]{:S(2)}) collective-permute-start(bf16[576,1792]{1,0:T(8,128)(2,1)S(1)} %get-tuple-element.13.kv_ref.refs_2_), channel_id=1, source_target_pairs={{0,1},{1,0},{2,3},{3,2},{4,5},{5,4},{6,7},{7,6},{8,9},{9,8},{10,11... | collective-permute-start | bytes 6193160 | tf_op jit(solution)/shard_map/ppermute | solution.py:496
  5.7 33.3 %collective-permute-start = (bf16[512,768]{1,0:T(8,128)(2,1)S(1)}, bf16[512,768]{1,0:T(8,128)(2,1)S(1)}, u32[]{:S(2)}, u32[]{:S(2)}) collective-permute-start(bf16[512,768]{1,0:T(8,128)(2,1)S(1)} %bitcast.3), channel_id=1, source_target_pairs={{1,2},{3,4},{5,6},{7,8},{9,10},{11,12},{13,14},{2,1},{4,3},{6,5},{... | collective-permute-start | bytes 2359304 | tf_op jit(solution)/shard_map/ppermute | solution.py:496
  9.1 4.8 %collective-permute-start.2 = (f32[112,128]{1,0:T(8,128)S(1)}, f32[112,128]{1,0:T(8,128)S(1)}, u32[]{:S(2)}, u32[]{:S(2)}) collective-permute-start(f32[112,128]{1,0:T(8,128)S(1)} %get-tuple-element.21.refs_0_), channel_id=1, source_target_pairs={{0,1},{1,0},{2,3},{3,2},{4,5},{5,4},{6,7},{7,6},{8,9},{9,8},{10,11... | collective-permute-start | bytes 172040 | tf_op jit(solution)/shard_map/ppermute | solution.py:496
  14.0 9.2 %collective-permute-start.3 = (f32[112,128]{1,0:T(8,128)S(1)}, f32[112,128]{1,0:T(8,128)S(1)}, u32[]{:S(2)}, u32[]{:S(2)}) collective-permute-start(f32[112,128]{1,0:T(8,128)S(1)} %shard_map.100.refs_0_), channel_id=1, source_target_pairs={{0,4},{1,5},{2,6},{3,7},{4,0},{5,1},{6,2},{7,3},{8,12},{9,13},{10,... | collective-permute-start | bytes 172040 | tf_op jit(solution)/shard_map/ppermute | solution.py:496
  23.4 5.1 %collective-permute-start.4 = (f32[112,128]{1,0:T(8,128)S(1)}, f32[112,128]{1,0:T(8,128)S(1)}, u32[]{:S(2)}, u32[]{:S(2)}) collective-permute-start(f32[112,128]{1,0:T(8,128)S(1)} %shard_map.101.refs_0_), channel_id=1, source_target_pairs={{0,8},{1,9},{2,10},{3,11},{4,12},{5,13},{6,14},{7,15},{8,0},{9,1},... | collective-permute-start | bytes 172040 | tf_op jit(solution)/shard_map/ppermute | solution.py:496
  28.7 4.2 %collective-permute-start.5 = (f32[112,128]{1,0:T(8,128)S(1)}, f32[112,128]{1,0:T(8,128)S(1)}, u32[]{:S(2)}, u32[]{:S(2)}) collective-permute-start(f32[112,128]{1,0:T(8,128)S(1)} %shard_map.102.refs_0_), channel_id=1, source_target_pairs={{0,2},{1,3},{2,0},{3,1},{4,6},{5,7},{6,4},{7,5},{8,10},{9,11},{10,... | collective-permute-start | bytes 172040 | tf_op jit(solution)/shard_map/ppermute | solution.py:496
  36.5 2.4 %copy-start = (bf16[768,768]{1,0:T(8,128)(2,1)S(1)}, bf16[768,768]{1,0:T(8,128)(2,1)}, u32[]{:S(2)}) copy-start(bf16[768,768]{1,0:T(8,128)(2,1)} %k_w.1) | copy-start | bytes 3538948
  36.5 2.4 %copy-start.1 = (bf16[768,768]{1,0:T(8,128)(2,1)S(1)}, bf16[768,768]{1,0:T(8,128)(2,1)}, u32[]{:S(2)}) copy-start(bf16[768,768]{1,0:T(8,128)(2,1)} %v_w.1) | copy-start | bytes 3538948
  36.5 2.4 %copy-start.3 = (bf16[768,768]{1,0:T(8,128)(2,1)S(1)}, bf16[768,768]{1,0:T(8,128)(2,1)}, u32[]{:S(2)}) copy-start(bf16[768,768]{1,0:T(8,128)(2,1)} %o_w.1) | copy-start | bytes 3538948
  36.6 2.4 %copy-start.6 = (f32[768]{0:T(1024)S(1)}, f32[768]{0:T(1024)}, u32[]{:S(2)}) copy-start(f32[768]{0:T(1024)} %gain_ref.1) | copy-start | bytes 9220

commit v5 on v4

--- a/solution.py
+++ b/solution.py
@@ -1,3 +1,4 @@
+import functools
 import math
 
 import jax
@@ -35,13 +36,6 @@
     feats = tokens.astype(F32)
     mean_sq = jnp.mean(feats * feats, axis=-1, keepdims=True)
     return feats * lax.rsqrt(mean_sq + EPS) * gain
-
-
-def shift_columns(normed, cols):
-    rows = normed.shape[0] // cols
-    return jnp.concatenate(
-        [pltpu.roll(normed[r * cols : (r + 1) * cols], RAD, 0) for r in range(rows)], axis=0
-    )
 
 
 def lane_heads(heads):
@@ -129,17 +123,17 @@
     return jnp.where(place < 3 * pairs, mixed, 0.0)
 
 
-def store_rows(ref, pitch, cols, value, lane):
+def store_rows(ref, pitch, cols, first, value, lane):
     for r in range(value.shape[0] // cols):
         row = value[r * cols : (r + 1) * cols]
         lanes = slice(lane, lane + value.shape[1])
-        ref[r * pitch : r * pitch + cols, lanes] = row
-        ref[r * pitch + cols : (r + 1) * pitch, lanes] = row[: pitch - cols]
-
-
-def store_keys(keys, heads, cols, pitch, ref, invalid):
+        base = (first + r) * pitch
+        ref[base : base + cols, lanes] = row
+        ref[base + cols : base + pitch, lanes] = row[: pitch - cols]
+
+
+def store_key_times(keys, heads, cols, pitch, first, ref, invalid):
     width = heads * HEAD
-    store_rows(ref, pitch, cols, keys, 0)
     times = key_times(time_pieces(keys, heads, lane_heads(heads)), heads)
     place = row_iota((pitch, LANES))
     outside = (place < RAD) | (place >= cols + RAD)
@@ -150,15 +144,38 @@
     for r in range(keys.shape[0] // cols):
         row = times[r * cols : (r + 1) * cols]
         row = jnp.concatenate([row, row[: pitch - cols]], axis=0)
-        ref[r * pitch : (r + 1) * pitch, width : width + LANES] = (row + bias).astype(BF16)
-
-
-def store_values(values, heads, cols, pitch, ref):
+        base = (first + r) * pitch
+        ref[base : base + pitch, width : width + LANES] = (row + bias).astype(BF16)
+
+
+def store_value_times(values, heads, cols, pitch, first, ref):
     width = heads * HEAD
-    base = width + LANES
-    store_rows(ref, pitch, cols, values, base)
-    times = value_times(time_pieces(values, heads, value_lane_heads(heads), heads // 4), heads).astype(BF16)
-    store_rows(ref, pitch, cols, times, base + width)
+    pieces = time_pieces(values, heads, value_lane_heads(heads), heads // 4)
+    times = value_times(pieces, heads).astype(BF16)
+    store_rows(ref, pitch, cols, first, times, 2 * width + LANES)
+
+
+def project_strips(strips, k_w, v_w, heads, cols, pitch, ref, invalid):
+    width = heads * HEAD
+    behind = None
+    first = 0
+    for weight in (k_w, v_w):
+        for number, strip in enumerate(strips):
+            first = sum(s.shape[0] for s in strips[:number]) // cols
+            points = jnp.dot(strip, weight[...], preferred_element_type=F32).astype(BF16)
+            lane = 0 if weight is k_w else width + LANES
+            store_rows(ref, pitch, cols, first, points, lane)
+            if behind is not None:
+                behind()
+            if weight is k_w:
+                behind = functools.partial(
+                    store_key_times, points, heads, cols, pitch, first, ref, invalid
+                )
+            else:
+                behind = functools.partial(
+                    store_value_times, points, heads, cols, pitch, first, ref
+                )
+    behind()
 
 
 def window_bias(mask_ref, first, heads):
@@ -187,6 +204,11 @@
     for piece in range(1, pieces):
         hit = hit | (lane == piece * heads + head)
     return hit
+
+
+def head_scales(scale_ref, heads):
+    scale = scale_ref[...][None, :] * DOUBLE_LOG2E
+    return [scale[:, h : h + 1] for h in range(heads)]
 
 
 def as_factor(hit):
@@ -205,7 +227,7 @@
     keeps = [
         as_factor(head_mask(heads, h, lane, SPLIT) | (lane >= SPLIT * heads)) for h in range(heads)
     ]
-    scale = [scale_ref[h] * DOUBLE_LOG2E for h in range(heads)]
+    scale = head_scales(scale_ref, heads)
     half = rows * BLOCK
     parts = (slice(0, half), slice(half, 2 * half))
 
@@ -281,33 +303,30 @@
         finish(last, pair, *behind[pair])
 
 
-def project_body(gain_hbm, own_hbm, k_hbm, v_hbm, kv_ref, normed_ref, gain_ref, own_ref, k_w, v_w, sems):
+def setup_body(near_mask, far_mask, *, heads):
+    half = near_mask.shape[0] // 2
+    odd = lax.axis_index(AXIS) % 2
+    window_bias(near_mask.at[:half], RAD, heads)
+    window_bias(near_mask.at[half:], 2 * RAD * (1 - odd), heads)
+    window_bias(far_mask, 2 * RAD * odd, heads)
+
+
+def project_body(mask_ref, gain_ref, own_ref, k_w, v_w, kv_ref, normed_ref):
+    del mask_ref
     cells, width = own_ref.shape
     heads = width // HEAD
     cols = LANES
     rows = cells // cols
     pitch = kv_ref.shape[0] // rows
-    strips = [slice(r * cols, (r + 1) * cols) for r in range(rows)]
-    moves = [(gain_hbm, gain_ref)] + [(own_hbm.at[part], own_ref.at[part]) for part in strips]
-    moves += [(k_hbm, k_w), (v_hbm, v_w)]
-    copies = [pltpu.make_async_copy(src, dst, sems.at[i]) for i, (src, dst) in enumerate(moves)]
-    for copy in copies:
-        copy.start()
-    copies[0].wait()
     gain = gain_ref[...][None, :]
     shifted = []
-    for r, part in enumerate(strips):
-        copies[1 + r].wait()
+    for r in range(rows):
+        part = slice(r * cols, (r + 1) * cols)
         normed = normalize(own_ref[part], gain)
         normed_ref[part] = normed.astype(BF16)
         shifted.append(pltpu.roll(normed, RAD, 0).astype(BF16))
-    shifted = jnp.concatenate(shifted, axis=0)
-    copies[-2].wait()
-    keys = jnp.dot(shifted, k_w[...], preferred_element_type=F32).astype(BF16)
-    copies[-1].wait()
-    values = jnp.dot(shifted, v_w[...], preferred_element_type=F32).astype(BF16)
-    store_keys(keys, heads, cols, pitch, kv_ref, None)
-    store_values(values, heads, cols, pitch, kv_ref)
+    halves = [jnp.concatenate(shifted[i : i + 2], axis=0) for i in range(0, rows, 2)]
+    project_strips(halves, k_w, v_w, heads, cols, pitch, kv_ref, None)
 
 
 def query_body(scale_ref, pool_ref, normed_ref, q_w, kv_ref, q_ref, out_ref):
@@ -316,7 +335,7 @@
     heads = width // HEAD
     cols = LANES
     extra = width + LANES
-    rows = q_ref.shape[0] // cols
+    rows = normed_ref.shape[0] // cols
     pitch = kv_ref.shape[0] // rows
     lane = lane_iota((count, LANES))
     q_time = query_times(time_pieces(pq, heads, lane_heads(heads)), heads)
@@ -340,7 +359,7 @@
         part = slice(r * cols, (r + 1) * cols)
         q_ref[part, width:] = (times[part] + query_features(cols, heads, r)).astype(BF16)
     scale = jnp.concatenate(
-        [jnp.full((count, 1), scale_ref[h] * DOUBLE_LOG2E, F32) for h in range(heads)], axis=0
+        [jnp.broadcast_to(c, (count, 1)) for c in head_scales(scale_ref, heads)], axis=0
     )
     scores = scores * scale
     peak = jnp.max(scores, axis=-1, keepdims=True)
@@ -352,7 +371,7 @@
     )
     total = jnp.dot(jnp.concatenate([hi, lo], axis=0), values, preferred_element_type=F32)
     total = total[: heads * count] + total[heads * count :]
-    stats = zero
+    stats = jnp.zeros((count, LANES), F32)
     for h in range(heads):
         part = slice(h * count, (h + 1) * count)
         time = jnp.where(value_mask(heads, h), total[part, width:], 0.0)
@@ -366,14 +385,10 @@
     out_ref[width // LANES * count :, :] = stats
 
 
-def near_body(scale_ref, q_ref, own_ref, mate_ref, peak_ref, space_ref, time_ref, mask_ref, *, blocks):
+def near_body(scale_ref, q_ref, own_ref, mate_ref, mask_ref, peak_ref, space_ref, time_ref, *, blocks):
     width = q_ref.shape[1] - LANES
     heads = width // HEAD
     size = q_ref.shape[0] // LANES * BLOCK
-    half = mask_ref.shape[0] // 2
-    odd = lax.axis_index(AXIS) % 2
-    window_bias(mask_ref.at[:half], RAD, heads)
-    window_bias(mask_ref.at[half:], 2 * RAD * (1 - odd), heads)
     mine = [value_mask(heads, 2 * j) | value_mask(heads, 2 * j + 1) for j in range(heads // 2)]
     block_times = {}
 
@@ -392,35 +407,68 @@
     window_attention(q_ref, (own_ref, mate_ref), mask_ref, scale_ref, heads, blocks, finish)
 
 
-def far_body(
-    scale_ref, gain_ref, far_ref, k_w, v_w, o_w, own_ref, q_ref,
-    peak_a, space_a, time_a, peak_b, space_b, time_b, out_ref, kv_ref, mask_ref, mix_ref,
+def far_keys_body(gain_ref, far_ref, k_w, v_w, kv_ref):
+    cells, width = far_ref.shape
+    heads = width // HEAD
+    cols = LANES
+    rows = cells // cols
+    pitch = kv_ref.shape[0] // rows
+    index = lax.axis_index(AXIS)
+    invalid = (index == 0) | (index == lax.axis_size(AXIS) - 1)
+    gain = gain_ref[...][None, :]
+    shifted = []
+    for r in range(rows):
+        normed = normalize(far_ref[r * cols : (r + 1) * cols], gain)
+        shifted.append(pltpu.roll(normed, RAD, 0).astype(BF16))
+    halves = [jnp.concatenate(shifted[i : i + 2], axis=0) for i in range(0, rows, 2)]
+    project_strips(halves, k_w, v_w, heads, cols, pitch, kv_ref, invalid)
+
+
+def far_first_body(*refs, blocks):
+    *inputs, out_hbm, mix_ref, out_ref, sems = refs
+    far_blocks(*inputs, out_hbm, mix_ref, out_ref, sems, blocks)
+
+
+def far_last_body(so_far, part_ref, other_ref, *refs, blocks, count, step):
+    del so_far
+    *inputs, out_hbm, pooled_hbm, mix_ref, out_ref, sems, pooled_ref, pooled_sem = refs
+    merge_body(part_ref, other_ref, pooled_ref, count=count, step=step, last=True)
+    copy = pltpu.make_async_copy(pooled_ref, pooled_hbm, pooled_sem)
+    copy.start()
+    far_blocks(*inputs, out_hbm, mix_ref, out_ref, sems, blocks)
+    copy.wait()
+
+
+def far_blocks(
+    scale_ref, kv_ref, o_w, own_ref, q_ref, mask_ref, peak_ref, space_ref, time_ref,
+    out_hbm, mix_ref, out_ref, sems, blocks,
 ):
     width = own_ref.shape[1]
     heads = width // HEAD
     cols = LANES
     rows = own_ref.shape[0] // cols
     size = rows * BLOCK
-    pitch = kv_ref.shape[0] // rows
-    index = lax.axis_index(AXIS)
-    odd = index % 2
-    invalid = (index == 0) | (index == lax.axis_size(AXIS) - 1)
-    window_bias(mask_ref, 2 * RAD * odd, heads)
-    shifted = normalize(far_ref[...], gain_ref[...][None, :])
-    shifted = shift_columns(shifted, cols).astype(BF16)
-    keys = jnp.dot(shifted, k_w[...], preferred_element_type=F32).astype(BF16)
-    values = jnp.dot(shifted, v_w[...], preferred_element_type=F32).astype(BF16)
-    store_keys(keys, heads, cols, pitch, kv_ref, invalid)
-    store_values(values, heads, cols, pitch, kv_ref)
+    strip = 2 * BLOCK
+    chunk0 = blocks[0] // 2
     low = lane_iota((1, LANES)) < HEAD
     mine = [value_mask(heads, 2 * j) | value_mask(heads, 2 * j + 1) for j in range(heads // 2)]
 
+    def copy_out(chunk):
+        columns = slice(chunk * strip, (chunk + 1) * strip)
+        place = chunk - chunk0
+        return pltpu.make_async_copy(out_ref.at[place], out_hbm.at[:, columns], sems.at[place])
+
+    def mix_out(chunk):
+        projected = jnp.dot(mix_ref[chunk - chunk0], o_w[...], preferred_element_type=F32)
+        for r in range(rows):
+            start = r * cols + chunk * strip
+            tokens = own_ref[start : start + strip].astype(F32)
+            mixed = tokens + projected[r * strip : (r + 1) * strip]
+            out_ref[chunk - chunk0, r] = mixed.astype(BF16)
+        copy_out(chunk).start()
+
     def finish(block, pair, far_peak, far_space, far_times, scale):
-        second = block * size >= peak_a.shape[0]
-        peak_ref, space_ref, time_ref = (
-            (peak_b, space_b, time_b) if second else (peak_a, space_a, time_a)
-        )
-        place = block * size - (peak_a.shape[0] if second else 0)
+        place = (block - blocks[0]) * size
         part = slice(place, place + size)
         tile = slice(pair * LANES, (pair + 1) * LANES)
         near_peak = peak_ref[part, tile]
@@ -432,13 +480,16 @@
         time = jnp.where(low, *half_sums(times))
         spread = time * time - jnp.where(low, *half_sums(mean * mean))
         attended = (mean * lax.rsqrt(spread)).astype(BF16)
+        chunk, side = block // 2, block % 2
         for r in range(rows):
-            start = r * cols + block * BLOCK
-            mix_ref[start : start + BLOCK, tile] = attended[r * BLOCK : (r + 1) * BLOCK]
-
-    window_attention(q_ref, (kv_ref,), mask_ref, scale_ref, heads, range(cols // BLOCK), finish)
-    projected = jnp.dot(mix_ref[...], o_w[...], preferred_element_type=F32)
-    out_ref[...] = (own_ref[...].astype(F32) + projected).astype(BF16)
+            start = (2 * r + side) * BLOCK
+            mix_ref[chunk - chunk0, start : start + BLOCK, tile] = attended[r * BLOCK : (r + 1) * BLOCK]
+        if side and pair == heads // 2 - 1:
+            mix_out(chunk)
+
+    window_attention(q_ref, (kv_ref,), mask_ref, scale_ref, heads, blocks, finish)
+    for chunk in range(chunk0, chunk0 + len(blocks) // 2):
+        copy_out(chunk).wait()
 
 
 def merge_body(mine_ref, other_ref, out_ref, *, count, step, last):
@@ -472,18 +523,22 @@
         out_ref[tiles * count :, :] = stats
 
 
-SMEM = pl.BlockSpec(memory_space=pltpu.SMEM)
 VMEM = pl.BlockSpec(memory_space=pltpu.VMEM)
 HBM = pl.BlockSpec(memory_space=pltpu.HBM)
 
 
-def local_call(body, specs, args, outs, scratch=(), limit=24):
+def local_call(
+    body, specs, args, outs, scratch=(), limit=24, flops=None, out_specs=None, aliases=None
+):
     return pl.pallas_call(
         body,
         out_shape=outs,
         in_specs=list(specs),
-        out_specs=jax.tree.map(lambda _: VMEM, outs),
+        out_specs=out_specs or jax.tree.map(lambda _: VMEM, outs),
         scratch_shapes=list(scratch),
+        input_output_aliases=aliases or {},
+        cost_estimate=flops
+        and pl.CostEstimate(flops=flops, transcendentals=0, bytes_accessed=0),
         compiler_params=pltpu.CompilerParams(vmem_limit_bytes=limit << 20),
     )(*args)
 
@@ -514,23 +569,24 @@
     far = exchange(own, cross)
     extra = width + LANES
     pitch = cols + WIDE - BLOCK
-    in_hbm = [
-        pltpu.with_memory_space_constraint(a, pltpu.HBM)
-        for a in (norm_gain, own, key_weight, value_weight)
-    ]
+    near_mask, far_mask = local_call(
+        functools.partial(setup_body, heads=heads),
+        (),
+        (),
+        (struct((2 * rows * WIDE, LANES), BF16), struct((rows * WIDE, LANES), BF16)),
+        limit=8,
+        flops=1 << 32,
+    )
     keys_values, normed = local_call(
         project_body,
-        (HBM,) * 4,
-        in_hbm,
+        (VMEM,) * 5,
+        (near_mask, norm_gain, own, key_weight, value_weight),
         (struct((rows * pitch, 2 * extra), BF16), struct((cells, width), BF16)),
-        [pltpu.VMEM((width,), F32), pltpu.VMEM((cells, width), BF16)]
-        + [pltpu.VMEM((width, width), BF16)] * 2
-        + [pltpu.SemaphoreType.DMA((3 + rows,))],
     )
     mate = exchange(keys_values, swap)
     queries, part = local_call(
         query_body,
-        (SMEM,) + (VMEM,) * 4,
+        (VMEM,) * 5,
         (head_scale, pool_queries, normed, query_weight, keys_values),
         (
             struct((cells, extra), BF16),
@@ -541,42 +597,60 @@
     split = cols // BLOCK // 2
     for blocks in (range(split), range(split, 2 * split)):
         size = split * rows * BLOCK
-        near += local_call(
+        near.append(local_call(
             lambda *refs, blocks=blocks: near_body(*refs, blocks=blocks),
-            (SMEM, VMEM, VMEM, VMEM),
-            (head_scale, queries, keys_values, mate),
+            (VMEM,) * 5,
+            (head_scale, queries, keys_values, mate, near_mask),
             (
                 struct((size, width), F32),
                 struct((size, width), F32),
                 struct((size, LANES), F32),
             ),
-            [pltpu.VMEM((2 * rows * WIDE, LANES), BF16)],
-        )
+        ))
     steps = hop_steps(ring)
-    for hop, step in enumerate(steps):
+    for step in steps:
         other = exchange(part, [(i, i ^ step) for i in range(ring)])
-        last = hop == len(steps) - 1
+        if step == steps[-1]:
+            break
         part = local_call(
-            lambda *refs, step=step, last=last: merge_body(
-                *refs, count=count, step=step, last=last
-            ),
+            lambda *refs, step=step: merge_body(*refs, count=count, step=step, last=False),
             (VMEM, VMEM),
             (part, other),
-            struct((count, width) if last else part.shape, F32),
+            struct(part.shape, F32),
             limit=4,
         )
+    far_keys_values = local_call(
+        far_keys_body,
+        (VMEM,) * 4,
+        (norm_gain, far, key_weight, value_weight),
+        struct((rows * pitch, 2 * extra), BF16),
+    )
+    shared = (head_scale, far_keys_values, out_weight, own, queries, far_mask)
+    chunks = split // 2
+    scratch = [
+        pltpu.VMEM((chunks, 2 * rows * BLOCK, width), BF16),
+        pltpu.VMEM((chunks, rows, 2 * BLOCK, width), BF16),
+        pltpu.SemaphoreType.DMA((chunks,)),
+    ]
     mixed = local_call(
-        far_body,
-        (SMEM,) + (VMEM,) * 13,
-        (head_scale, norm_gain, far, key_weight, value_weight, out_weight, own, queries, *near),
-        struct((cells, width), BF16),
-        [
-            pltpu.VMEM((rows * pitch, 2 * extra), BF16),
-            pltpu.VMEM((rows * WIDE, LANES), BF16),
-            pltpu.VMEM((cells, width), BF16),
-        ],
-    )
-    return mixed.reshape(rows, cols, width), part
+        functools.partial(far_first_body, blocks=range(split)),
+        (VMEM,) * 9,
+        shared + tuple(near[0]),
+        struct(tokens.shape, BF16),
+        scratch,
+        out_specs=HBM,
+    )
+    return local_call(
+        functools.partial(
+            far_last_body, blocks=range(split, 2 * split), count=count, step=steps[-1]
+        ),
+        (HBM,) + (VMEM,) * 11,
+        (mixed, part, other) + shared + tuple(near[1]),
+        (struct(tokens.shape, BF16), struct((count, width), F32)),
+        scratch + [pltpu.VMEM((count, width), F32), pltpu.SemaphoreType.DMA(())],
+        out_specs=(HBM, HBM),
+        aliases={0: 0},
+    )
 
 
 def solution(mesh):

time: 46.5 us -> 41.3 us (0.89)
  Pallas kernels: 20.7 us -> 17 us
  waiting for transfers between devices: 14.7 us -> 11.5 us
  local copies, waits for them, and re-layouts: 0.04 us -> 1.74 us
    pallas_call x9 -> x11, Pallas kernels: 20.7 us -> 17 us  [local_call(): pl.pallas_call(body, out_shape=outs, in_specs=list(specs), out_specs=out_...]
    ppermute x6, waiting for transfers between devices: 14.7 us -> 11.5 us  [exchange(): return lax.ppermute(value, AXIS, pairs)]
    unnamed x16, local copies, waits for them, and re-layouts: 0.04 us -> 1.74 us
  transfers between devices with their start and end apart: 6 -> 6, of which waited for: 4 -> 3; matrix products, arithmetic and copies ran while one was open for 0% -> 0% of each run, Pallas kernels for 19% -> 27%
where the time goes in v5:
time: 41.3 us; the launch traced here: 41.1 us
  Pallas kernels  17 us (41%)
  waiting for transfers between devices  11.5 us (28%)
  starting transfers between devices  9.92 us (24%)
  local copies, waits for them, and re-layouts  1.74 us (4%)
  between operations  0.97 us (2%)
    pallas_call x11, Pallas kernels, local_call(): pl.pallas_call(body, out_shape=outs, in_specs=list(specs), out_specs=out_...  17 us
    ppermute x6, waiting for transfers between devices, exchange(): return lax.ppermute(value, AXIS, pairs)  11.5 us
    ppermute x6, starting transfers between devices, exchange(): return lax.ppermute(value, AXIS, pairs)  9.92 us
    unnamed x16, local copies, waits for them, and re-layouts  1.74 us
  transfers between devices with their start and end apart: 6, of which 3 were waited for; matrix products, arithmetic and copies ran while one was open for 0% of the time, Pallas kernels for 27%

profile of v5, /device:TPU:0, one launch (start us, length us, event | category | flops | bytes accessed | tf_op | source)
XLA Modules:
  0.0 41.1 jit_solution(13771157443089718754)
XLA Ops:
  0.6 0.0 copy-start
  0.6 0.0 copy-start.1
  0.7 0.0 copy-start.2
  0.7 0.0 copy-start.6
  0.7 0.1 shard_map.96
  0.8 1.0 %copy-done = bf16[4,128,768]{2,1,0:T(8,128)(2,1)S(1)} copy-done((bf16[4,128,768]{2,1,0:T(8,128)(2,1)S(1)}, bf16[4,128,768]{2,1,0:T(8,128)(2,1)}, u32[]{:S(2)}) %copy-start) | copy-done | bytes 786456
  1.8 0.4 copy-done.1
  2.1 0.4 copy-done.2
  2.5 0.0 copy-done.6
  2.5 0.0 copy-start.4
  2.5 0.0 copy-start.5
  2.5 0.0 copy-start.7
  2.5 2.0 %shard_map.97 = (bf16[576,1792]{1,0:T(8,128)(2,1)S(1)}, bf16[512,768]{1,0:T(8,128)(2,1)S(1)}) custom-call(bf16[256,128]{1,0:T(8,128)(2,1)S(1)} %get-tuple-element.14.mask_ref.refs_4_, f32[768]{0:T(1024)S(1)} %copy-done.6, bf16[512,768]{1,0:T(8,128)(2,1)S(1)} %bitcast.1, bf16[768,768]{1,0:T(8,128)(2,1)S(1)} %copy-done.1, bf16[768,768]{1,0:T(8,128)(2,1)S(1)} %copy-done.2), custom_call_target="tpu_custom_call" | custom-call | tf_op jit(solution)/shard_map/pallas_call | solution.py:533
  4.5 0.6 %collective-permute-start.1 = (bf16[576,1792]{1,0:T(8,128)(2,1)S(1)}, bf16[576,1792]{1,0:T(8,128)(2,1)S(1)}, u32[]{:S(2)}, u32[]{:S(2)}) collective-permute-start(bf16[576,1792]{1,0:T(8,128)(2,1)S(1)} %get-tuple-element.16.kv_ref.refs_2_), channel_id=1, source_target_pairs={{0,1},{1,0},{2,3},{3,2},{4,5},{5,4},{6,7},{7,6},{8,9},{9,8},{10,11... | collective-permute-start | bytes 6193160 | tf_op jit(solution)/shard_map/ppermute | solution.py:551
  5.0 0.9 %collective-permute-start = (bf16[512,768]{1,0:T(8,128)(2,1)S(1)}, bf16[512,768]{1,0:T(8,128)(2,1)S(1)}, u32[]{:S(2)}, u32[]{:S(2)}) collective-permute-start(bf16[512,768]{1,0:T(8,128)(2,1)S(1)} %bitcast.2), channel_id=1, source_target_pairs={{1,2},{3,4},{5,6},{7,8},{9,10},{11,12},{13,14},{2,1},{4,3},{6,5},{... | collective-permute-start | bytes 2359304 | tf_op jit(solution)/shard_map/ppermute | solution.py:551
  5.9 0.0 copy-done.4
  5.9 0.0 copy-done.5
  6.0 0.0 copy-done.7
  6.0 1.9 %shard_map.98 = (bf16[512,896]{1,0:T(8,128)(2,1)S(1)}, f32[112,128]{1,0:T(8,128)S(1)}) custom-call(f32[12]{0:T(128)S(1)} %copy-done.7, bf16[16,768]{1,0:T(8,128)(2,1)S(1)} %copy-done.5, bf16[512,768]{1,0:T(8,128)(2,1)S(1)} %get-tuple-element.15.normed_ref, bf16[768,768]{1,0:T(8,128)(2,1)S(1)} %copy-done.4, bf16[576,1792]{1,0:T(8,128)(2,1)S(1)} %get-tuple-element.16.kv_ref.refs_2_), custom_call_target="tpu_custom_call" | custom-call | tf_op jit(solution)/shard_map/pallas_call | solution.py:533
  7.9 3.9 %collective-permute-start.2 = (f32[112,128]{1,0:T(8,128)S(1)}, f32[112,128]{1,0:T(8,128)S(1)}, u32[]{:S(2)}, u32[]{:S(2)}) collective-permute-start(f32[112,128]{1,0:T(8,128)S(1)} %get-tuple-element.22.refs_0_), channel_id=1, source_target_pairs={{0,1},{1,0},{2,3},{3,2},{4,5},{5,4},{6,7},{7,6},{8,9},{9,8},{10,11... | collective-permute-start | bytes 172040 | tf_op jit(solution)/shard_map/ppermute | solution.py:551
  11.8 0.9 %collective-permute-done.2.refs_1_ = f32[112,128]{1,0:T(8,128)S(1)} collective-permute-done((f32[112,128]{1,0:T(8,128)S(1)}, f32[112,128]{1,0:T(8,128)S(1)}, u32[]{:S(2)}, u32[]{:S(2)}) %collective-permute-start.2) | collective-permute-done | bytes 57376 | tf_op jit(solution)/shard_map/ppermute | solution.py:551
  12.7 0.2 shard_map.101.refs_0_
  12.9 1.8 %collective-permute-start.3 = (f32[112,128]{1,0:T(8,128)S(1)}, f32[112,128]{1,0:T(8,128)S(1)}, u32[]{:S(2)}, u32[]{:S(2)}) collective-permute-start(f32[112,128]{1,0:T(8,128)S(1)} %shard_map.101.refs_0_), channel_id=1, source_target_pairs={{0,4},{1,5},{2,6},{3,7},{4,0},{5,1},{6,2},{7,3},{8,12},{9,13},{10,... | collective-permute-start | bytes 172040 | tf_op jit(solution)/shard_map/ppermute | solution.py:551
  14.7 8.2 %collective-permute-done.3.refs_1_ = f32[112,128]{1,0:T(8,128)S(1)} collective-permute-done((f32[112,128]{1,0:T(8,128)S(1)}, f32[112,128]{1,0:T(8,128)S(1)}, u32[]{:S(2)}, u32[]{:S(2)}) %collective-permute-start.3) | collective-permute-done | bytes 57376 | tf_op jit(solution)/shard_map/ppermute | solution.py:551
  22.9 0.2 shard_map.102.refs_0_
  23.0 2.7 %collective-permute-start.4 = (f32[112,128]{1,0:T(8,128)S(1)}, f32[112,128]{1,0:T(8,128)S(1)}, u32[]{:S(2)}, u32[]{:S(2)}) collective-permute-start(f32[112,128]{1,0:T(8,128)S(1)} %shard_map.102.refs_0_), channel_id=1, source_target_pairs={{0,8},{1,9},{2,10},{3,11},{4,12},{5,13},{6,14},{7,15},{8,0},{9,1},... | collective-permute-start | bytes 172040 | tf_op jit(solution)/shard_map/ppermute | solution.py:551
  25.7 2.5 %collective-permute-done.4.refs_1_ = f32[112,128]{1,0:T(8,128)S(1)} collective-permute-done((f32[112,128]{1,0:T(8,128)S(1)}, f32[112,128]{1,0:T(8,128)S(1)}, u32[]{:S(2)}, u32[]{:S(2)}) %collective-permute-start.4) | collective-permute-done | bytes 57376 | tf_op jit(solution)/shard_map/ppermute | solution.py:551
  28.2 0.2 shard_map.103.part_ref
  28.3 0.1 collective-permute-start.5
  28.4 0.0 collective-permute-done.far_ref
  28.4 2.0 %shard_map.95.refs_1_ = bf16[576,1792]{1,0:T(8,128)(2,1)S(1)} custom-call(f32[768]{0:T(1024)S(1)} %copy-done.6, bf16[512,768]{1,0:T(8,128)(2,1)S(1)} %collective-permute-done.far_ref, bf16[768,768]{1,0:T(8,128)(2,1)S(1)} %copy-done.1, bf16[768,768]{1,0:T(8,128)(2,1)S(1)} %copy-done.2), custom_call_target="tpu_custom_call" | custom-call | tf_op jit(solution)/shard_map/pallas_call | solution.py:533
  30.4 0.0 collective-permute-done.1.refs_3_
  30.5 0.0 copy-start.3
  30.5 1.8 %shard_map.99 = (f32[256,768]{1,0:T(8,128)S(1)}, f32[256,768]{1,0:T(8,128)S(1)}, f32[256,128]{1,0:T(8,128)S(1)}) custom-call(f32[12]{0:T(128)S(1)} %copy-done.7, bf16[512,896]{1,0:T(8,128)(2,1)S(1)} %get-tuple-element.17.refs_1_.refs_4_, bf16[576,1792]{1,0:T(8,128)(2,1)S(1)} %get-tuple-element.16.kv_ref.refs_2_, ...), custom_call_target="tpu_custom_call" | custom-call | tf_op jit(solution)/shard_map/pallas_call | solution.py:533
  32.3 0.0 copy-done.3
  32.3 3.2 %shard_map.100.so_far = bf16[4,128,768]{2,1,0:T(8,128)(2,1)} custom-call(f32[12]{0:T(128)S(1)} %copy-done.7, bf16[576,1792]{1,0:T(8,128)(2,1)S(1)} %shard_map.95.refs_1_, bf16[768,768]{1,0:T(8,128)(2,1)S(1)} %copy-done.3, bf16[512,768]{1,0:T(8,128)(2,1)S(1)} %bitcast.3, bf16[512,896]{1,0:T(8,128)(2,1)S(1)} %get-tuple-element.17.refs_1_.refs_4_, ...), custom_call_target="tpu_custom_call" | custom-call | tf_op jit(solution)/shard_map/pallas_call | solution.py:533
  35.5 1.8 %shard_map.104 = (f32[256,768]{1,0:T(8,128)S(1)}, f32[256,768]{1,0:T(8,128)S(1)}, f32[256,128]{1,0:T(8,128)S(1)}) custom-call(f32[12]{0:T(128)S(1)} %copy-done.7, bf16[512,896]{1,0:T(8,128)(2,1)S(1)} %get-tuple-element.17.refs_1_.refs_4_, bf16[576,1792]{1,0:T(8,128)(2,1)S(1)} %get-tuple-element.16.kv_ref.refs_2_, ...), custom_call_target="tpu_custom_call" | custom-call | tf_op jit(solution)/shard_map/pallas_call | solution.py:533
  37.3 0.0 collective-permute-done.5.other_ref
  37.3 3.6 %shard_map.105 = (bf16[4,128,768]{2,1,0:T(8,128)(2,1)}, f32[16,768]{1,0:T(8,128)}) custom-call(bf16[4,128,768]{2,1,0:T(8,128)(2,1)} %shard_map.100.so_far, f32[112,128]{1,0:T(8,128)S(1)} %shard_map.103.part_ref, f32[112,128]{1,0:T(8,128)S(1)} %collective-permute-done.5.other_ref, f32[12]{0:T(128)S(1)} %copy-done.7, ...), custom_call_target="tpu_custom_call", output_to_operand_aliasing={{0}: (0, {})} | custom-call | tf_op jit(solution)/shard_map/pallas_call | solution.py:533
Async XLA Ops:
  0.6 1.1 %copy-start = (bf16[4,128,768]{2,1,0:T(8,128)(2,1)S(1)}, bf16[4,128,768]{2,1,0:T(8,128)(2,1)}, u32[]{:S(2)}) copy-start(bf16[4,128,768]{2,1,0:T(8,128)(2,1)} %param.8) | copy-start | bytes 2359300
  0.6 1.5 %copy-start.1 = (bf16[768,768]{1,0:T(8,128)(2,1)S(1)}, bf16[768,768]{1,0:T(8,128)(2,1)}, u32[]{:S(2)}) copy-start(bf16[768,768]{1,0:T(8,128)(2,1)} %k_w.3) | copy-start | bytes 3538948
  0.7 1.9 %copy-start.2 = (bf16[768,768]{1,0:T(8,128)(2,1)S(1)}, bf16[768,768]{1,0:T(8,128)(2,1)}, u32[]{:S(2)}) copy-start(bf16[768,768]{1,0:T(8,128)(2,1)} %v_w.3) | copy-start | bytes 3538948
  0.7 1.8 %copy-start.6 = (f32[768]{0:T(1024)S(1)}, f32[768]{0:T(1024)}, u32[]{:S(2)}) copy-start(f32[768]{0:T(1024)} %gain_ref.3) | copy-start | bytes 9220
  2.5 3.4 %copy-start.4 = (bf16[768,768]{1,0:T(8,128)(2,1)S(1)}, bf16[768,768]{1,0:T(8,128)(2,1)}, u32[]{:S(2)}) copy-start(bf16[768,768]{1,0:T(8,128)(2,1)} %q_w.1) | copy-start | bytes 3538948
  2.5 3.4 %copy-start.5 = (bf16[16,768]{1,0:T(8,128)(2,1)S(1)}, bf16[16,768]{1,0:T(8,128)(2,1)}, u32[]{:S(2)}) copy-start(bf16[16,768]{1,0:T(8,128)(2,1)} %pool_ref.1) | copy-start | bytes 73732
  2.5 3.4 %copy-start.7 = (f32[12]{0:T(128)S(1)}, f32[12]{0:T(128)}, u32[]{:S(2)}) copy-start(f32[12]{0:T(128)} %refs_0_.7) | copy-start | bytes 148
  4.5 26.0 %collective-permute-start.1 = (bf16[576,1792]{1,0:T(8,128)(2,1)S(1)}, bf16[576,1792]{1,0:T(8,128)(2,1)S(1)}, u32[]{:S(2)}, u32[]{:S(2)}) collective-permute-start(bf16[576,1792]{1,0:T(8,128)(2,1)S(1)} %get-tuple-element.16.kv_ref.refs_2_), channel_id=1, source_target_pairs={{0,1},{1,0},{2,3},{3,2},{4,5},{5,4},{6,7},{7,6},{8,9},{9,8},{10,11... | collective-permute-start | bytes 6193160 | tf_op jit(solution)/shard_map/ppermute | solution.py:551
  5.0 23.4 %collective-permute-start = (bf16[512,768]{1,0:T(8,128)(2,1)S(1)}, bf16[512,768]{1,0:T(8,128)(2,1)S(1)}, u32[]{:S(2)}, u32[]{:S(2)}) collective-permute-start(bf16[512,768]{1,0:T(8,128)(2,1)S(1)} %bitcast.2), channel_id=1, source_target_pairs={{1,2},{3,4},{5,6},{7,8},{9,10},{11,12},{13,14},{2,1},{4,3},{6,5},{... | collective-permute-start | bytes 2359304 | tf_op jit(solution)/shard_map/ppermute | solution.py:551
  7.9 4.8 %collective-permute-start.2 = (f32[112,128]{1,0:T(8,128)S(1)}, f32[112,128]{1,0:T(8,128)S(1)}, u32[]{:S(2)}, u32[]{:S(2)}) collective-permute-start(f32[112,128]{1,0:T(8,128)S(1)} %get-tuple-element.22.refs_0_), channel_id=1, source_target_pairs={{0,1},{1,0},{2,3},{3,2},{4,5},{5,4},{6,7},{7,6},{8,9},{9,8},{10,11... | collective-permute-start | bytes 172040 | tf_op jit(solution)/shard_map/ppermute | solution.py:551
  12.9 10.0 %collective-permute-start.3 = (f32[112,128]{1,0:T(8,128)S(1)}, f32[112,128]{1,0:T(8,128)S(1)}, u32[]{:S(2)}, u32[]{:S(2)}) collective-permute-start(f32[112,128]{1,0:T(8,128)S(1)} %shard_map.101.refs_0_), channel_id=1, source_target_pairs={{0,4},{1,5},{2,6},{3,7},{4,0},{5,1},{6,2},{7,3},{8,12},{9,13},{10,... | collective-permute-start | bytes 172040 | tf_op jit(solution)/shard_map/ppermute | solution.py:551
  23.0 5.1 %collective-permute-start.4 = (f32[112,128]{1,0:T(8,128)S(1)}, f32[112,128]{1,0:T(8,128)S(1)}, u32[]{:S(2)}, u32[]{:S(2)}) collective-permute-start(f32[112,128]{1,0:T(8,128)S(1)} %shard_map.102.refs_0_), channel_id=1, source_target_pairs={{0,8},{1,9},{2,10},{3,11},{4,12},{5,13},{6,14},{7,15},{8,0},{9,1},... | collective-permute-start | bytes 172040 | tf_op jit(solution)/shard_map/ppermute | solution.py:551
  28.3 9.0 %collective-permute-start.5 = (f32[112,128]{1,0:T(8,128)S(1)}, f32[112,128]{1,0:T(8,128)S(1)}, u32[]{:S(2)}, u32[]{:S(2)}) collective-permute-start(f32[112,128]{1,0:T(8,128)S(1)} %shard_map.103.part_ref), channel_id=1, source_target_pairs={{0,2},{1,3},{2,0},{3,1},{4,6},{5,7},{6,4},{7,5},{8,10},{9,11},{10,... | collective-permute-start | bytes 172040 | tf_op jit(solution)/shard_map/ppermute | solution.py:551
  30.5 1.8 %copy-start.3 = (bf16[768,768]{1,0:T(8,128)(2,1)S(1)}, bf16[768,768]{1,0:T(8,128)(2,1)}, u32[]{:S(2)}) copy-start(bf16[768,768]{1,0:T(8,128)(2,1)} %refs_2_.3) | copy-start | bytes 3538948
